TPU v7x, 512 devices: a whole 4x4x16 slice. The times are simulated.
512 devices in a mesh: cls: 8 (over z_lo, core), ptcl: 64 (over y, z_hi, x).
Axes of the slice: x: 4, y: 4, z: 16 (z_hi: 4, z_lo: 4; z = z_hi * 4 + z_lo), core: 2. Of those that a mesh axis runs over, the one named last changes fastest.
Arguments:
- particles: bfloat16 [65536, 2048], P('ptcl')
- panels: bfloat16 [8, 128, 2048], P('cls', 'ptcl')
- sigma2: float32 [32], replicated, may hold values from 0.5 to 2
- defocus_bins: int32 [65536], P('ptcl'), may hold values from 0 to 15
- half_sets: int32 [65536], P('ptcl'), may hold values 0 or 1
- prior_mask: int32 [65536, 8], P('ptcl', 'cls'), may hold values from 0 to 1, as said below
- orient_ids: int32 [128], replicated, may hold values from 0 to 127, each once
Outputs:
- half_maps: float32 [8, 256, 2048], P('cls', 'ptcl')
- log_evidence: float32 [65536], P('ptcl')
Inputs may be any that keep to these rules, and one draw needn't show every extreme that they name: `prior_mask`: every particle allows at least one class. `orient_ids`: each direction 0 to 127 appears once.
All inputs are finite; a program needn't handle non-finite values. No bound on the sum of `half_sets` on one device may be relied on, other than what follows from the above.
Results may differ from a plain program's by a relative error of at most 0.0015.
The roundings to bfloat16 on the way count: a program that leaves them out, or rounds other values in their place, can miss the bound.
Values may be sent and summed in bfloat16 or wider, within the bound.
No kernel may reach another device: no remote copies, remote signals or barrier semaphores. Data moves between devices by JAX's collectives and lax.ppermute only.
A program may use at most 64 MiB of HBM per device.

v0:
```python
import jax
import jax.numpy as jnp
from jax import lax
from jax.sharding import PartitionSpec as P

PIXC = 1024
ORIENT = 128
NSHELL = 32
NBIN = 16


def from_partner(shard, axis, apart):
    return lax.ppermute(shard, axis, [(i, i ^ 1 << apart) for i in range(lax.axis_size(axis))])


def ctf_table():
    bins = jnp.arange(NBIN, dtype=jnp.float32)
    defocus = (bins + 1.0) / NBIN
    radius = (jnp.arange(PIXC, dtype=jnp.float32) + 0.5) / PIXC
    phase = 0.3 + 2.5 * defocus[:, None] * radius[None, :]
    return jnp.sin(phase) + 0.1 * jnp.cos(phase)


def lookup_small(indices, values):
    count = values.shape[0]
    match = indices[:, None] == jnp.arange(count, dtype=jnp.int32)[None, :]
    return jnp.sum(jnp.where(match, values[None, :], 0.0), axis=1)


def contract_rows(left, right):
    return lax.dot_general(
        left, right, (((0,), (0,)), ((), ())), preferred_element_type=jnp.float32
    )


def on_device(particles, panels, sigma2, defocus_bins, half_sets, prior_mask, orient_ids):
    shells = jnp.arange(PIXC, dtype=jnp.int32) * NSHELL // PIXC
    inverse_noise = lookup_small(shells, 1.0 / sigma2)
    table = ctf_table()
    onehot_bin = (defocus_bins[:, None] == jnp.arange(NBIN, dtype=jnp.int32)[None, :]).astype(
        jnp.float32
    )
    contrast = jnp.dot(onehot_bin, table, precision=lax.Precision.HIGHEST)
    doubled = jnp.concatenate([contrast, contrast], axis=1)
    noise_pair = jnp.concatenate([inverse_noise, inverse_noise])
    images = particles.astype(jnp.float32)
    weighted = (images * doubled * noise_pair[None, :]).astype(jnp.bfloat16)
    power = (contrast * contrast * inverse_noise[None, :]).astype(jnp.bfloat16)
    piece = lax.all_gather(panels[0], "ptcl", axis=0, tiled=True)
    piece_f = piece.astype(jnp.float32)
    piece_power = (piece_f[:, :PIXC] ** 2 + piece_f[:, PIXC:] ** 2).astype(jnp.bfloat16)
    direct = lax.dot_general(
        weighted, piece, (((1,), (1,)), ((), ())), preferred_element_type=jnp.float32
    )
    norm_part = lax.dot_general(
        power, piece_power, (((1,), (1,)), ((), ())), preferred_element_type=jnp.float32
    )
    scores = direct - 0.5 * norm_part
    allowed = (prior_mask[:, 0] > 0)[:, None]
    masked = jnp.where(allowed, scores, -1e30)
    local_peak = jnp.max(masked, axis=1)
    peak = lax.pmax(local_peak, "cls")
    weights_exp = jnp.where(allowed, jnp.exp(masked - peak[:, None]), 0.0)
    total = lax.psum(jnp.sum(weights_exp, axis=1), "cls")
    log_evidence = peak + jnp.log(total)
    posterior = (weights_exp / total[:, None]).astype(jnp.bfloat16)
    permuter = (orient_ids[:, None] == jnp.arange(ORIENT, dtype=jnp.int32)[None, :]).astype(
        jnp.bfloat16
    )
    by_direction = jnp.dot(posterior, permuter, preferred_element_type=jnp.float32).astype(
        jnp.bfloat16
    )
    half_col = half_sets.astype(jnp.bfloat16)[:, None]
    split_post = jnp.concatenate([by_direction * (1 - half_col), by_direction * half_col], axis=1)
    centred = (images * doubled).astype(jnp.bfloat16)
    squares_ctf = (contrast * contrast).astype(jnp.bfloat16)
    stacked = jnp.concatenate([centred, squares_ctf], axis=1)
    summed = lax.psum_scatter(
        contract_rows(split_post, stacked), "ptcl", scatter_dimension=0, tiled=True
    )
    data = summed[:, : 2 * PIXC]
    weight = summed[:, 2 * PIXC :]
    top_bit = lax.axis_size("ptcl").bit_length() - 2
    partner = from_partner(data.astype(jnp.bfloat16), "ptcl", top_bit).astype(data.dtype)
    half_index = lax.axis_index("ptcl") // (lax.axis_size("ptcl") // 2)

    def per_shell(values):
        summed_rows = jnp.sum(values, axis=0)
        folded = summed_rows[:PIXC] + summed_rows[PIXC:]
        return jnp.sum(folded.reshape(NSHELL, PIXC // NSHELL), axis=1)

    cross = per_shell(data * partner)
    own_power = per_shell(data * data)
    is_first = half_index == 0
    stats = jnp.stack(
        [0.5 * cross, jnp.where(is_first, own_power, 0.0), jnp.where(is_first, 0.0, own_power)]
    )
    totals = lax.psum(stats, "ptcl")
    fsc = totals[0] / jnp.sqrt(totals[1] * totals[2] + 1e-06)
    factor = (1.0 + lookup_small(shells, fsc)) / 2.0
    factor_pair = jnp.concatenate([factor, factor])
    weight_pair = jnp.concatenate([weight, weight], axis=1)
    half_maps = data * factor_pair[None, :] / (weight_pair + 1.0)
    return (half_maps[None], log_evidence)


def solution(mesh):
    placed = (
        P("ptcl", None),
        P("cls", "ptcl", None),
        P(),
        P("ptcl"),
        P("ptcl"),
        P("ptcl", "cls"),
        P(),
    )
    return jax.shard_map(
        on_device,
        mesh=mesh,
        in_specs=placed,
        out_specs=(P("cls", "ptcl", None), P("ptcl")),
        check_vma=False,
    )
```

profile of v0, /device:TPU:32, one launch (start us, length us, event | category | flops | bytes accessed | tf_op | source)
XLA Modules:
  0.0 1377.2 jit_solution(9083316655074497782)
XLA Ops:
  7.3 0.7 broadcast_divide_fusion
  8.0 6.4 copy.14
  14.5 234.2 %all-gather = bf16[1,128,2048]{2,0,1:T(2,128)(2,1)S(1)} all-gather(bf16[1,2,2048]{2,0,1:T(2,128)(2,1)S(1)} %copy.15), channel_id=2, replica_groups=mesh['cls'=8,'ptcl'=64] {'ptcl'}, dimensions={1}, use_global_device_ids=true | all-gather | bytes 532480 | tf_op jit(solution)/shard_map/all_gather | solution.py:49
  248.7 0.4 bitcast_convert_fusion
  249.1 2.2 multiply_convert_fusion.3
  251.3 3.3 fusion
  254.6 1.5 fusion.5
  256.2 0.7 fusion.46
  256.9 10.0 pmax.7
  267.0 13.5 psum.14
  280.5 0.3 broadcast_multiply_fusion.1
  280.9 5.8 fusion.1
  286.7 1.3 dynamic-slice
  288.6 848.2 %all-reduce.3.cloned.1.call-done = f32[256,3072]{1,0:T(8,128)} async-done(((f32[256,3072]{1,0:T(8,128)}), f32[256,3072]{1,0:T(8,128)}) %all-reduce.3.cloned.1.call-update) | async-done | bytes 3145744
  1136.8 0.8 dynamic-slice_convert_fusion
  1137.6 1.9 collective-permute-start
  1139.5 0.6 log_add_fusion
  1140.2 0.8 dynamic-slice.3
  1141.0 3.8 collective-permute-done
  1144.8 0.9 multiply_reduce_fusion.1
  1145.8 0.1 reduce_sum.68
  1145.9 0.1 reduce_sum.66
  1146.1 222.7 %psum.15 = f32[3,32]{1,0:T(4,128)S(1)} all-reduce(f32[3,32]{1,0:T(4,128)S(1)} %pad_maximum_fusion.2), channel_id=1, replica_groups=mesh['cls'=8,'ptcl'=64] {'ptcl'}, use_global_device_ids=true, to_apply=%region_10.11 | all-reduce | flops 96 | bytes 768 | tf_op jit(solution)/shard_map/psum | solution.py:98
  1368.9 1.5 fusion.35
  (33 shorter events, 0.6 us)
Async XLA Ops:
  7.2 1129.6 %all-reduce.3.cloned.1.call-start = ((), (), s32[]{:S(2)}) async-start(), calls=%async_computation | async-start | bytes 6291456
  8.0 6.4 copy-start.1
  8.0 241.0 %copy-start.2 = (s32[1024]{0:T(1024)S(1)}, s32[1024]{0:T(1024)}, u32[]{:S(2)}) copy-start(s32[1024]{0:T(1024)} %param.10) | copy-start | bytes 12292
  248.7 2.6 copy-start
  254.6 1.5 copy-start.3
  256.1 24.4 %copy-start.4 = (s32[1024]{0:T(1024)S(1)}, s32[1024]{0:T(1024)}, u32[]{:S(2)}) copy-start(s32[1024]{0:T(1024)} %param.11) | copy-start | bytes 12292
  256.1 24.4 %copy-start.5 = (s32[128]{0:T(128)S(1)}, s32[128]{0:T(128)}, u32[]{:S(2)}) copy-start(s32[128]{0:T(128)} %param.13) | copy-start | bytes 1540
  1137.6 7.1 collective-permute-start
Sparse Core Ops, SparseCore 0:
  286.8 849.9 all-reduce.2
where the time goes:
time: 1380 us
  waiting for transfers between devices  852 us (62%)
  blocking collectives  480 us (35%)
  between operations  14.9 us (1%)
    unnamed x2, waiting for transfers between devices  848 us
    all_gather x1, blocking collectives, on_device(): piece = lax.all_gather(panels[0], 'ptcl', axis=0, tiled=True)  234 us
    psum x1, blocking collectives, on_device(): totals = lax.psum(stats, 'ptcl')  223 us
  transfers between devices with their start and end apart: 2, of which 2 were waited for; matrix products, arithmetic and copies ran while one was open for 0% of the time, Pallas kernels for 0%

commit v1 on v0

v1 whole, which is shorter than its diff:
```python
import jax
import jax.numpy as jnp
from jax import lax
from jax.sharding import Mesh
from jax.sharding import PartitionSpec as P

PIXC = 1024
ORIENT = 128
NSHELL = 32
NBIN = 16
AXES = ("zl", "co", "y", "zh", "x")
CLS = ("zl", "co")
PTCL = ("y", "zh", "x")
EXTRA = 128


def ctf_table():
    bins = jnp.arange(NBIN, dtype=jnp.float32)
    defocus = (bins + 1.0) / NBIN
    radius = (jnp.arange(PIXC, dtype=jnp.float32) + 0.5) / PIXC
    phase = 0.3 + 2.5 * defocus[:, None] * radius[None, :]
    return jnp.sin(phase) + 0.1 * jnp.cos(phase)


def lookup_small(indices, values):
    count = values.shape[0]
    match = indices[:, None] == jnp.arange(count, dtype=jnp.int32)[None, :]
    return jnp.sum(jnp.where(match, values[None, :], 0.0), axis=1)


def exchange(blocks, axes):
    return lax.all_to_all(blocks, axes, split_axis=0, concat_axis=0, tiled=True)


def from_all(shard, axes, count):
    return exchange(jnp.broadcast_to(shard[None], (count,) + shard.shape), axes)


def row_maps():
    r = jnp.arange(2 * ORIENT, dtype=jnp.int32)
    j, half, zh, x, y = r % 2, (r // 2) % 2, (r // 4) % 4, (r // 16) % 4, r // 64
    return 4 * (((y % 2) * 4 + zh) * 4 + x) + 2 * (y // 2) + j, half


def gathered_orients():
    r = jnp.arange(ORIENT, dtype=jnp.int32)
    j, zh, x, y = r % 2, (r // 2) % 4, (r // 8) % 4, r // 32
    return ((y * 4 + zh) * 4 + x) * 2 + j


def three_parts(table):
    high = table.astype(jnp.bfloat16)
    rest = table - high.astype(jnp.float32)
    mid = rest.astype(jnp.bfloat16)
    low = (rest - mid.astype(jnp.float32)).astype(jnp.bfloat16)
    return high, mid, low


def on_device(particles, panels, sigma2, defocus_bins, half_sets, prior_mask, orient_ids):
    by_zh = from_all(panels[0], "zh", 4).reshape(8, 2 * PIXC)
    piece = from_all(by_zh, ("y", "x"), 16).reshape(ORIENT, 2 * PIXC)

    shells = jnp.arange(PIXC, dtype=jnp.int32) * NSHELL // PIXC
    inverse_noise = lookup_small(shells, 1.0 / sigma2)
    table = ctf_table()
    match = defocus_bins[:, None] == jnp.arange(NBIN, dtype=jnp.int32)[None, :]
    onehot = match.astype(jnp.float32)
    contrast = jnp.dot(onehot, table, precision=lax.Precision.HIGHEST)
    doubled = jnp.concatenate([contrast, contrast], axis=1)
    noise_pair = jnp.concatenate([inverse_noise, inverse_noise])
    images = particles.astype(jnp.float32)
    weighted = (images * doubled * noise_pair[None, :]).astype(jnp.bfloat16)
    centred = (images * doubled).astype(jnp.bfloat16)
    power = (table * table * inverse_noise[None, :]).astype(jnp.bfloat16)
    squares = (table * table).astype(jnp.bfloat16).astype(jnp.float32)

    piece_f = piece.astype(jnp.float32)
    piece_power = (piece_f[:, :PIXC] ** 2 + piece_f[:, PIXC:] ** 2).astype(jnp.bfloat16)
    direct = lax.dot_general(
        piece, weighted, (((1,), (1,)), ((), ())), preferred_element_type=jnp.float32
    )
    norm_table = lax.dot_general(
        piece_power, power, (((1,), (1,)), ((), ())), preferred_element_type=jnp.float32
    )
    norm_part = lax.dot_general(
        norm_table, onehot, (((1,), (1,)), ((), ())), precision=lax.Precision.HIGHEST
    )
    scores = direct - 0.5 * norm_part
    allowed = (prior_mask.reshape(-1) > 0)[None, :]
    masked = jnp.where(allowed, scores, -1e30)
    own_peak = jnp.max(masked, axis=0)
    own_exp = jnp.where(allowed, jnp.exp(masked - own_peak[None, :]), 0.0)
    own_total = jnp.sum(own_exp, axis=0)

    both = from_all(jnp.stack([own_peak, own_total]), CLS, 8)
    peak = jnp.max(both[:, 0], axis=0)
    total = jnp.sum(both[:, 1] * jnp.exp(both[:, 0] - peak[None, :]), axis=0)
    log_evidence = peak + jnp.log(total)
    posterior = (own_exp * (jnp.exp(own_peak - peak) / total)[None, :]).astype(jnp.bfloat16)

    direction, half = row_maps()
    select = jnp.sum(
        jnp.where(
            gathered_orients()[:, None] == jnp.arange(ORIENT, dtype=jnp.int32)[None, :],
            orient_ids[None, :],
            0,
        ),
        axis=1,
    )
    permuter = (direction[:, None] == select[None, :]).astype(jnp.bfloat16)
    by_direction = jnp.dot(permuter, posterior, preferred_element_type=jnp.float32)
    split_post = jnp.where(half[:, None] == half_sets[None, :], by_direction, 0.0).astype(
        jnp.bfloat16
    )
    data_part = jnp.dot(split_post, centred, preferred_element_type=jnp.float32)
    bin_part = jnp.dot(split_post, match.astype(jnp.bfloat16), preferred_element_type=jnp.float32)

    top = jnp.max(jnp.abs(data_part), axis=1, keepdims=True)
    expo = jnp.clip(jnp.floor(jnp.log2(jnp.maximum(top, 1e-30))), -100.0, 126.0) - 13.0
    small = (data_part * jnp.exp2(-expo)).astype(jnp.float16)
    bin_high = bin_part.astype(jnp.float16)
    bin_low = (bin_part - bin_high.astype(jnp.float32)).astype(jnp.float16)
    side = jnp.concatenate(
        [bin_high, bin_low, jnp.broadcast_to(expo, (2 * ORIENT, EXTRA - 2 * NBIN)).astype(jnp.float16)],
        axis=1,
    )
    packed = jnp.concatenate([small, side], axis=1).reshape(16, 16, 2 * PIXC + EXTRA)
    came = exchange(packed, ("y", "x")).astype(jnp.float32)
    unscale = jnp.exp2(came[:, :, -1:])
    data_16 = jnp.sum(came[:, :, : 2 * PIXC] * unscale, axis=0)
    bins_16 = jnp.sum(came[:, :, 2 * PIXC :], axis=0)
    second = jnp.concatenate([data_16, bins_16], axis=1).reshape(4, 4, 2 * PIXC + EXTRA)
    summed = jnp.sum(exchange(second, "zh"), axis=0)
    data = summed[:, : 2 * PIXC]
    bins = summed[:, 2 * PIXC : 2 * PIXC + NBIN] + summed[:, 2 * PIXC + NBIN : 2 * PIXC + 2 * NBIN]
    weight = jnp.dot(bins, squares, precision=lax.Precision.HIGHEST)
    weight_pair = jnp.concatenate([weight, weight], axis=1)
    scaled = data / (weight_pair + 1.0)

    upper = lax.axis_index("y") // 2
    keep = jnp.where(upper == 0, scaled[:2], scaled[2:])
    give = jnp.where(upper == 0, scaled[2:], scaled[:2])
    got = lax.ppermute(give, "y", [(i, i ^ 2) for i in range(4)])

    def per_shell(values):
        summed_rows = jnp.sum(values, axis=0)
        folded = summed_rows[:PIXC] + summed_rows[PIXC:]
        return jnp.sum(folded.reshape(NSHELL, PIXC // NSHELL), axis=1)

    stats = jnp.concatenate(
        [
            per_shell(data[:2] * data[2:]),
            per_shell(data[:2] * data[:2]),
            per_shell(data[2:] * data[2:]),
            jnp.zeros((32,), jnp.float32),
        ]
    )
    stats = jnp.sum(from_all(stats[None], ("y", "x"), 16), axis=0)
    totals = jnp.sum(from_all(stats, "zh", 4), axis=0).reshape(4, NSHELL)
    fsc = totals[0] / jnp.sqrt(totals[1] * totals[2] + 1e-06)
    factor = (1.0 + lookup_small(shells, fsc)) / 2.0
    factor_pair = jnp.concatenate([factor, factor])
    first = jnp.where(upper == 0, keep, got)
    last = jnp.where(upper == 0, got, keep)
    half_maps = jnp.concatenate([first, last], axis=0) * factor_pair[None, :]
    return (half_maps[None], log_evidence)


def solution(mesh):
    split = Mesh(mesh.devices.reshape(4, 2, 4, 4, 4), AXES)
    placed = (
        P(PTCL, None),
        P(CLS, PTCL, None),
        P(),
        P(PTCL),
        P(PTCL),
        P(PTCL, CLS),
        P(),
    )
    return jax.shard_map(
        on_device,
        mesh=split,
        in_specs=placed,
        out_specs=(P(CLS, PTCL, None), P(PTCL)),
        check_vma=False,
    )
```

time: 1380 us -> 187 us (0.14)
  waiting for transfers between devices: 852 us -> 48.1 us
  blocking collectives: 480 us -> 24.8 us
  starting transfers between devices: 1.96 us -> 38.6 us
  other arithmetic: 7.91 us -> 31.7 us
  between operations: 14.9 us -> 0.99 us
    unnamed x2 -> x0, waiting for transfers between devices: 848 us -> none
    psum x2 -> x0, blocking collectives: 236 us -> none  [the longest x1 223 us: on_device(): totals = lax.psum(stats, 'ptcl')]
    all_gather x1 -> x0, blocking collectives: 234 us -> none  [on_device(): piece = lax.all_gather(panels[0], 'ptcl', axis=0, tiled=True)]
    all_to_all x0 -> x6, waiting for transfers between devices: none -> 48.1 us  [exchange(): return lax.all_to_all(blocks, axes, split_axis=0, concat_axis=0, tiled=True)]
    all_to_all x0 -> x6, starting transfers between devices: none -> 35.5 us  [exchange(): return lax.all_to_all(blocks, axes, split_axis=0, concat_axis=0, tiled=True)]
    all_to_all x0 -> x1, blocking collectives: none -> 24.8 us  [exchange(): return lax.all_to_all(blocks, axes, split_axis=0, concat_axis=0, tiled=True)]
    reduce_sum x1 -> x8, other arithmetic: 0.11 us -> 22 us  [the longest x1 21.4 us: on_device(): data_16 = jnp.sum(came[:, :, :2 * PIXC] * unscale, axis=0)]
  transfers between devices with their start and end apart: 2 -> 7, of which waited for: 2 -> 5; matrix products, arithmetic and copies ran while one was open for 0% -> 6% of each run, Pallas kernels for 0% -> 0%
where the time goes in v1:
time: 187 us; the launch traced here: 186 us
  waiting for transfers between devices  48.1 us (26%)
  starting transfers between devices  38.6 us (21%)
  other arithmetic  31.7 us (17%)
  blocking collectives  24.8 us (13%)
  local copies, waits for them, and re-layouts  22.2 us (12%)
  matrix products  19.3 us (10%)
    all_to_all x6, waiting for transfers between devices, exchange(): return lax.all_to_all(blocks, axes, split_axis=0, concat_axis=0, tiled=True)  48.1 us
    all_to_all x6, starting transfers between devices, exchange(): return lax.all_to_all(blocks, axes, split_axis=0, concat_axis=0, tiled=True)  35.5 us
    all_to_all x1, blocking collectives, exchange(): return lax.all_to_all(blocks, axes, split_axis=0, concat_axis=0, tiled=True)  24.8 us
    reduce_sum x1, other arithmetic, on_device(): data_16 = jnp.sum(came[:, :, :2 * PIXC] * unscale, axis=0)  21.4 us
    all_to_all x1, local copies, waits for them, and re-layouts, exchange(): return lax.all_to_all(blocks, axes, split_axis=0, concat_axis=0, tiled=True)  9 us
    dot_general x1, matrix products, on_device(): data_part = jnp.dot(split_post, centred, preferred_element_type=jnp.float32)  7.39 us
    unnamed x9, local copies, waits for them, and re-layouts  6.43 us
    dot_general x1, matrix products, on_device(): lax.dot_general(piece, weighted, (((1,), (1,)), ((), ())), preferred_elem...  5.43 us
  transfers between devices with their start and end apart: 7, of which 5 were waited for; matrix products, arithmetic and copies ran while one was open for 6% of the time, Pallas kernels for 0%

profile of v1, /device:TPU:32, one launch (start us, length us, event | category | flops | bytes accessed | tf_op | source)
XLA Modules:
  0.0 185.7 jit_solution(15598901970763728901)
XLA Ops:
  0.6 1.3 broadcast_in_dim.125
  2.0 14.2 %all-to-all-start = ((bf16[4,2,2048]{2,1,0:T(2,128)(2,1)}), bf16[4,2,2048]{2,1,0:T(2,128)(2,1)S(1)}, u32[]{:S(2)}, u32[]{:S(2)}) async-start(bf16[4,2,2048]{2,1,0:T(2,128)(2,1)} %broadcast_in_dim.125), calls=%async_computation | async-start | bytes 65536 | tf_op jit(solution)/shard_map/all_to_all | solution.py:32
  16.9 12.0 %all-to-all-done = bf16[4,2,2048]{2,1,0:T(2,128)(2,1)S(1)} async-done(((bf16[4,2,2048]{2,1,0:T(2,128)(2,1)}), bf16[4,2,2048]{2,1,0:T(2,128)(2,1)S(1)}, u32[]{:S(2)}, u32[]{:S(2)}) %all-to-all-start) | async-done | bytes 32800 | tf_op jit(solution)/shard_map/all_to_all | solution.py:32
  28.9 0.9 broadcast_in_dim.127
  29.8 7.0 %all-to-all-start.1 = ((bf16[16,8,2048]{2,1,0:T(8,128)(2,1)}), bf16[16,8,2048]{2,1,0:T(8,128)(2,1)S(1)}, u32[]{:S(2)}, u32[]{:S(2)}) async-start(bf16[16,8,2048]{2,1,0:T(8,128)(2,1)} %broadcast_in_dim.127), calls=%async_computation.1 | async-start | bytes 1048576 | tf_op jit(solution)/shard_map/all_to_all | solution.py:32
  36.9 6.4 %copy.51 = bf16[1024,2048]{0,1:T(8,128)(2,1)} copy(bf16[1024,2048]{1,0:T(8,128)(2,1)} %param.7) | data formatting | bytes 8388608 | tf_op args[0]
  43.3 4.0 %fusion.13 = f32[1024,1024]{0,1:T(8,128)} fusion(s32[1024]{0:T(1024)S(1)} %copy-done, f32[1024]{0:T(1024)S(1)} %add_multiply_fusion.1, f32[16]{0:T(128)S(1)} %add_multiply_fusion.2), kind=kOutput, calls=%fused_computation.26 | convolution fusion | flops 201408512 | bytes 4202560 | tf_op jit(solution)/shard_map/dot_general | solution.py:68
  48.0 5.4 %fusion.6 = f32[128,1024]{1,0:T(8,128)S(1)} fusion(f32[1024,1024]{0,1:T(8,128)} %fusion.13, bf16[1024,2048]{0,1:T(8,128)(2,1)} %copy.51, f32[2048]{0:T(1024)S(1)} %pad_maximum_fusion.1, bf16[16,8,2048]{2,1,0:T(8,128)(2,1)S(1)} %all-to-all-done.1), kind=kOutput, calls=%fused_computation.11 | convolution fusion | flops 547356672 | bytes 9445376 | tf_op jit(solution)/shard_map/dot_general | solution.py:79
  54.8 4.3 %all-to-all-start.2 = ((f32[8,2,1024]{2,1,0:T(2,128)}), f32[8,2,1024]{2,1,0:T(2,128)S(1)}, u32[]{:S(2)}, u32[]{:S(2)}) async-start(f32[8,2,1024]{2,1,0:T(2,128)} %broadcast_in_dim.130), calls=%async_computation.2 | async-start | bytes 131072 | tf_op jit(solution)/shard_map/all_to_all | solution.py:32
  59.3 4.5 %all-to-all-done.2 = f32[8,2,1024]{2,1,0:T(2,128)S(1)} async-done(((f32[8,2,1024]{2,1,0:T(2,128)}), f32[8,2,1024]{2,1,0:T(2,128)S(1)}, u32[]{:S(2)}, u32[]{:S(2)}) %all-to-all-start.2) | async-done | bytes 65568 | tf_op jit(solution)/shard_map/all_to_all | solution.py:32
  64.8 7.4 %abs_reduce_fusion = (f32[256]{0:T(256)S(1)}, f32[256,2048]{1,0:T(8,128)}) fusion(bf16[256,1024]{1,0:T(8,128)(2,1)S(1)} %fusion.5, f32[1024,1024]{0,1:T(8,128)} %fusion.13, bf16[1024,2048]{0,1:T(8,128)(2,1)} %copy.51), kind=kOutput, calls=%fused_computation.8 | convolution fusion | flops 1083178752 | bytes 11011072 | tf_op jit(solution)/shard_map/dot_general | solution.py:115
  73.0 1.8 multiply_convert_fusion.2
  75.0 1.1 concatenate.37
  76.1 24.8 %all_to_all.35 = f16[16,16,2176]{2,1,0:T(8,128)(2,1)S(1)} all-to-all(f16[16,16,2176]{2,1,0:T(8,128)(2,1)S(1)} %bitcast.36), channel_id=1, replica_groups=mesh['zl'=4,'co'=2,'y'=4,'zh'=4,'x'=4] {'y','x'}, dimensions={0} | all-to-all | bytes 2228224 | tf_op jit(solution)/shard_map/all_to_all | solution.py:32
  100.8 9.0 %copy.55 = f16[16,16,2176]{1,0,2:T(8,128)(2,1)} copy(f16[16,16,2176]{2,1,0:T(8,128)(2,1)S(1)} %all_to_all.35) | data formatting | bytes 2228224 | tf_op jit(solution)/shard_map/all_to_all | solution.py:32
  109.8 4.8 %convert_element_type.63 = f32[16,16,2176]{1,0,2:T(8,128)S(1)} convert(f16[16,16,2176]{1,0,2:T(8,128)(2,1)} %copy.55) | non-fusion elementwise | flops 557056 | bytes 3342336 | tf_op jit(solution)/shard_map/convert_element_type | solution.py:128
  114.9 21.4 %fusion = f32[16,2048]{0,1:T(8,128)S(1)} fusion(f32[16,16,2176]{1,0,2:T(8,128)S(1)} %convert_element_type.63, f32[16,16]{1,0:T(8,128)S(1)} %fusion.45), kind=kLoop, calls=%fused_computation.1 | loop fusion | flops 1015808 | bytes 2229248 | tf_op jit(solution)/shard_map/reduce_sum | solution.py:130
  137.4 3.3 %all-to-all-start.4 = ((f32[4,4,2176]{2,1,0:T(4,128)}), f32[4,4,2176]{2,1,0:T(4,128)S(1)}, u32[]{:S(2)}, u32[]{:S(2)}) async-start(f32[4,4,2176]{2,1,0:T(4,128)} %reshape.394), calls=%async_computation.4 | async-start | bytes 278528 | tf_op jit(solution)/shard_map/all_to_all | solution.py:32
  140.7 15.1 %all-to-all-done.4 = f32[4,4,2176]{2,1,0:T(4,128)S(1)} async-done(((f32[4,4,2176]{2,1,0:T(4,128)}), f32[4,4,2176]{2,1,0:T(4,128)S(1)}, u32[]{:S(2)}, u32[]{:S(2)}) %all-to-all-start.4) | async-done | bytes 139296 | tf_op jit(solution)/shard_map/all_to_all | solution.py:32
  157.7 3.5 %all-to-all-start.5 = ((f32[16,1,128]{2,1,0:T(1,128)}), f32[16,1,128]{2,1,0:T(1,128)S(1)}, u32[]{:S(2)}, u32[]{:S(2)}) async-start(f32[16,1,128]{2,1,0:T(1,128)} %broadcast_in_dim.134), calls=%async_computation.5 | async-start | bytes 16384 | tf_op jit(solution)/shard_map/all_to_all | solution.py:32
  161.2 7.4 %all-to-all-done.5 = f32[16,1,128]{2,1,0:T(1,128)S(1)} async-done(((f32[16,1,128]{2,1,0:T(1,128)}), f32[16,1,128]{2,1,0:T(1,128)S(1)}, u32[]{:S(2)}, u32[]{:S(2)}) %all-to-all-start.5) | async-done | bytes 8224 | tf_op jit(solution)/shard_map/all_to_all | solution.py:32
  169.2 3.2 %all-to-all-start.6 = ((f32[4,1,128]{2,1,0:T(1,128)}), f32[4,1,128]{2,1,0:T(1,128)S(1)}, u32[]{:S(2)}, u32[]{:S(2)}) async-start(f32[4,1,128]{2,1,0:T(1,128)} %broadcast_in_dim.135), calls=%async_computation.6 | async-start | bytes 4096 | tf_op jit(solution)/shard_map/all_to_all | solution.py:32
  172.4 3.1 %collective-permute-start = (f32[2,2048]{1,0:T(2,128)S(1)}, f32[2,2048]{1,0:T(2,128)S(1)}, u32[]{:S(2)}, u32[]{:S(2)}) collective-permute-start(f32[2,2048]{1,0:T(2,128)S(1)} %broadcast_select_fusion), channel_id=1, source_target_pairs={{0,32},{16,48},{32,0},{48,16},{1,33},{17,49},{33,1},{49,17},{2,34}... | collective-permute-start | bytes 49160 | tf_op jit(solution)/shard_map/ppermute | solution.py:143
  175.6 9.2 %all-to-all-done.6 = f32[4,1,128]{2,1,0:T(1,128)S(1)} async-done(((f32[4,1,128]{2,1,0:T(1,128)}), f32[4,1,128]{2,1,0:T(1,128)S(1)}, u32[]{:S(2)}, u32[]{:S(2)}) %all-to-all-start.6) | async-done | bytes 2080 | tf_op jit(solution)/shard_map/all_to_all | solution.py:32
  (68 shorter events, 9.6 us)
Async XLA Ops:
  2.0 26.9 %all-to-all-start = ((bf16[4,2,2048]{2,1,0:T(2,128)(2,1)}), bf16[4,2,2048]{2,1,0:T(2,128)(2,1)S(1)}, u32[]{:S(2)}, u32[]{:S(2)}) async-start(bf16[4,2,2048]{2,1,0:T(2,128)(2,1)} %broadcast_in_dim.125), calls=%async_computation | async-start | bytes 65536 | tf_op jit(solution)/shard_map/all_to_all | solution.py:32
  29.8 17.6 %all-to-all-start.1 = ((bf16[16,8,2048]{2,1,0:T(8,128)(2,1)}), bf16[16,8,2048]{2,1,0:T(8,128)(2,1)S(1)}, u32[]{:S(2)}, u32[]{:S(2)}) async-start(bf16[16,8,2048]{2,1,0:T(8,128)(2,1)} %broadcast_in_dim.127), calls=%async_computation.1 | async-start | bytes 1048576 | tf_op jit(solution)/shard_map/all_to_all | solution.py:32
  36.9 6.4 %copy-start.1 = (s32[1024,1]{0,1:T(1,128)S(1)}, s32[1024,1]{0,1:T(1,128)}, u32[]{:S(2)}) copy-start(s32[1024,1]{0,1:T(1,128)} %param.12) | copy-start | bytes 12292
  36.9 6.5 %copy-start = (s32[1024]{0:T(1024)S(1)}, s32[1024]{0:T(1024)}, u32[]{:S(2)}) copy-start(s32[1024]{0:T(1024)} %param.10) | copy-start | bytes 12292
  47.9 11.2 %copy-start.3 = (s32[128]{0:T(128)S(1)}, s32[128]{0:T(128)}, u32[]{:S(2)}) copy-start(s32[128]{0:T(128)} %param.13) | copy-start | bytes 1540
  47.9 16.5 %copy-start.2 = (s32[1024]{0:T(1024)S(1)}, s32[1024]{0:T(1024)}, u32[]{:S(2)}) copy-start(s32[1024]{0:T(1024)} %param.11) | copy-start | bytes 12292
  54.8 8.9 %all-to-all-start.2 = ((f32[8,2,1024]{2,1,0:T(2,128)}), f32[8,2,1024]{2,1,0:T(2,128)S(1)}, u32[]{:S(2)}, u32[]{:S(2)}) async-start(f32[8,2,1024]{2,1,0:T(2,128)} %broadcast_in_dim.130), calls=%async_computation.2 | async-start | bytes 131072 | tf_op jit(solution)/shard_map/all_to_all | solution.py:32
  137.4 18.5 %all-to-all-start.4 = ((f32[4,4,2176]{2,1,0:T(4,128)}), f32[4,4,2176]{2,1,0:T(4,128)S(1)}, u32[]{:S(2)}, u32[]{:S(2)}) async-start(f32[4,4,2176]{2,1,0:T(4,128)} %reshape.394), calls=%async_computation.4 | async-start | bytes 278528 | tf_op jit(solution)/shard_map/all_to_all | solution.py:32
  157.7 10.9 %all-to-all-start.5 = ((f32[16,1,128]{2,1,0:T(1,128)}), f32[16,1,128]{2,1,0:T(1,128)S(1)}, u32[]{:S(2)}, u32[]{:S(2)}) async-start(f32[16,1,128]{2,1,0:T(1,128)} %broadcast_in_dim.134), calls=%async_computation.5 | async-start | bytes 16384 | tf_op jit(solution)/shard_map/all_to_all | solution.py:32
  169.2 15.6 %all-to-all-start.6 = ((f32[4,1,128]{2,1,0:T(1,128)}), f32[4,1,128]{2,1,0:T(1,128)S(1)}, u32[]{:S(2)}, u32[]{:S(2)}) async-start(f32[4,1,128]{2,1,0:T(1,128)} %broadcast_in_dim.135), calls=%async_computation.6 | async-start | bytes 4096 | tf_op jit(solution)/shard_map/all_to_all | solution.py:32
  172.4 12.6 %collective-permute-start = (f32[2,2048]{1,0:T(2,128)S(1)}, f32[2,2048]{1,0:T(2,128)S(1)}, u32[]{:S(2)}, u32[]{:S(2)}) collective-permute-start(f32[2,2048]{1,0:T(2,128)S(1)} %broadcast_select_fusion), channel_id=1, source_target_pairs={{0,32},{16,48},{32,0},{48,16},{1,33},{17,49},{33,1},{49,17},{2,34}... | collective-permute-start | bytes 49160 | tf_op jit(solution)/shard_map/ppermute | solution.py:143

commit v2 on v0

v2 whole, which is shorter than its diff:
```python
import jax
import jax.numpy as jnp
from jax import lax
from jax.experimental import pallas as pl
from jax.experimental.pallas import tpu as pltpu
from jax.sharding import Mesh
from jax.sharding import PartitionSpec as P

PIXC = 1024
COLS = 2 * PIXC
ORIENT = 128
ROWS = 2 * ORIENT
NSHELL = 32
NBIN = 16
AXES = ("zl", "co", "y", "zh", "x")
CLS = ("zl", "co")
PTCL = ("y", "zh", "x")
PLANE = ("y", "x")
SIDE = 128
WIDE = COLS + SIDE
CODE = 32767.0
F32 = jnp.float32
BF16 = jnp.bfloat16
HIGHEST = lax.Precision.HIGHEST
PARAMS = pltpu.CompilerParams(vmem_limit_bytes=48 * 1024 * 1024)


def ctf_table():
    bins = jnp.arange(NBIN, dtype=F32)
    defocus = (bins + 1.0) / NBIN
    radius = (jnp.arange(PIXC, dtype=F32) + 0.5) / PIXC
    phase = 0.3 + 2.5 * defocus[:, None] * radius[None, :]
    return jnp.sin(phase) + 0.1 * jnp.cos(phase)


def lookup_small(indices, values):
    count = values.shape[0]
    match = indices[:, None] == jnp.arange(count, dtype=jnp.int32)[None, :]
    return jnp.sum(jnp.where(match, values[None, :], 0.0), axis=1)


def exchange(blocks, axes):
    return lax.all_to_all(blocks, axes, split_axis=0, concat_axis=0, tiled=True)


def from_all(shard, axes, count):
    return exchange(jnp.broadcast_to(shard[None], (count,) + shard.shape), axes)


def row_maps():
    r = jnp.arange(ROWS, dtype=jnp.int32)
    j, swap, zh, x, y = r % 2, (r // 2) % 2, (r // 4) % 4, (r // 16) % 4, r // 64
    direction = 4 * (((y % 2) * 4 + zh) * 4 + x) + 2 * (y // 2) + j
    return direction, (swap + y // 2) % 2


def gathered_orients():
    r = jnp.arange(ORIENT, dtype=jnp.int32)
    j, zh, x, y = r % 2, (r // 2) % 4, (r // 8) % 4, r // 32
    return ((y * 4 + zh) * 4 + x) * 2 + j


def three_parts(table, axis):
    high = table.astype(BF16)
    rest = table - high.astype(F32)
    mid = rest.astype(BF16)
    low = (rest - mid.astype(F32)).astype(BF16)
    return jnp.concatenate([high, mid, low], axis=axis)


def table_parts(table):
    high = lax.reduce_precision(table, 8, 7)
    mid = lax.reduce_precision(table - high, 8, 7)
    low = table - high - mid
    return jnp.concatenate([high, mid, low], axis=0).astype(BF16)


def bin_match(bins, copies):
    row = lax.broadcasted_iota(jnp.int32, (copies * NBIN, bins.shape[1]), 0)
    return jnp.where(row % NBIN == bins, 1.0, 0.0).astype(BF16)


def contract(left, right, dims):
    return lax.dot_general(left, right, (dims, ((), ())), preferred_element_type=F32)


def encode(values):
    top = jnp.max(jnp.abs(values), axis=1, keepdims=True)
    expo = jnp.floor(jnp.log2(jnp.maximum(top, 1e-30))) + 1.0
    root = jnp.sqrt(jnp.sqrt(jnp.minimum(jnp.abs(values) * jnp.exp2(-expo), 1.0)))
    size = jnp.floor(root * CODE + 0.5)
    codes = jnp.where(values < 0.0, -size, size).astype(jnp.int32).astype(jnp.int16)
    return codes, expo


def side_block(sums, expo, unit):
    fixed = jnp.floor(sums * unit + 0.5).astype(jnp.int32)
    high = lax.shift_right_arithmetic(fixed, 16)
    low = (fixed & 65535) - 32768
    tail = jnp.broadcast_to(expo.astype(jnp.int32), (sums.shape[0], SIDE - 2 * NBIN))
    return jnp.concatenate([high, low, tail], axis=1).astype(jnp.int16)


def decode_sum(ref, count, unit):
    data = jnp.zeros((ref.shape[1], COLS), F32)
    sums = jnp.zeros((ref.shape[1], NBIN), F32)
    for source in range(count):
        side = ref[source, :, COLS:].astype(jnp.int32)
        scale = jnp.exp2(side[:, SIDE - 1 :].astype(F32))
        root = ref[source, :, :COLS].astype(jnp.int32).astype(F32) * (1.0 / CODE)
        data = data + root * jnp.abs(root) * (root * root) * scale
        fixed = side[:, :NBIN] * 65536 + (side[:, NBIN : 2 * NBIN] + 32768)
        sums = sums + fixed.astype(F32) * (1.0 / unit)
    return data, sums


def image_kernel(x_ref, bins_ref, table_ref, noise_ref, centred_ref, weighted_ref):
    match = bin_match(bins_ref[...], 3)
    contrast = contract(match, table_ref[...], ((0,), (0,)))
    noise = noise_ref[...]
    for part in range(2):
        cols = slice(part * PIXC, (part + 1) * PIXC)
        product = x_ref[:, cols].astype(F32) * contrast
        centred_ref[:, cols] = product.astype(BF16)
        weighted_ref[:, cols] = (product * noise).astype(BF16)


def score_kernel(panel_ref, weighted_ref, power_ref, bins_ref, mask_ref, exp_ref, pair_ref, norm_ref):
    @pl.when(pl.program_id(0) == 0)
    def _():
        real = panel_ref[:, :PIXC].astype(F32)
        imag = panel_ref[:, PIXC:].astype(F32)
        panel_power = (real * real + imag * imag).astype(BF16)
        norm = contract(panel_power, power_ref[...], ((1,), (1,)))
        norm_ref[...] = three_parts(norm, 1)

    direct = contract(panel_ref[...], weighted_ref[...], ((1,), (1,)))
    norm_part = contract(norm_ref[...], bin_match(bins_ref[...], 3), ((1,), (0,)))
    scores = direct - 0.5 * norm_part
    allowed = mask_ref[...] > 0
    masked = jnp.where(allowed, scores, -1e30)
    peak = jnp.max(masked, axis=0, keepdims=True)
    weights = jnp.where(allowed, jnp.exp(masked - peak), 0.0)
    exp_ref[...] = weights
    total = jnp.sum(weights, axis=0, keepdims=True)
    pair = jnp.concatenate([peak, total], axis=0)
    pair_ref[...] = jnp.broadcast_to(pair[None], pair_ref.shape)


def project_kernel(
    exp_ref, own_ref, both_ref, permuter_ref, row_half_ref, half_ref, bins_ref, centred_ref,
    packed_ref, evidence_ref, post_ref, data_ref
):
    step = pl.program_id(0)
    width = centred_ref.shape[1]

    @pl.when(step == 0)
    def _():
        own_peak = own_ref[0, 0:1, :]
        peak = both_ref[0, 0:1, :]
        for c in range(1, both_ref.shape[0]):
            peak = jnp.maximum(peak, both_ref[c, 0:1, :])
        total = jnp.zeros_like(peak)
        for c in range(both_ref.shape[0]):
            total = total + both_ref[c, 1:2, :] * jnp.exp(both_ref[c, 0:1, :] - peak)
        evidence_ref[...] = peak + jnp.log(total)
        posterior = (exp_ref[...] * (jnp.exp(own_peak - peak) / total)).astype(BF16)
        by_direction = contract(permuter_ref[...], posterior, ((1,), (0,)))
        kept = row_half_ref[...] == half_ref[...]
        post_ref[...] = jnp.where(kept, by_direction, 0.0).astype(BF16)

    data_ref[step] = contract(post_ref[...], centred_ref[...], ((1,), (0,)))

    @pl.when(step == pl.num_programs(0) - 1)
    def _():
        sums = contract(post_ref[...], bin_match(bins_ref[...], 1), ((1,), (1,)))
        for block in range(16):
            rows = slice(block * 16, block * 16 + 16)
            values = jnp.concatenate(
                [data_ref[s, rows, :] for s in range(data_ref.shape[0])], axis=1
            )
            codes, expo = encode(values)
            packed_ref[block, :, :COLS] = codes
            packed_ref[block, :, COLS:] = side_block(sums[rows], expo, 2.0**20)


def plane_kernel(came_ref, packed_ref):
    data, sums = decode_sum(came_ref, 16, 2.0**20)
    codes, expo = encode(data)
    side = side_block(sums, expo, 2.0**16)
    for other in range(4):
        packed_ref[other, :, :COLS] = codes
        packed_ref[other, :, COLS:] = side


def shell_kernel(where_ref, came_ref, squares_ref, shells_ref, keep_ref, give_ref, stats_ref):
    upper = where_ref[0]
    zh = where_ref[1]
    data, sums = decode_sum(came_ref, 4, 2.0**16)
    cross = jnp.zeros((1, COLS), F32)
    first = jnp.zeros((1, COLS), F32)
    second = jnp.zeros((1, COLS), F32)
    own_data = jnp.zeros((4, COLS), F32)
    own_sums = jnp.zeros((4, NBIN), F32)
    for z in range(4):
        rows = data[4 * z : 4 * z + 4]
        own_data = jnp.where(zh == z, rows, own_data)
        own_sums = jnp.where(zh == z, sums[4 * z : 4 * z + 4], own_sums)
        cross = cross + jnp.sum(rows[:2] * rows[2:], axis=0, keepdims=True)
        first = first + jnp.sum(rows[:2] * rows[:2], axis=0, keepdims=True)
        second = second + jnp.sum(rows[2:] * rows[2:], axis=0, keepdims=True)
    power0 = jnp.where(upper == 0, first, second)
    power1 = jnp.where(upper == 0, second, first)
    three = jnp.concatenate([cross, power0, power1, jnp.zeros((5, COLS), F32)], axis=0)
    folded = three[:, :PIXC] + three[:, PIXC:]
    by_shell = jnp.dot(folded, shells_ref[...], precision=HIGHEST, preferred_element_type=F32)
    stats_ref[...] = jnp.broadcast_to(by_shell[None], stats_ref.shape)
    weight = jnp.dot(own_sums, squares_ref[...], precision=HIGHEST, preferred_element_type=F32)
    for part in range(2):
        cols = slice(part * PIXC, (part + 1) * PIXC)
        scaled = own_data[:, cols] / (weight + 1.0)
        keep_ref[:, cols] = scaled[:2]
        give_ref[:, cols] = scaled[2:]


def finish_kernel(where_ref, came_ref, keep_ref, got_ref, shells_ref, out_ref):
    totals = came_ref[0]
    for source in range(1, 16):
        totals = totals + came_ref[source]
    fsc = totals[0:1] / jnp.sqrt(totals[1:2] * totals[2:3] + 1e-06)
    half = jnp.broadcast_to((1.0 + fsc) / 2.0, (8, ORIENT))
    factor = lax.dot_general(
        half, shells_ref[...], (((1,), (1,)), ((), ())), precision=HIGHEST,
        preferred_element_type=F32,
    )[0:1]
    low = where_ref[0] == 0
    for part in range(2):
        cols = slice(part * PIXC, (part + 1) * PIXC)
        keep = keep_ref[:, cols] * factor
        got = got_ref[:, cols] * factor
        out_ref[0, 0:2, cols] = jnp.where(low, keep, got)
        out_ref[0, 2:4, cols] = jnp.where(low, got, keep)


def full(shape):
    return pl.BlockSpec(shape, lambda i: (0,) * len(shape))


def on_device(particles, panels, sigma2, defocus_bins, half_sets, prior_mask, orient_ids):
    count = particles.shape[0]
    block = count // 4
    by_zh = from_all(panels[0], "zh", 4).reshape(8, COLS)
    piece = from_all(by_zh, PLANE, 16).reshape(ORIENT, COLS)

    shells = jnp.arange(PIXC, dtype=jnp.int32) * NSHELL // PIXC
    inverse_noise = lookup_small(shells, 1.0 / sigma2)
    table = ctf_table()
    power = (table * table * inverse_noise[None, :]).astype(BF16)
    squares = (table * table).astype(BF16).astype(F32)
    shell_match = (shells[:, None] == jnp.arange(ORIENT, dtype=jnp.int32)[None, :]).astype(F32)
    bins_row = defocus_bins[None, :]
    where = jnp.stack([lax.axis_index("y") // 2, lax.axis_index("zh")]).astype(jnp.int32)

    direction, row_half = row_maps()
    match = gathered_orients()[:, None] == jnp.arange(ORIENT, dtype=jnp.int32)[None, :]
    select = jnp.sum(jnp.where(match, orient_ids[None, :], 0), axis=1)
    permuter = (direction[:, None] == select[None, :]).astype(BF16)

    centred, weighted = pl.pallas_call(
        image_kernel,
        grid=(4,),
        in_specs=[
            pl.BlockSpec((block, COLS), lambda i: (i, 0)),
            pl.BlockSpec((1, block), lambda i: (0, i)),
            full((3 * NBIN, PIXC)),
            full((1, PIXC)),
        ],
        out_specs=[pl.BlockSpec((block, COLS), lambda i: (i, 0))] * 2,
        out_shape=[jax.ShapeDtypeStruct((count, COLS), BF16)] * 2,
        compiler_params=PARAMS,
        name="images",
    )(particles, bins_row, table_parts(table), inverse_noise[None, :])

    own_exp, pair = pl.pallas_call(
        score_kernel,
        grid=(4,),
        in_specs=[
            full((ORIENT, COLS)),
            pl.BlockSpec((block, COLS), lambda i: (i, 0)),
            full((NBIN, PIXC)),
            pl.BlockSpec((1, block), lambda i: (0, i)),
            pl.BlockSpec((1, block), lambda i: (0, i)),
        ],
        out_specs=[
            pl.BlockSpec((ORIENT, block), lambda i: (0, i)),
            pl.BlockSpec((8, 2, block), lambda i: (0, 0, i)),
        ],
        out_shape=[
            jax.ShapeDtypeStruct((ORIENT, count), F32),
            jax.ShapeDtypeStruct((8, 2, count), F32),
        ],
        scratch_shapes=[pltpu.VMEM((ORIENT, 3 * NBIN), BF16)],
        compiler_params=PARAMS,
        name="scores",
    )(piece, weighted, power, bins_row, prior_mask.reshape(1, count))

    both = exchange(pair, CLS)
    packed, evidence = pl.pallas_call(
        project_kernel,
        grid=(4,),
        in_specs=[
            full((ORIENT, count)),
            full((8, 2, count)),
            full((8, 2, count)),
            full((ROWS, ORIENT)),
            full((ROWS, 1)),
            full((1, count)),
            full((1, count)),
            pl.BlockSpec((count, COLS // 4), lambda i: (0, i)),
        ],
        out_specs=[full((16, 16, WIDE)), full((1, count))],
        out_shape=[
            jax.ShapeDtypeStruct((16, 16, WIDE), jnp.int16),
            jax.ShapeDtypeStruct((1, count), F32),
        ],
        scratch_shapes=[
            pltpu.VMEM((ROWS, count), BF16),
            pltpu.VMEM((4, ROWS, COLS // 4), F32),
        ],
        compiler_params=PARAMS,
        name="project",
    )(own_exp, pair, both, permuter, row_half[:, None], half_sets[None, :], bins_row, centred)

    second = pl.pallas_call(
        plane_kernel,
        out_shape=jax.ShapeDtypeStruct((4, 16, WIDE), jnp.int16),
        compiler_params=PARAMS,
        name="plane",
    )(exchange(packed, PLANE))

    smem = pl.BlockSpec(memory_space=pltpu.SMEM)
    vmem = pl.BlockSpec(memory_space=pltpu.VMEM)
    keep, give, stats = pl.pallas_call(
        shell_kernel,
        in_specs=[smem, vmem, vmem, vmem],
        out_shape=[
            jax.ShapeDtypeStruct((2, COLS), F32),
            jax.ShapeDtypeStruct((2, COLS), F32),
            jax.ShapeDtypeStruct((16, 8, ORIENT), F32),
        ],
        compiler_params=PARAMS,
        name="shells",
    )(where, exchange(second, "zh"), squares, shell_match)

    got = lax.ppermute(give, "y", [(i, i ^ 2) for i in range(4)])
    half_maps = pl.pallas_call(
        finish_kernel,
        in_specs=[smem, vmem, vmem, vmem, vmem],
        out_shape=jax.ShapeDtypeStruct((1, 4, COLS), F32),
        compiler_params=PARAMS,
        name="finish",
    )(where, exchange(stats, PLANE), keep, got, shell_match)
    return (half_maps, evidence.reshape(count))


def solution(mesh):
    split = Mesh(mesh.devices.reshape(4, 2, 4, 4, 4), AXES)
    placed = (
        P(PTCL, None),
        P(CLS, PTCL, None),
        P(),
        P(PTCL),
        P(PTCL),
        P(PTCL, CLS),
        P(),
    )
    return jax.shard_map(
        on_device,
        mesh=split,
        in_specs=placed,
        out_specs=(P(CLS, PTCL, None), P(PTCL)),
        check_vma=False,
    )
```

time: 1380 us -> 134 us (0.10)
  the two profiles are of different devices: /device:TPU:32 before, /device:TPU:2 now
where the time goes in v2:
time: 134 us; the launch traced here: 133 us
  starting transfers between devices  39.2 us (29%)
  waiting for transfers between devices  39 us (29%)
  blocking collectives  23.3 us (17%)
  Pallas kernels  20 us (15%)
  local copies, waits for them, and re-layouts  9.27 us (7%)
  other arithmetic  1.78 us (1%)
    all_to_all x5, waiting for transfers between devices, exchange(): return lax.all_to_all(blocks, axes, split_axis=0, concat_axis=0, tiled=True)  36.7 us
    all_to_all x5, starting transfers between devices, exchange(): return lax.all_to_all(blocks, axes, split_axis=0, concat_axis=0, tiled=True)  34.3 us
    all_to_all x1, blocking collectives, exchange(): return lax.all_to_all(blocks, axes, split_axis=0, concat_axis=0, tiled=True)  23.3 us
    unnamed x16, local copies, waits for them, and re-layouts  7.03 us
    pallas_call x1, Pallas kernels, on_device(): pl.pallas_call(project_kernel, grid=(4,), in_specs=[full((ORIENT, count))...  6.04 us
    pallas_call x1, Pallas kernels, on_device(): pl.pallas_call(image_kernel, grid=(4,), in_specs=[pl.BlockSpec((block, CO...  5.66 us
    ppermute x1, starting transfers between devices, on_device(): got = lax.ppermute(give, 'y', [(i, i ^ 2) for i in range(4)])  4.87 us
    pallas_call x1, Pallas kernels, on_device(): pl.pallas_call(score_kernel, grid=(4,), in_specs=[full((ORIENT, COLS)), p...  3.23 us
  transfers between devices with their start and end apart: 6, of which 4 were waited for; matrix products, arithmetic and copies ran while one was open for 1% of the time, Pallas kernels for 4%

profile of v2, /device:TPU:2, one launch (start us, length us, event | category | flops | bytes accessed | tf_op | source)
XLA Modules:
  0.0 133.4 jit_solution(5108940153310552708)
XLA Ops:
  0.7 1.3 broadcast_in_dim.62
  2.0 15.1 %all-to-all-start = ((bf16[4,2,2048]{2,1,0:T(2,128)(2,1)}), bf16[4,2,2048]{2,1,0:T(2,128)(2,1)S(1)}, u32[]{:S(2)}, u32[]{:S(2)}) async-start(bf16[4,2,2048]{2,1,0:T(2,128)(2,1)} %broadcast_in_dim.62), calls=%async_computation | async-start | bytes 65536 | tf_op jit(solution)/shard_map/all_to_all | solution.py:43
  17.1 0.7 broadcast_divide_fusion
  17.9 12.0 %all-to-all-done = bf16[4,2,2048]{2,1,0:T(2,128)(2,1)S(1)} async-done(((bf16[4,2,2048]{2,1,0:T(2,128)(2,1)}), bf16[4,2,2048]{2,1,0:T(2,128)(2,1)S(1)}, u32[]{:S(2)}, u32[]{:S(2)}) %all-to-all-start) | async-done | bytes 32800 | tf_op jit(solution)/shard_map/all_to_all | solution.py:43
  29.8 0.9 broadcast_in_dim.64
  30.7 7.5 %all-to-all-start.1 = ((bf16[16,8,2048]{2,1,0:T(8,128)(2,1)}), bf16[16,8,2048]{2,1,0:T(8,128)(2,1)S(1)}, u32[]{:S(2)}, u32[]{:S(2)}) async-start(bf16[16,8,2048]{2,1,0:T(8,128)(2,1)} %broadcast_in_dim.64), calls=%async_computation.1 | async-start | bytes 1048576 | tf_op jit(solution)/shard_map/all_to_all | solution.py:43
  38.6 0.7 copy-done.3
  39.3 5.7 %images.1 = (bf16[1024,2048]{1,0:T(8,128)(2,1)S(1)}, bf16[1024,2048]{1,0:T(8,128)(2,1)}) custom-call(bf16[1024,2048]{1,0:T(8,128)(2,1)} %x_ref.1, s32[1,1024]{1,0:T(1,128)S(1)} %bitcast.10, bf16[48,1024]{1,0:T(8,128)(2,1)S(1)} %pad_maximum_fusion.table_ref, f32[1,1024]{1,0:T(1,128)S(1)} %bitcast.13), custom_call_target="tpu_custom_call" | custom-call | tf_op jit(solution)/shard_map/images/pallas_call | solution.py:269
  44.9 2.0 %copy-done = bf16[1024,2048]{1,0:T(8,128)(2,1)} copy-done((bf16[1024,2048]{1,0:T(8,128)(2,1)}, bf16[1024,2048]{1,0:T(8,128)(2,1)S(1)}, u32[]{:S(2)}) %copy-start) | copy-done | bytes 4194328
  47.2 2.2 %copy-done.2 = bf16[1024,2048]{1,0:T(8,128)(2,1)S(1)} copy-done((bf16[1024,2048]{1,0:T(8,128)(2,1)S(1)}, bf16[1024,2048]{1,0:T(8,128)(2,1)}, u32[]{:S(2)}) %copy-start.2) | copy-done | bytes 4194328
  49.4 3.2 %scores.1 = (f32[128,1024]{1,0:T(8,128)S(1)}, f32[8,2,1024]{2,1,0:T(2,128)}) custom-call(bf16[128,2048]{1,0:T(8,128)(2,1)S(1)} %bitcast.9, bf16[1024,2048]{1,0:T(8,128)(2,1)S(1)} %copy-done.2, bf16[16,1024]{1,0:T(8,128)(2,1)S(1)} %get-tuple-element.21.power_ref, s32[1,1024]{1,0:T(1,128)S(1)} %bitcast.11, s32[1,1024]{1,0:T(1,128)S(1)} %bitcast.14), custom_call_target="tpu_custom_call" | custom-call | tf_op jit(solution)/shard_map/scores/pallas_call | solution.py:284
  52.6 3.3 %all-to-all-start.2 = ((f32[8,2,1024]{2,1,0:T(2,128)}), f32[8,2,1024]{2,1,0:T(2,128)S(1)}, u32[]{:S(2)}, u32[]{:S(2)}) async-start(f32[8,2,1024]{2,1,0:T(2,128)} %get-tuple-element.13.own_ref), calls=%async_computation.2 | async-start | bytes 131072 | tf_op jit(solution)/shard_map/all_to_all | solution.py:43
  56.1 5.7 %all-to-all-done.2.both_ref = f32[8,2,1024]{2,1,0:T(2,128)S(1)} async-done(((f32[8,2,1024]{2,1,0:T(2,128)}), f32[8,2,1024]{2,1,0:T(2,128)S(1)}, u32[]{:S(2)}, u32[]{:S(2)}) %all-to-all-start.2) | async-done | bytes 65568 | tf_op jit(solution)/shard_map/all_to_all | solution.py:43
  61.8 2.2 %copy-done.1 = bf16[1024,2048]{1,0:T(8,128)(2,1)S(1)} copy-done((bf16[1024,2048]{1,0:T(8,128)(2,1)S(1)}, bf16[1024,2048]{1,0:T(8,128)(2,1)}, u32[]{:S(2)}) %copy-start.1) | copy-done | bytes 4194328
  64.0 6.0 %project.1 = (s16[16,16,2176]{2,1,0:T(8,128)(2,1)S(1)}, f32[1,1024]{1,0:T(1,128)}) custom-call(f32[128,1024]{1,0:T(8,128)S(1)} %get-tuple-element.12.exp_ref, f32[8,2,1024]{2,1,0:T(2,128)} %get-tuple-element.13.own_ref, f32[8,2,1024]{2,1,0:T(2,128)S(1)} %all-to-all-done.2.both_ref, bf16[256,128]{1,0:T(8,128)(2,1)S(1)} %compare_convert_fusion.permuter_ref, ...), custom_call_target="tpu_custom_call" | custom-call | tf_op jit(solution)/shard_map/project/pallas_call | solution.py:308
  70.0 23.3 %all_to_all.30.came_ref = s16[16,16,2176]{2,1,0:T(8,128)(2,1)S(1)} all-to-all(s16[16,16,2176]{2,1,0:T(8,128)(2,1)S(1)} %get-tuple-element.15), channel_id=1, replica_groups=mesh['zl'=4,'co'=2,'y'=4,'zh'=4,'x'=4] {'y','x'}, dimensions={0} | all-to-all | bytes 2228224 | tf_op jit(solution)/shard_map/all_to_all | solution.py:43
  93.4 1.5 %plane.1 = s16[4,16,2176]{2,1,0:T(8,128)(2,1)} custom-call(s16[16,16,2176]{2,1,0:T(8,128)(2,1)S(1)} %all_to_all.30.came_ref), custom_call_target="tpu_custom_call" | custom-call | tf_op jit(solution)/shard_map/plane/pallas_call | solution.py:334
  94.9 3.4 %all-to-all-start.4 = ((s16[4,16,2176]{2,1,0:T(8,128)(2,1)}), s16[4,16,2176]{2,1,0:T(8,128)(2,1)S(1)}, u32[]{:S(2)}, u32[]{:S(2)}) async-start(s16[4,16,2176]{2,1,0:T(8,128)(2,1)} %plane.1), calls=%async_computation.4 | async-start | bytes 557056 | tf_op jit(solution)/shard_map/all_to_all | solution.py:43
  98.7 19.1 %all-to-all-done.4.came_ref = s16[4,16,2176]{2,1,0:T(8,128)(2,1)S(1)} async-done(((s16[4,16,2176]{2,1,0:T(8,128)(2,1)}), s16[4,16,2176]{2,1,0:T(8,128)(2,1)S(1)}, u32[]{:S(2)}, u32[]{:S(2)}) %all-to-all-start.4) | async-done | bytes 278560 | tf_op jit(solution)/shard_map/all_to_all | solution.py:43
  117.7 1.9 %shells.1 = (f32[2,2048]{1,0:T(2,128)S(1)}, f32[2,2048]{1,0:T(2,128)S(1)}, f32[16,8,128]{2,1,0:T(8,128)}) custom-call(s32[2]{0:T(128)S(1)} %pad_add_fusion.where_ref, s16[4,16,2176]{2,1,0:T(8,128)(2,1)S(1)} %all-to-all-done.4.came_ref, f32[16,1024]{1,0:T(8,128)S(1)} %get-tuple-element.20.squares_ref, f32[1024,128]{1,0:T(8,128)S(1)} %fusion.shells_ref), custom_call_target="tpu_custom_call" | custom-call | tf_op jit(solution)/shard_map/shells/pallas_call | solution.py:343
  119.6 4.9 %all-to-all-start.5 = ((f32[16,8,128]{2,1,0:T(8,128)}), f32[16,8,128]{2,1,0:T(8,128)S(1)}, u32[]{:S(2)}, u32[]{:S(2)}) async-start(f32[16,8,128]{2,1,0:T(8,128)} %get-tuple-element.16), calls=%async_computation.5 | async-start | bytes 131072 | tf_op jit(solution)/shard_map/all_to_all | solution.py:43
  124.5 4.9 %collective-permute-start = (f32[2,2048]{1,0:T(2,128)S(1)}, f32[2,2048]{1,0:T(2,128)S(1)}, u32[]{:S(2)}, u32[]{:S(2)}) collective-permute-start(f32[2,2048]{1,0:T(2,128)S(1)} %get-tuple-element.18), channel_id=1, source_target_pairs={{0,32},{16,48},{32,0},{48,16},{1,33},{17,49},{33,1},{49,17},{2,34}... | collective-permute-start | bytes 49160 | tf_op jit(solution)/shard_map/ppermute | solution.py:355
  129.4 2.2 %collective-permute-done.got_ref = f32[2,2048]{1,0:T(2,128)S(1)} collective-permute-done((f32[2,2048]{1,0:T(2,128)S(1)}, f32[2,2048]{1,0:T(2,128)S(1)}, u32[]{:S(2)}, u32[]{:S(2)}) %collective-permute-start) | collective-permute-done | bytes 16416 | tf_op jit(solution)/shard_map/ppermute | solution.py:355
  131.7 1.7 %finish.1 = f32[1,4,2048]{2,1,0:T(4,128)} custom-call(s32[2]{0:T(128)S(1)} %pad_add_fusion.where_ref, f32[16,8,128]{2,1,0:T(8,128)S(1)} %all-to-all-done.5.came_ref, f32[2,2048]{1,0:T(2,128)S(1)} %get-tuple-element.17.keep_ref, f32[2,2048]{1,0:T(2,128)S(1)} %collective-permute-done.got_ref, f32[1024,128]{1,0:T(8,128)S(1)} %fusion.shells_ref), custom_call_target="tpu_custom_call" | custom-call | tf_op jit(solution)/shard_map/finish/pallas_call | solution.py:356
  (28 shorter events, 1.2 us)
Async XLA Ops:
  0.6 46.6 %copy-start.4 = (s32[1024]{0:T(1024)S(1)}, s32[1024]{0:T(1024)}, u32[]{:S(2)}) copy-start(s32[1024]{0:T(1024)} %param.10) | copy-start | bytes 12292
  0.6 46.2 %copy-start.7 = (s32[128]{0:T(128)S(1)}, s32[128]{0:T(128)}, u32[]{:S(2)}) copy-start(s32[128]{0:T(128)} %param.13) | copy-start | bytes 1540
  0.7 46.5 %copy-start.5 = (s32[1024,1]{0,1:T(1,128)S(1)}, s32[1024,1]{0,1:T(1,128)}, u32[]{:S(2)}) copy-start(s32[1024,1]{0,1:T(1,128)} %param.12) | copy-start | bytes 12292
  2.0 27.8 %all-to-all-start = ((bf16[4,2,2048]{2,1,0:T(2,128)(2,1)}), bf16[4,2,2048]{2,1,0:T(2,128)(2,1)S(1)}, u32[]{:S(2)}, u32[]{:S(2)}) async-start(bf16[4,2,2048]{2,1,0:T(2,128)(2,1)} %broadcast_in_dim.62), calls=%async_computation | async-start | bytes 65536 | tf_op jit(solution)/shard_map/all_to_all | solution.py:43
  30.7 16.4 %all-to-all-start.1 = ((bf16[16,8,2048]{2,1,0:T(8,128)(2,1)}), bf16[16,8,2048]{2,1,0:T(8,128)(2,1)S(1)}, u32[]{:S(2)}, u32[]{:S(2)}) async-start(bf16[16,8,2048]{2,1,0:T(8,128)(2,1)} %broadcast_in_dim.64), calls=%async_computation.1 | async-start | bytes 1048576 | tf_op jit(solution)/shard_map/all_to_all | solution.py:43
  38.6 0.7 copy-start.3
  39.3 22.6 %copy-start.6 = (s32[1024]{0:T(1024)S(1)}, s32[1024]{0:T(1024)}, u32[]{:S(2)}) copy-start(s32[1024]{0:T(1024)} %param.11) | copy-start | bytes 12292
  44.9 2.0 %copy-start = (bf16[1024,2048]{1,0:T(8,128)(2,1)}, bf16[1024,2048]{1,0:T(8,128)(2,1)S(1)}, u32[]{:S(2)}) copy-start(bf16[1024,2048]{1,0:T(8,128)(2,1)S(1)} %get-tuple-element.14.centred_ref) | copy-start | bytes 12582916
  47.2 2.2 %copy-start.2 = (bf16[1024,2048]{1,0:T(8,128)(2,1)S(1)}, bf16[1024,2048]{1,0:T(8,128)(2,1)}, u32[]{:S(2)}) copy-start(bf16[1024,2048]{1,0:T(8,128)(2,1)} %get-tuple-element.11.weighted_ref) | copy-start | bytes 12582916
  52.6 9.2 %all-to-all-start.2 = ((f32[8,2,1024]{2,1,0:T(2,128)}), f32[8,2,1024]{2,1,0:T(2,128)S(1)}, u32[]{:S(2)}, u32[]{:S(2)}) async-start(f32[8,2,1024]{2,1,0:T(2,128)} %get-tuple-element.13.own_ref), calls=%async_computation.2 | async-start | bytes 131072 | tf_op jit(solution)/shard_map/all_to_all | solution.py:43
  61.8 2.2 %copy-start.1 = (bf16[1024,2048]{1,0:T(8,128)(2,1)S(1)}, bf16[1024,2048]{1,0:T(8,128)(2,1)}, u32[]{:S(2)}) copy-start(bf16[1024,2048]{1,0:T(8,128)(2,1)} %copy-done) | copy-start | bytes 12582916
  94.9 22.8 %all-to-all-start.4 = ((s16[4,16,2176]{2,1,0:T(8,128)(2,1)}), s16[4,16,2176]{2,1,0:T(8,128)(2,1)S(1)}, u32[]{:S(2)}, u32[]{:S(2)}) async-start(s16[4,16,2176]{2,1,0:T(8,128)(2,1)} %plane.1), calls=%async_computation.4 | async-start | bytes 557056 | tf_op jit(solution)/shard_map/all_to_all | solution.py:43
  119.6 12.1 %all-to-all-start.5 = ((f32[16,8,128]{2,1,0:T(8,128)}), f32[16,8,128]{2,1,0:T(8,128)S(1)}, u32[]{:S(2)}, u32[]{:S(2)}) async-start(f32[16,8,128]{2,1,0:T(8,128)} %get-tuple-element.16), calls=%async_computation.5 | async-start | bytes 131072 | tf_op jit(solution)/shard_map/all_to_all | solution.py:43
  124.5 7.1 %collective-permute-start = (f32[2,2048]{1,0:T(2,128)S(1)}, f32[2,2048]{1,0:T(2,128)S(1)}, u32[]{:S(2)}, u32[]{:S(2)}) collective-permute-start(f32[2,2048]{1,0:T(2,128)S(1)} %get-tuple-element.18), channel_id=1, source_target_pairs={{0,32},{16,48},{32,0},{48,16},{1,33},{17,49},{33,1},{49,17},{2,34}... | collective-permute-start | bytes 49160 | tf_op jit(solution)/shard_map/ppermute | solution.py:355

commit v3 on v0

v3 whole, which is shorter than its diff:
```python
import jax
import jax.numpy as jnp
from jax import lax
from jax.experimental import pallas as pl
from jax.experimental.pallas import tpu as pltpu
from jax.sharding import Mesh
from jax.sharding import PartitionSpec as P

PIXC = 1024
COLS = 2 * PIXC
ORIENT = 128
ROWS = 2 * ORIENT
NSHELL = 32
NBIN = 16
AXES = ("zl", "co", "y", "zh", "x")
CLS = ("zl", "co")
PTCL = ("y", "zh", "x")
PLANE = ("y", "x")
SIDE = 128
WIDE = COLS + SIDE
CODE = 32767.0
PARTS = 4
PART = COLS // PARTS
F32 = jnp.float32
BF16 = jnp.bfloat16
HIGHEST = lax.Precision.HIGHEST


def ctf_table():
    bins = jnp.arange(NBIN, dtype=F32)
    defocus = (bins + 1.0) / NBIN
    radius = (jnp.arange(PIXC, dtype=F32) + 0.5) / PIXC
    phase = 0.3 + 2.5 * defocus[:, None] * radius[None, :]
    return jnp.sin(phase) + 0.1 * jnp.cos(phase)


def lookup_small(indices, values):
    count = values.shape[0]
    match = indices[:, None] == jnp.arange(count, dtype=jnp.int32)[None, :]
    return jnp.sum(jnp.where(match, values[None, :], 0.0), axis=1)


def exchange(blocks, axes):
    return lax.all_to_all(blocks, axes, split_axis=0, concat_axis=0, tiled=True)


def from_all(shard, axes, count):
    return exchange(jnp.broadcast_to(shard[None], (count,) + shard.shape), axes)


def row_maps():
    r = jnp.arange(ROWS, dtype=jnp.int32)
    j, swap, zh, x, y = r % 2, (r // 2) % 2, (r // 4) % 4, (r // 16) % 4, r // 64
    direction = 4 * (((y % 2) * 4 + zh) * 4 + x) + 2 * (y // 2) + j
    return direction, (swap + y // 2) % 2


def gathered_orients():
    r = jnp.arange(ORIENT, dtype=jnp.int32)
    j, zh, x, y = r % 2, (r // 2) % 4, (r // 8) % 4, r // 32
    return ((y * 4 + zh) * 4 + x) * 2 + j


def three_parts(table, axis):
    high = table.astype(BF16)
    rest = table - high.astype(F32)
    mid = rest.astype(BF16)
    low = (rest - mid.astype(F32)).astype(BF16)
    return jnp.concatenate([high, mid, low], axis=axis)


def table_parts(table):
    high = lax.reduce_precision(table, 8, 7)
    mid = lax.reduce_precision(table - high, 8, 7)
    low = table - high - mid
    return jnp.concatenate([high, mid, low], axis=0).astype(BF16)


def bin_match(bins, copies):
    row = lax.broadcasted_iota(jnp.int32, (copies * NBIN, bins.shape[1]), 0)
    return jnp.where(row % NBIN == bins, 1.0, 0.0).astype(BF16)


def contract(left, right, dims):
    return lax.dot_general(left, right, (dims, ((), ())), preferred_element_type=F32)


def encode(values):
    size = jnp.abs(values)
    top = jnp.max(size, axis=1, keepdims=True)
    expo = jnp.floor(jnp.log2(jnp.maximum(top, 1e-30))) + 1.0
    root = lax.rsqrt(lax.rsqrt(jnp.maximum(size * jnp.exp2(-expo), 1e-36)))
    code = root * CODE + 0.5
    codes = jnp.where(values < 0.0, -code, code).astype(jnp.int32).astype(jnp.int16)
    return codes, expo


def side_block(sums, expos, unit):
    fixed = jnp.floor(sums * unit + 0.5).astype(jnp.int32)
    high = lax.shift_right_arithmetic(fixed, 16)
    low = (fixed & 65535) - 32768
    shape = (sums.shape[0], SIDE - 2 * NBIN)
    lane = lax.broadcasted_iota(jnp.int32, shape, 1)
    tail = jnp.zeros(shape, F32)
    for part, expo in enumerate(expos):
        tail = jnp.where(lane == part, expo, tail)
    return jnp.concatenate([high, low, tail.astype(jnp.int32)], axis=1).astype(jnp.int16)


def decode_part(ref, count, part):
    cols = slice(part * PART, (part + 1) * PART)
    at = COLS + 2 * NBIN + part
    data = jnp.zeros((ref.shape[1], PART), F32)
    for source in range(count):
        expo = ref[source, :, COLS:].astype(jnp.int32)[:, at - COLS : at - COLS + 1]
        scale = jnp.exp2(expo.astype(F32)) * (1.0 / CODE**4)
        root = ref[source, :, cols].astype(jnp.int32).astype(F32)
        data = data + root * jnp.abs(root) * (root * root) * scale
    return data


def decode_bins(ref, count, unit):
    sums = jnp.zeros((ref.shape[1], NBIN), F32)
    for source in range(count):
        side = ref[source, :, COLS:].astype(jnp.int32)
        fixed = side[:, :NBIN] * 65536 + (side[:, NBIN : 2 * NBIN] + 32768)
        sums = sums + fixed.astype(F32) * (1.0 / unit)
    return sums


def image_kernel(
    x_ref, bins_ref, table_ref, noise_ref, centred_ref, weighted_ref, x_buf, centred_buf,
    weighted_buf, sems
):
    noise = noise_ref[...]
    step = x_buf.shape[0] // PARTS
    spans = [slice(i * step, (i + 1) * step) for i in range(PARTS)]
    reads, writes = [], []
    for i, rows in enumerate(spans):
        reads.append(pltpu.make_async_copy(x_ref.at[rows], x_buf.at[rows], sems.at[0, i]))
        reads[i].start()
    for i, rows in enumerate(spans):
        match = bin_match(bins_ref[:, rows], 3)
        contrast = contract(match, table_ref[...], ((0,), (0,)))
        reads[i].wait()
        for part in range(2):
            cols = slice(part * PIXC, (part + 1) * PIXC)
            product = x_buf[rows, cols].astype(F32) * contrast
            centred_buf[rows, cols] = product.astype(BF16)
            weighted_buf[rows, cols] = (product * noise).astype(BF16)
        for k, buf, out in ((1, centred_buf, centred_ref), (2, weighted_buf, weighted_ref)):
            writes.append(pltpu.make_async_copy(buf.at[rows], out.at[rows], sems.at[k, i]))
            writes[-1].start()
    for write in writes:
        write.wait()


def score_kernel(
    panel_ref, power_ref, bins_ref, mask_ref, weighted_ref, exp_ref, pair_ref, weighted_buf, sems
):
    step = weighted_buf.shape[0] // PARTS
    reads = []
    for i in range(PARTS):
        rows = slice(i * step, (i + 1) * step)
        reads.append(
            pltpu.make_async_copy(weighted_ref.at[rows], weighted_buf.at[rows], sems.at[i])
        )
        reads[i].start()
    real = panel_ref[:, :PIXC].astype(F32)
    imag = panel_ref[:, PIXC:].astype(F32)
    panel_power = (real * real + imag * imag).astype(BF16)
    norm = three_parts(contract(panel_power, power_ref[...], ((1,), (1,))), 1)
    for i in range(PARTS):
        rows = slice(i * step, (i + 1) * step)
        norm_part = contract(norm, bin_match(bins_ref[:, rows], 3), ((1,), (0,)))
        reads[i].wait()
        direct = contract(panel_ref[...], weighted_buf[rows, :], ((1,), (1,)))
        scores = direct - 0.5 * norm_part
        allowed = mask_ref[:, rows] > 0
        masked = jnp.where(allowed, scores, -1e30)
        peak = jnp.max(masked, axis=0, keepdims=True)
        weights = jnp.where(allowed, jnp.exp(masked - peak), 0.0)
        exp_ref[:, rows] = weights
        total = jnp.sum(weights, axis=0, keepdims=True)
        pair = jnp.concatenate([peak, total], axis=0)
        for other in range(8):
            pair_ref[other, :, rows] = pair


def project_kernel(
    exp_ref, own_ref, both_ref, permuter_ref, row_half_ref, half_ref, bins_ref, centred_ref,
    packed_ref, evidence_ref, centred_buf, sems
):
    spans = [slice(part * PART, (part + 1) * PART) for part in range(PARTS)]
    reads = []
    for part, cols in enumerate(spans):
        reads.append(
            pltpu.make_async_copy(centred_ref.at[:, cols], centred_buf.at[:, cols], sems.at[part])
        )
        reads[part].start()
    own_peak = own_ref[0, 0:1, :]
    peak = both_ref[0, 0:1, :]
    for c in range(1, both_ref.shape[0]):
        peak = jnp.maximum(peak, both_ref[c, 0:1, :])
    total = jnp.zeros_like(peak)
    for c in range(both_ref.shape[0]):
        total = total + both_ref[c, 1:2, :] * jnp.exp(both_ref[c, 0:1, :] - peak)
    evidence_ref[...] = peak + jnp.log(total)
    posterior = (exp_ref[...] * (jnp.exp(own_peak - peak) / total)).astype(BF16)
    by_direction = contract(permuter_ref[...], posterior, ((1,), (0,)))
    kept = row_half_ref[...] == half_ref[...]
    post = jnp.where(kept, by_direction, 0.0).astype(BF16)
    sums = contract(post, bin_match(bins_ref[...], 1), ((1,), (1,)))
    expos = []
    for part, cols in enumerate(spans):
        reads[part].wait()
        codes, expo = encode(contract(post, centred_buf[:, cols], ((1,), (0,))))
        expos.append(expo)
        packed_ref[:, cols] = codes
    packed_ref[:, COLS:] = side_block(sums, expos, 2.0**20)


def plane_kernel(came_ref, packed_ref):
    expos = []
    for part in range(PARTS):
        codes, expo = encode(decode_part(came_ref, 16, part))
        expos.append(expo)
        for other in range(4):
            packed_ref[other, :, part * PART : (part + 1) * PART] = codes
    side = side_block(decode_bins(came_ref, 16, 2.0**20), expos, 2.0**16)
    for other in range(4):
        packed_ref[other, :, COLS:] = side


def shell_kernel(where_ref, came_ref, squares_ref, shells_ref, keep_ref, stats_ref):
    upper = where_ref[0]
    zh = where_ref[1]
    data = jnp.concatenate([decode_part(came_ref, 4, part) for part in range(PARTS)], axis=1)
    sums = decode_bins(came_ref, 4, 2.0**16)
    cross = jnp.zeros((1, COLS), F32)
    first = jnp.zeros((1, COLS), F32)
    second = jnp.zeros((1, COLS), F32)
    own_data = jnp.zeros((4, COLS), F32)
    own_sums = jnp.zeros((4, NBIN), F32)
    for z in range(4):
        rows = data[4 * z : 4 * z + 4]
        own_data = jnp.where(zh == z, rows, own_data)
        own_sums = jnp.where(zh == z, sums[4 * z : 4 * z + 4], own_sums)
        cross = cross + jnp.sum(rows[:2] * rows[2:], axis=0, keepdims=True)
        first = first + jnp.sum(rows[:2] * rows[:2], axis=0, keepdims=True)
        second = second + jnp.sum(rows[2:] * rows[2:], axis=0, keepdims=True)
    power0 = jnp.where(upper == 0, first, second)
    power1 = jnp.where(upper == 0, second, first)
    three = jnp.concatenate([cross, power0, power1, jnp.zeros((5, COLS), F32)], axis=0)
    folded = three[:, :PIXC] + three[:, PIXC:]
    by_shell = jnp.dot(folded, shells_ref[...], precision=HIGHEST, preferred_element_type=F32)
    weight = jnp.dot(own_sums, squares_ref[...], precision=HIGHEST, preferred_element_type=F32)
    whole = own_data / (jnp.concatenate([weight, weight], axis=1) + 1.0)
    keep_ref[...] = whole[:2]
    for other in range(16):
        stats_ref[other, :, PART:] = by_shell
    for part in range(PARTS):
        piece = whole[2:, part * PART : (part + 1) * PART]
        for other in range(16):
            stats_ref[other, 2 * part : 2 * part + 2, :PART] = piece


def finish_kernel(where_ref, came_ref, keep_ref, shells_ref, out_ref):
    totals = came_ref[0, :, PART:]
    for source in range(1, 16):
        totals = totals + came_ref[source, :, PART:]
    fsc = totals[0:1] / jnp.sqrt(totals[1:2] * totals[2:3] + 1e-06)
    half = jnp.broadcast_to((1.0 + fsc) / 2.0, (8, ORIENT))
    factor = lax.dot_general(
        half, shells_ref[...], (((1,), (1,)), ((), ())), precision=HIGHEST,
        preferred_element_type=F32,
    )[0:1]
    low = where_ref[0] == 0
    partner = came_ref[where_ref[2]]
    for part in range(PARTS):
        cols = slice(part * PART, (part + 1) * PART)
        start = (part * PART) % PIXC
        scale = factor[:, start : start + PART]
        keep = keep_ref[:, cols] * scale
        got = partner[2 * part : 2 * part + 2, :PART] * scale
        out_ref[0, 0:2, cols] = jnp.where(low, keep, got)
        out_ref[0, 2:4, cols] = jnp.where(low, got, keep)


def call(kernel, name, out_shape, mega, *args, scalars=0, far=(), far_out=(), scratch=()):
    def space(i, hbm):
        if i < 0:
            return pl.BlockSpec(memory_space=pltpu.MemorySpace.SMEM)
        return pl.BlockSpec(
            memory_space=pltpu.MemorySpace.HBM if i in hbm else pltpu.MemorySpace.VMEM
        )

    args = [
        pltpu.with_memory_space_constraint(arg, pltpu.MemorySpace.HBM) if i in far else arg
        for i, arg in enumerate(args)
    ]
    return pl.pallas_call(
        kernel,
        in_specs=[space(i if i >= scalars else -1, far) for i in range(len(args))],
        out_specs=[space(i, far_out) for i in range(len(out_shape))],
        out_shape=out_shape,
        scratch_shapes=scratch,
        compiler_params=pltpu.CompilerParams(vmem_limit_bytes=mega * 1024 * 1024),
        name=name,
    )(*args)


def on_device(particles, panels, sigma2, defocus_bins, half_sets, prior_mask, orient_ids):
    count = particles.shape[0]
    of = jax.ShapeDtypeStruct

    shells = jnp.arange(PIXC, dtype=jnp.int32) * NSHELL // PIXC
    inverse_noise = lookup_small(shells, 1.0 / sigma2)
    table = ctf_table()
    power = (table * table * inverse_noise[None, :]).astype(BF16)
    squares = (table * table).astype(BF16).astype(F32)
    shell_match = (shells[:, None] == jnp.arange(ORIENT, dtype=jnp.int32)[None, :]).astype(F32)
    bins_row = defocus_bins[None, :]
    y, zh, x = lax.axis_index("y"), lax.axis_index("zh"), lax.axis_index("x")
    where = jnp.stack([y // 2, zh, (y ^ 2) * 4 + x]).astype(jnp.int32)

    direction, row_half = row_maps()
    match = gathered_orients()[:, None] == jnp.arange(ORIENT, dtype=jnp.int32)[None, :]
    select = jnp.sum(jnp.where(match, orient_ids[None, :], 0), axis=1)
    permuter = (direction[:, None] == select[None, :]).astype(BF16)

    images = pltpu.VMEM((count, COLS), BF16)
    centred, weighted = call(
        image_kernel, "images", [pltpu.MemorySpace.HBM((count, COLS), BF16)] * 2, 24,
        particles, bins_row, table_parts(table), inverse_noise[None, :],
        far=(0,), far_out=(0, 1),
        scratch=[images] * 3 + [pltpu.SemaphoreType.DMA((3, PARTS))],
    )
    by_zh = from_all(panels[0], "zh", 4)
    by_zh, centred, weighted = lax.optimization_barrier((by_zh, centred, weighted))
    piece = from_all(by_zh.reshape(8, COLS), PLANE, 16).reshape(ORIENT, COLS)

    own_exp, pair = call(
        score_kernel, "scores", [of((ORIENT, count), F32), of((8, 2, count), F32)], 14,
        piece, power, bins_row, prior_mask.reshape(1, count), weighted,
        far=(4,), scratch=[images, pltpu.SemaphoreType.DMA((PARTS,))],
    )
    packed, evidence = call(
        project_kernel, "project", [of((ROWS, WIDE), jnp.int16), of((1, count), F32)], 20,
        own_exp, pair, exchange(pair, CLS), permuter, row_half[:, None], half_sets[None, :],
        bins_row, centred, far=(7,), scratch=[images, pltpu.SemaphoreType.DMA((PARTS,))],
    )
    (second,) = call(
        plane_kernel, "plane", [of((4, 16, WIDE), jnp.int16)], 8,
        exchange(packed.reshape(16, 16, WIDE), PLANE),
    )
    keep, stats = call(
        shell_kernel, "shells", [of((2, COLS), F32), of((16, 8, PART + ORIENT), F32)], 8,
        where, exchange(second, "zh"), squares, shell_match, scalars=1,
    )
    (half_maps,) = call(
        finish_kernel, "finish", [of((1, 4, COLS), F32)], 8,
        where, exchange(stats, PLANE), keep, shell_match, scalars=1,
    )
    return (half_maps, evidence.reshape(count))


def solution(mesh):
    split = Mesh(mesh.devices.reshape(4, 2, 4, 4, 4), AXES)
    placed = (
        P(PTCL, None),
        P(CLS, PTCL, None),
        P(),
        P(PTCL),
        P(PTCL),
        P(PTCL, CLS),
        P(),
    )
    return jax.shard_map(
        on_device,
        mesh=split,
        in_specs=placed,
        out_specs=(P(CLS, PTCL, None), P(PTCL)),
        check_vma=False,
    )
```

time: 1380 us -> 132 us (0.10)
  waiting for transfers between devices: 852 us -> 39.2 us
  blocking collectives: 480 us -> 32.8 us
  starting transfers between devices: 1.96 us -> 33.4 us
  Pallas kernels: 0 us -> 20.7 us
  between operations: 14.9 us -> 0.78 us
    unnamed x2 -> x0, waiting for transfers between devices: 848 us -> none
    psum x2 -> x0, blocking collectives: 236 us -> none  [the longest x1 223 us: on_device(): totals = lax.psum(stats, 'ptcl')]
    all_gather x1 -> x0, blocking collectives: 234 us -> none  [on_device(): piece = lax.all_gather(panels[0], 'ptcl', axis=0, tiled=True)]
    all_to_all x0 -> x4, waiting for transfers between devices: none -> 39.2 us  [exchange(): return lax.all_to_all(blocks, axes, split_axis=0, concat_axis=0, tiled=True)]
    all_to_all x0 -> x4, starting transfers between devices: none -> 33.4 us  [exchange(): return lax.all_to_all(blocks, axes, split_axis=0, concat_axis=0, tiled=True)]
    all_to_all x0 -> x2, blocking collectives: none -> 32.8 us  [exchange(): return lax.all_to_all(blocks, axes, split_axis=0, concat_axis=0, tiled=True)]
    pallas_call x0 -> x6, Pallas kernels: none -> 20.7 us  [call(): pl.pallas_call(kernel, in_specs=[space(i if i >= scalars else -1, far) fo...]
  transfers between devices with their start and end apart: 2 -> 4, of which waited for: 2 -> 4; matrix products, arithmetic and copies ran while one was open for 0% -> 1% of each run, Pallas kernels for 0% -> 4%
where the time goes in v3:
time: 132 us
  waiting for transfers between devices  39.2 us (30%)
  starting transfers between devices  33.4 us (25%)
  blocking collectives  32.8 us (25%)
  Pallas kernels  20.7 us (16%)
  local copies, waits for them, and re-layouts  2.93 us (2%)
  other arithmetic  1.78 us (1%)
    all_to_all x4, waiting for transfers between devices, exchange(): return lax.all_to_all(blocks, axes, split_axis=0, concat_axis=0, tiled=True)  39.2 us
    all_to_all x4, starting transfers between devices, exchange(): return lax.all_to_all(blocks, axes, split_axis=0, concat_axis=0, tiled=True)  33.4 us
    all_to_all x2, blocking collectives, exchange(): return lax.all_to_all(blocks, axes, split_axis=0, concat_axis=0, tiled=True)  32.8 us
    pallas_call x6, Pallas kernels, call(): pl.pallas_call(kernel, in_specs=[space(i if i >= scalars else -1, far) fo...  20.7 us
  transfers between devices with their start and end apart: 4, of which 4 were waited for; matrix products, arithmetic and copies ran while one was open for 1% of the time, Pallas kernels for 4%

profile of v3, /device:TPU:32, one launch (start us, length us, event | category | flops | bytes accessed | tf_op | source)
XLA Modules:
  0.0 131.6 jit_solution(8300709666534152660)
XLA Ops:
  0.7 1.3 %broadcast_in_dim.62 = bf16[4,2,2048]{2,1,0:T(2,128)(2,1)} broadcast(bf16[2,2048]{1,0:T(2,128)(2,1)} %bitcast.19), dimensions={1,2} | broadcast | bytes 40960 | tf_op jit(solution)/shard_map/broadcast_in_dim | solution.py:48
  2.0 14.2 %all-to-all-start = ((bf16[4,2,2048]{2,1,0:T(2,128)(2,1)}), bf16[4,2,2048]{2,1,0:T(2,128)(2,1)S(1)}, u32[]{:S(2)}, u32[]{:S(2)}) async-start(bf16[4,2,2048]{2,1,0:T(2,128)(2,1)} %broadcast_in_dim.62), calls=%async_computation | async-start | bytes 65536 | tf_op jit(solution)/shard_map/all_to_all | solution.py:44
  16.2 0.7 broadcast_divide_fusion
  17.0 0.3 fusion.17
  17.3 0.7 copy-done
  18.0 5.8 %images.1 = (bf16[1024,2048]{1,0:T(8,128)(2,1)}, bf16[1024,2048]{1,0:T(8,128)(2,1)}) custom-call(bf16[1024,2048]{1,0:T(8,128)(2,1)} %x_ref.1, s32[1,1024]{1,0:T(1,128)S(1)} %bitcast.13, bf16[48,1024]{1,0:T(8,128)(2,1)S(1)} %pad_maximum_fusion.table_ref, f32[1,1024]{1,0:T(1,128)S(1)} %bitcast.16), custom_call_target="tpu_custom_call" | custom-call | tf_op jit(solution)/shard_map/images/pallas_call | solution.py:302
  23.8 5.1 %all-to-all-done = bf16[4,2,2048]{2,1,0:T(2,128)(2,1)S(1)} async-done(((bf16[4,2,2048]{2,1,0:T(2,128)(2,1)}), bf16[4,2,2048]{2,1,0:T(2,128)(2,1)S(1)}, u32[]{:S(2)}, u32[]{:S(2)}) %all-to-all-start) | async-done | bytes 32800 | tf_op jit(solution)/shard_map/all_to_all | solution.py:44
  28.9 0.9 broadcast_in_dim.68
  29.8 7.0 %all-to-all-start.1 = ((bf16[16,8,2048]{2,1,0:T(8,128)(2,1)}), bf16[16,8,2048]{2,1,0:T(8,128)(2,1)S(1)}, u32[]{:S(2)}, u32[]{:S(2)}) async-start(bf16[16,8,2048]{2,1,0:T(8,128)(2,1)} %broadcast_in_dim.68), calls=%async_computation.1 | async-start | bytes 1048576 | tf_op jit(solution)/shard_map/all_to_all | solution.py:44
  36.9 0.2 select_reduce_fusion.1
  37.2 9.8 %all-to-all-done.1 = bf16[16,8,2048]{2,1,0:T(8,128)(2,1)S(1)} async-done(((bf16[16,8,2048]{2,1,0:T(8,128)(2,1)}), bf16[16,8,2048]{2,1,0:T(8,128)(2,1)S(1)}, u32[]{:S(2)}, u32[]{:S(2)}) %all-to-all-start.1) | async-done | bytes 524320 | tf_op jit(solution)/shard_map/all_to_all | solution.py:44
  47.0 4.9 %scores.1 = (f32[128,1024]{1,0:T(8,128)S(1)}, f32[8,2,1024]{2,1,0:T(2,128)}) custom-call(bf16[128,2048]{1,0:T(8,128)(2,1)S(1)} %bitcast.11, bf16[16,1024]{1,0:T(8,128)(2,1)S(1)} %get-tuple-element.25.power_ref, s32[1,1024]{1,0:T(1,128)S(1)} %bitcast.14, s32[1,1024]{1,0:T(1,128)S(1)} %bitcast.17, bf16[1024,2048]{1,0:T(8,128)(2,1)} %get-tuple-element.16.weighted_ref), custom_call_target="tpu_custom_call" | custom-call | tf_op jit(solution)/shard_map/scores/pallas_call | solution.py:302
  51.9 4.5 %all-to-all-start.2 = ((f32[8,2,1024]{2,1,0:T(2,128)}), f32[8,2,1024]{2,1,0:T(2,128)S(1)}, u32[]{:S(2)}, u32[]{:S(2)}) async-start(f32[8,2,1024]{2,1,0:T(2,128)} %get-tuple-element.18.own_ref), calls=%async_computation.2 | async-start | bytes 131072 | tf_op jit(solution)/shard_map/all_to_all | solution.py:44
  56.4 0.1 compare_convert_fusion.permuter_ref
  56.5 4.5 %all-to-all-done.2.both_ref = f32[8,2,1024]{2,1,0:T(2,128)S(1)} async-done(((f32[8,2,1024]{2,1,0:T(2,128)}), f32[8,2,1024]{2,1,0:T(2,128)S(1)}, u32[]{:S(2)}, u32[]{:S(2)}) %all-to-all-start.2) | async-done | bytes 65568 | tf_op jit(solution)/shard_map/all_to_all | solution.py:44
  61.1 5.4 %project.1 = (s16[256,2176]{1,0:T(8,128)(2,1)S(1)}, f32[1,1024]{1,0:T(1,128)}) custom-call(f32[128,1024]{1,0:T(8,128)S(1)} %get-tuple-element.17.exp_ref, f32[8,2,1024]{2,1,0:T(2,128)} %get-tuple-element.18.own_ref, f32[8,2,1024]{2,1,0:T(2,128)S(1)} %all-to-all-done.2.both_ref, bf16[256,128]{1,0:T(8,128)(2,1)S(1)} %compare_convert_fusion.permuter_ref, ...), custom_call_target="tpu_custom_call" | custom-call | tf_op jit(solution)/shard_map/project/pallas_call | solution.py:302
  66.5 20.7 %all_to_all.30.came_ref = s16[16,16,2176]{2,1,0:T(8,128)(2,1)S(1)} all-to-all(s16[16,16,2176]{2,1,0:T(8,128)(2,1)S(1)} %bitcast.12), channel_id=1, replica_groups=mesh['zl'=4,'co'=2,'y'=4,'zh'=4,'x'=4] {'y','x'}, dimensions={0} | all-to-all | bytes 2228224 | tf_op jit(solution)/shard_map/all_to_all | solution.py:44
  87.2 1.5 %plane.1 = s16[4,16,2176]{2,1,0:T(8,128)(2,1)} custom-call(s16[16,16,2176]{2,1,0:T(8,128)(2,1)S(1)} %all_to_all.30.came_ref), custom_call_target="tpu_custom_call" | custom-call | tf_op jit(solution)/shard_map/plane/pallas_call | solution.py:302
  88.7 7.6 %all-to-all-start.4 = ((s16[4,16,2176]{2,1,0:T(8,128)(2,1)}), s16[4,16,2176]{2,1,0:T(8,128)(2,1)S(1)}, u32[]{:S(2)}, u32[]{:S(2)}) async-start(s16[4,16,2176]{2,1,0:T(8,128)(2,1)} %plane.1), calls=%async_computation.4 | async-start | bytes 557056 | tf_op jit(solution)/shard_map/all_to_all | solution.py:44
  96.4 0.2 fusion.shells_ref
  96.6 19.8 %all-to-all-done.4.came_ref = s16[4,16,2176]{2,1,0:T(8,128)(2,1)S(1)} async-done(((s16[4,16,2176]{2,1,0:T(8,128)(2,1)}), s16[4,16,2176]{2,1,0:T(8,128)(2,1)S(1)}, u32[]{:S(2)}, u32[]{:S(2)}) %all-to-all-start.4) | async-done | bytes 278560 | tf_op jit(solution)/shard_map/all_to_all | solution.py:44
  116.4 1.3 %shells.1 = (f32[2,2048]{1,0:T(2,128)S(1)}, f32[16,8,640]{2,1,0:T(8,128)S(1)}) custom-call(s32[3]{0:T(128)S(1)} %pad_add_fusion.where_ref, s16[4,16,2176]{2,1,0:T(8,128)(2,1)S(1)} %all-to-all-done.4.came_ref, f32[16,1024]{1,0:T(8,128)S(1)} %get-tuple-element.24.squares_ref, f32[1024,128]{1,0:T(8,128)S(1)} %fusion.shells_ref), custom_call_target="tpu_custom_call" | custom-call | tf_op jit(solution)/shard_map/shells/pallas_call | solution.py:302
  117.8 12.1 %all_to_all.31.came_ref = f32[16,8,640]{2,1,0:T(8,128)S(1)} all-to-all(f32[16,8,640]{2,1,0:T(8,128)S(1)} %get-tuple-element.21), channel_id=1, replica_groups=mesh['zl'=4,'co'=2,'y'=4,'zh'=4,'x'=4] {'y','x'}, dimensions={0} | all-to-all | bytes 655360 | tf_op jit(solution)/shard_map/all_to_all | solution.py:44
  129.8 1.7 %finish.1 = f32[1,4,2048]{2,1,0:T(4,128)} custom-call(s32[3]{0:T(128)S(1)} %pad_add_fusion.where_ref, f32[16,8,640]{2,1,0:T(8,128)S(1)} %all_to_all.31.came_ref, f32[2,2048]{1,0:T(2,128)S(1)} %get-tuple-element.22.keep_ref, f32[1024,128]{1,0:T(8,128)S(1)} %fusion.shells_ref), custom_call_target="tpu_custom_call" | custom-call | tf_op jit(solution)/shard_map/finish/pallas_call | solution.py:302
  (19 shorter events, 0.4 us)
Async XLA Ops:
  0.6 46.3 %copy-start.1 = (s32[1024]{0:T(1024)S(1)}, s32[1024]{0:T(1024)}, u32[]{:S(2)}) copy-start(s32[1024]{0:T(1024)} %param.10) | copy-start | bytes 12292
  0.6 36.2 %copy-start.4 = (s32[128]{0:T(128)S(1)}, s32[128]{0:T(128)}, u32[]{:S(2)}) copy-start(s32[128]{0:T(128)} %param.13) | copy-start | bytes 1540
  0.7 46.3 %copy-start.2 = (s32[1024,1]{0,1:T(1,128)S(1)}, s32[1024,1]{0,1:T(1,128)}, u32[]{:S(2)}) copy-start(s32[1024,1]{0,1:T(1,128)} %param.12) | copy-start | bytes 12292
  2.0 26.9 %all-to-all-start = ((bf16[4,2,2048]{2,1,0:T(2,128)(2,1)}), bf16[4,2,2048]{2,1,0:T(2,128)(2,1)S(1)}, u32[]{:S(2)}, u32[]{:S(2)}) async-start(bf16[4,2,2048]{2,1,0:T(2,128)(2,1)} %broadcast_in_dim.62), calls=%async_computation | async-start | bytes 65536 | tf_op jit(solution)/shard_map/all_to_all | solution.py:44
  17.3 0.7 copy-start
  23.8 37.2 %copy-start.3 = (s32[1024]{0:T(1024)S(1)}, s32[1024]{0:T(1024)}, u32[]{:S(2)}) copy-start(s32[1024]{0:T(1024)} %param.11) | copy-start | bytes 12292
  29.8 17.1 %all-to-all-start.1 = ((bf16[16,8,2048]{2,1,0:T(8,128)(2,1)}), bf16[16,8,2048]{2,1,0:T(8,128)(2,1)S(1)}, u32[]{:S(2)}, u32[]{:S(2)}) async-start(bf16[16,8,2048]{2,1,0:T(8,128)(2,1)} %broadcast_in_dim.68), calls=%async_computation.1 | async-start | bytes 1048576 | tf_op jit(solution)/shard_map/all_to_all | solution.py:44
  51.9 9.2 %all-to-all-start.2 = ((f32[8,2,1024]{2,1,0:T(2,128)}), f32[8,2,1024]{2,1,0:T(2,128)S(1)}, u32[]{:S(2)}, u32[]{:S(2)}) async-start(f32[8,2,1024]{2,1,0:T(2,128)} %get-tuple-element.18.own_ref), calls=%async_computation.2 | async-start | bytes 131072 | tf_op jit(solution)/shard_map/all_to_all | solution.py:44
  88.7 27.7 %all-to-all-start.4 = ((s16[4,16,2176]{2,1,0:T(8,128)(2,1)}), s16[4,16,2176]{2,1,0:T(8,128)(2,1)S(1)}, u32[]{:S(2)}, u32[]{:S(2)}) async-start(s16[4,16,2176]{2,1,0:T(8,128)(2,1)} %plane.1), calls=%async_computation.4 | async-start | bytes 557056 | tf_op jit(solution)/shard_map/all_to_all | solution.py:44

commit v4 on v3

--- a/solution.py
+++ b/solution.py
@@ -23,7 +23,6 @@
 PART = COLS // PARTS
 F32 = jnp.float32
 BF16 = jnp.bfloat16
-HIGHEST = lax.Precision.HIGHEST
 
 
 def ctf_table():
@@ -129,52 +128,78 @@
 
 
 def image_kernel(
-    x_ref, bins_ref, table_ref, noise_ref, centred_ref, weighted_ref, x_buf, centred_buf,
-    weighted_buf, sems
+    x_ref, bins_ref, table_ref, noise_ref, centred_near, centred_far, weighted_near, weighted_far,
+    x_buf, centred_buf, weighted_buf, sems
 ):
     noise = noise_ref[...]
-    step = x_buf.shape[0] // PARTS
-    spans = [slice(i * step, (i + 1) * step) for i in range(PARTS)]
-    reads, writes = [], []
-    for i, rows in enumerate(spans):
-        reads.append(pltpu.make_async_copy(x_ref.at[rows], x_buf.at[rows], sems.at[0, i]))
-        reads[i].start()
-    for i, rows in enumerate(spans):
+    steps = PARTS
+    step = x_buf.shape[0] // steps
+    edge = weighted_near.shape[0] // step
+
+    def read(i):
+        rows = pl.ds(i * step, step)
+        return pltpu.make_async_copy(x_ref.at[rows], x_buf.at[rows], sems.at[0, i])
+
+    def write(i, k):
+        if k == 1:
+            rows, buf, out = pl.ds(i * step, step), centred_buf, centred_far
+        else:
+            rows, buf, out = pl.ds((i - edge) * step, step), weighted_buf, weighted_far
+        return pltpu.make_async_copy(buf.at[rows], out.at[rows], sems.at[k, i])
+
+    def chunk(i, keep):
+        rows = pl.ds(pl.multiple_of(i * step, step), step)
         match = bin_match(bins_ref[:, rows], 3)
         contrast = contract(match, table_ref[...], ((0,), (0,)))
-        reads[i].wait()
+        read(i).wait()
         for part in range(2):
             cols = slice(part * PIXC, (part + 1) * PIXC)
             product = x_buf[rows, cols].astype(F32) * contrast
-            centred_buf[rows, cols] = product.astype(BF16)
-            weighted_buf[rows, cols] = (product * noise).astype(BF16)
-        for k, buf, out in ((1, centred_buf, centred_ref), (2, weighted_buf, weighted_ref)):
-            writes.append(pltpu.make_async_copy(buf.at[rows], out.at[rows], sems.at[k, i]))
-            writes[-1].start()
-    for write in writes:
-        write.wait()
+            rounded = product.astype(BF16)
+            if part == 0:
+                centred_near[rows, :] = rounded[:, :PART]
+                centred_buf[rows, : PIXC - PART] = rounded[:, PART:]
+            else:
+                centred_buf[rows, PIXC - PART :] = rounded
+            scaled = (product * noise).astype(BF16)
+            if keep:
+                weighted_near[rows, cols] = scaled
+            else:
+                weighted_buf[pl.ds(pl.multiple_of((i - edge) * step, step), step), cols] = scaled
+        write(i, 1).start()
+        if not keep:
+            write(i, 2).start()
+
+    for i in range(steps):
+        read(i).start()
+    lax.fori_loop(0, edge, lambda i, c: (chunk(i, True), c)[1], 0)
+    lax.fori_loop(edge, steps, lambda i, c: (chunk(i, False), c)[1], 0)
+    for i in range(steps):
+        write(i, 1).wait()
+        if i >= edge:
+            write(i, 2).wait()
 
 
 def score_kernel(
-    panel_ref, power_ref, bins_ref, mask_ref, weighted_ref, exp_ref, pair_ref, weighted_buf, sems
+    panel_ref, power_ref, bins_ref, mask_ref, near_ref, far_ref, exp_ref, pair_ref, far_buf, sems
 ):
-    step = weighted_buf.shape[0] // PARTS
-    reads = []
-    for i in range(PARTS):
-        rows = slice(i * step, (i + 1) * step)
-        reads.append(
-            pltpu.make_async_copy(weighted_ref.at[rows], weighted_buf.at[rows], sems.at[i])
-        )
-        reads[i].start()
+    step = near_ref.shape[0]
+
+    def read(i):
+        rows = pl.ds(i * step, step)
+        return pltpu.make_async_copy(far_ref.at[rows], far_buf.at[rows], sems.at[i])
+
+    for i in range(PARTS - 1):
+        read(i).start()
     real = panel_ref[:, :PIXC].astype(F32)
     imag = panel_ref[:, PIXC:].astype(F32)
     panel_power = (real * real + imag * imag).astype(BF16)
     norm = three_parts(contract(panel_power, power_ref[...], ((1,), (1,))), 1)
-    for i in range(PARTS):
-        rows = slice(i * step, (i + 1) * step)
+
+    def chunk(at, weighted):
+        rows = pl.ds(at, step)
         norm_part = contract(norm, bin_match(bins_ref[:, rows], 3), ((1,), (0,)))
-        reads[i].wait()
-        direct = contract(panel_ref[...], weighted_buf[rows, :], ((1,), (1,)))
+        direct = contract(panel_ref[...], weighted, ((1,), (1,)))
         scores = direct - 0.5 * norm_part
         allowed = mask_ref[:, rows] > 0
         masked = jnp.where(allowed, scores, -1e30)
@@ -186,18 +211,34 @@
         for other in range(8):
             pair_ref[other, :, rows] = pair
 
+    def far_chunk(i, carry):
+        read(i).wait()
+        start = pl.multiple_of(i * step, step)
+        chunk(pl.multiple_of(start + step, step), far_buf[pl.ds(start, step), :])
+        return carry
+
+    chunk(0, near_ref[...])
+    lax.fori_loop(0, PARTS - 1, far_chunk, 0)
+
+
+def split_kernel(exp_ref, permuter_ref, row_half_ref, half_ref, split_ref):
+    parts = three_parts(exp_ref[...], 0)
+    permuter = permuter_ref[...]
+    rows = contract(jnp.concatenate([permuter] * 3, axis=1), parts, ((1,), (0,)))
+    split_ref[...] = jnp.where(row_half_ref[...] == half_ref[...], rows, 0.0)
+
 
 def project_kernel(
-    exp_ref, own_ref, both_ref, permuter_ref, row_half_ref, half_ref, bins_ref, centred_ref,
-    packed_ref, evidence_ref, centred_buf, sems
+    split_ref, own_ref, both_ref, bins_ref, near_ref, far_ref, packed_ref, evidence_ref, far_buf,
+    sems
 ):
     spans = [slice(part * PART, (part + 1) * PART) for part in range(PARTS)]
-    reads = []
-    for part, cols in enumerate(spans):
-        reads.append(
-            pltpu.make_async_copy(centred_ref.at[:, cols], centred_buf.at[:, cols], sems.at[part])
-        )
-        reads[part].start()
+    reads = [
+        pltpu.make_async_copy(far_ref.at[:, cols], far_buf.at[:, cols], sems.at[part])
+        for part, cols in enumerate(spans[:-1])
+    ]
+    for read in reads:
+        read.start()
     own_peak = own_ref[0, 0:1, :]
     peak = both_ref[0, 0:1, :]
     for c in range(1, both_ref.shape[0]):
@@ -206,15 +247,16 @@
     for c in range(both_ref.shape[0]):
         total = total + both_ref[c, 1:2, :] * jnp.exp(both_ref[c, 0:1, :] - peak)
     evidence_ref[...] = peak + jnp.log(total)
-    posterior = (exp_ref[...] * (jnp.exp(own_peak - peak) / total)).astype(BF16)
-    by_direction = contract(permuter_ref[...], posterior, ((1,), (0,)))
-    kept = row_half_ref[...] == half_ref[...]
-    post = jnp.where(kept, by_direction, 0.0).astype(BF16)
+    post = (split_ref[...] * (jnp.exp(own_peak - peak) / total)).astype(BF16)
     sums = contract(post, bin_match(bins_ref[...], 1), ((1,), (1,)))
     expos = []
     for part, cols in enumerate(spans):
-        reads[part].wait()
-        codes, expo = encode(contract(post, centred_buf[:, cols], ((1,), (0,))))
+        if part == 0:
+            centred = near_ref[...]
+        else:
+            reads[part - 1].wait()
+            centred = far_buf[:, spans[part - 1]]
+        codes, expo = encode(contract(post, centred, ((1,), (0,))))
         expos.append(expo)
         packed_ref[:, cols] = codes
     packed_ref[:, COLS:] = side_block(sums, expos, 2.0**20)
@@ -253,8 +295,12 @@
     power1 = jnp.where(upper == 0, second, first)
     three = jnp.concatenate([cross, power0, power1, jnp.zeros((5, COLS), F32)], axis=0)
     folded = three[:, :PIXC] + three[:, PIXC:]
-    by_shell = jnp.dot(folded, shells_ref[...], precision=HIGHEST, preferred_element_type=F32)
-    weight = jnp.dot(own_sums, squares_ref[...], precision=HIGHEST, preferred_element_type=F32)
+    by_shell = contract(three_parts(folded, 0), shells_ref[...], ((1,), (0,)))
+    by_shell = by_shell[0:8] + by_shell[8:16] + by_shell[16:24]
+    squares = squares_ref[...]
+    weight = contract(
+        three_parts(own_sums, 1), jnp.concatenate([squares] * 3, axis=0), ((1,), (0,))
+    )
     whole = own_data / (jnp.concatenate([weight, weight], axis=1) + 1.0)
     keep_ref[...] = whole[:2]
     for other in range(16):
@@ -265,16 +311,14 @@
             stats_ref[other, 2 * part : 2 * part + 2, :PART] = piece
 
 
-def finish_kernel(where_ref, came_ref, keep_ref, shells_ref, out_ref):
+def finish_kernel(where_ref, came_ref, keep_ref, spread_ref, out_ref):
     totals = came_ref[0, :, PART:]
     for source in range(1, 16):
         totals = totals + came_ref[source, :, PART:]
     fsc = totals[0:1] / jnp.sqrt(totals[1:2] * totals[2:3] + 1e-06)
     half = jnp.broadcast_to((1.0 + fsc) / 2.0, (8, ORIENT))
-    factor = lax.dot_general(
-        half, shells_ref[...], (((1,), (1,)), ((), ())), precision=HIGHEST,
-        preferred_element_type=F32,
-    )[0:1]
+    factor = contract(three_parts(half, 0), spread_ref[...], ((1,), (0,)))
+    factor = factor[0:1] + factor[8:9] + factor[16:17]
     low = where_ref[0] == 0
     partner = came_ref[where_ref[2]]
     for part in range(PARTS):
@@ -318,37 +362,54 @@
     inverse_noise = lookup_small(shells, 1.0 / sigma2)
     table = ctf_table()
     power = (table * table * inverse_noise[None, :]).astype(BF16)
-    squares = (table * table).astype(BF16).astype(F32)
-    shell_match = (shells[:, None] == jnp.arange(ORIENT, dtype=jnp.int32)[None, :]).astype(F32)
-    bins_row = defocus_bins[None, :]
+    squares = (table * table).astype(BF16)
+    lanes = jnp.arange(ORIENT, dtype=jnp.int32)
+    shell_match = (shells[:, None] == lanes[None, :]).astype(BF16)
+    shell_spread = (lanes[:, None] == shells[None, :]).astype(BF16)
     y, zh, x = lax.axis_index("y"), lax.axis_index("zh"), lax.axis_index("x")
     where = jnp.stack([y // 2, zh, (y ^ 2) * 4 + x]).astype(jnp.int32)
 
     direction, row_half = row_maps()
     match = gathered_orients()[:, None] == jnp.arange(ORIENT, dtype=jnp.int32)[None, :]
     select = jnp.sum(jnp.where(match, orient_ids[None, :], 0), axis=1)
+
+    near, far = pltpu.MemorySpace.VMEM, pltpu.MemorySpace.HBM
+    first, rest = count // PARTS, count - count // PARTS
+    by_zh, bins_row, parts, noise_row, power, squares, select = lax.optimization_barrier(
+        (
+            from_all(panels[0], "zh", 4), defocus_bins[None, :], table_parts(table),
+            inverse_noise[None, :], power, squares, select,
+        )
+    )
     permuter = (direction[:, None] == select[None, :]).astype(BF16)
-
-    images = pltpu.VMEM((count, COLS), BF16)
-    centred, weighted = call(
-        image_kernel, "images", [pltpu.MemorySpace.HBM((count, COLS), BF16)] * 2, 24,
-        particles, bins_row, table_parts(table), inverse_noise[None, :],
-        far=(0,), far_out=(0, 1),
-        scratch=[images] * 3 + [pltpu.SemaphoreType.DMA((3, PARTS))],
-    )
-    by_zh = from_all(panels[0], "zh", 4)
-    by_zh, centred, weighted = lax.optimization_barrier((by_zh, centred, weighted))
+    centred_near, centred_far, weighted_near, weighted_far = call(
+        image_kernel, "images",
+        [
+            near((count, PART), BF16), far((count, COLS - PART), BF16),
+            near((first, COLS), BF16), far((rest, COLS), BF16),
+        ],
+        24, particles, bins_row, parts, noise_row,
+        far=(0,), far_out=(1, 3),
+        scratch=[
+            near((count, COLS), BF16), near((count, COLS - PART), BF16), near((rest, COLS), BF16),
+            pltpu.SemaphoreType.DMA((3, PARTS)),
+        ],
+    )
     piece = from_all(by_zh.reshape(8, COLS), PLANE, 16).reshape(ORIENT, COLS)
 
     own_exp, pair = call(
         score_kernel, "scores", [of((ORIENT, count), F32), of((8, 2, count), F32)], 14,
-        piece, power, bins_row, prior_mask.reshape(1, count), weighted,
-        far=(4,), scratch=[images, pltpu.SemaphoreType.DMA((PARTS,))],
+        piece, power, bins_row, prior_mask.reshape(1, count), weighted_near, weighted_far,
+        far=(5,), scratch=[near((rest, COLS), BF16), pltpu.SemaphoreType.DMA((PARTS,))],
+    )
+    (split,) = call(
+        split_kernel, "split", [of((ROWS, count), F32)], 8,
+        own_exp, permuter, row_half[:, None], half_sets[None, :],
     )
     packed, evidence = call(
         project_kernel, "project", [of((ROWS, WIDE), jnp.int16), of((1, count), F32)], 20,
-        own_exp, pair, exchange(pair, CLS), permuter, row_half[:, None], half_sets[None, :],
-        bins_row, centred, far=(7,), scratch=[images, pltpu.SemaphoreType.DMA((PARTS,))],
+        split, pair, exchange(pair, CLS), bins_row, centred_near, centred_far, far=(5,),
+        scratch=[near((count, COLS - PART), BF16), pltpu.SemaphoreType.DMA((PARTS,))],
     )
     (second,) = call(
         plane_kernel, "plane", [of((4, 16, WIDE), jnp.int16)], 8,
@@ -360,7 +421,7 @@
     )
     (half_maps,) = call(
         finish_kernel, "finish", [of((1, 4, COLS), F32)], 8,
-        where, exchange(stats, PLANE), keep, shell_match, scalars=1,
+        where, exchange(stats, PLANE), keep, shell_spread, scalars=1,
     )
     return (half_maps, evidence.reshape(count))
 

time: 132 us -> 127 us (0.962)
  blocking collectives: 32.8 us -> 20.7 us
  waiting for transfers between devices: 39.2 us -> 45 us
  Pallas kernels: 20.7 us -> 17.9 us
  local copies, waits for them, and re-layouts: 2.93 us -> 4.74 us
    all_to_all x2 -> x1, blocking collectives: 32.8 us -> 20.7 us  [exchange(): return lax.all_to_all(blocks, axes, split_axis=0, concat_axis=0, tiled=True)]
    all_to_all x4 -> x5, waiting for transfers between devices: 39.2 us -> 45 us  [exchange(): return lax.all_to_all(blocks, axes, split_axis=0, concat_axis=0, tiled=True)]
    pallas_call x6 -> x7, Pallas kernels: 20.7 us -> 17.9 us  [call(): pl.pallas_call(kernel, in_specs=[space(i if i >= scalars else -1, far) fo...]
    unnamed x10 -> x12, local copies, waits for them, and re-layouts: 0.7 us -> 2.53 us
    all_to_all x4 -> x5, starting transfers between devices: 33.4 us -> 34.4 us  [exchange(): return lax.all_to_all(blocks, axes, split_axis=0, concat_axis=0, tiled=True)]
  transfers between devices with their start and end apart: 4 -> 5, of which waited for: 4 -> 5; matrix products, arithmetic and copies ran while one was open for 1% -> 2% of each run, Pallas kernels for 4% -> 4%
where the time goes in v4:
time: 127 us; the launch traced here: 126 us
  waiting for transfers between devices  45 us (35%)
  starting transfers between devices  34.4 us (27%)
  blocking collectives  20.7 us (16%)
  Pallas kernels  17.9 us (14%)
  local copies, waits for them, and re-layouts  4.74 us (4%)
  other arithmetic  2.49 us (2%)
    all_to_all x5, waiting for transfers between devices, exchange(): return lax.all_to_all(blocks, axes, split_axis=0, concat_axis=0, tiled=True)  45 us
    all_to_all x5, starting transfers between devices, exchange(): return lax.all_to_all(blocks, axes, split_axis=0, concat_axis=0, tiled=True)  34.4 us
    all_to_all x1, blocking collectives, exchange(): return lax.all_to_all(blocks, axes, split_axis=0, concat_axis=0, tiled=True)  20.7 us
    pallas_call x7, Pallas kernels, call(): pl.pallas_call(kernel, in_specs=[space(i if i >= scalars else -1, far) fo...  17.9 us
  transfers between devices with their start and end apart: 5, of which 5 were waited for; matrix products, arithmetic and copies ran while one was open for 2% of the time, Pallas kernels for 4%

profile of v4, /device:TPU:32, one launch (start us, length us, event | category | flops | bytes accessed | tf_op | source)
XLA Modules:
  0.0 126.0 jit_solution(16953594116381654109)
XLA Ops:
  0.6 1.3 %broadcast_in_dim.39 = bf16[4,2,2048]{2,1,0:T(2,128)(2,1)} broadcast(bf16[2,2048]{1,0:T(2,128)(2,1)} %bitcast.19), dimensions={1,2} | broadcast | bytes 40960 | tf_op jit(solution)/shard_map/broadcast_in_dim | solution.py:47
  2.0 14.2 %all-to-all-start = ((bf16[4,2,2048]{2,1,0:T(2,128)(2,1)}), bf16[4,2,2048]{2,1,0:T(2,128)(2,1)S(1)}, u32[]{:S(2)}, u32[]{:S(2)}) async-start(bf16[4,2,2048]{2,1,0:T(2,128)(2,1)} %broadcast_in_dim.39), calls=%async_computation | async-start | bytes 65536 | tf_op jit(solution)/shard_map/all_to_all | solution.py:43
  16.2 0.7 broadcast_divide_fusion
  17.3 0.8 select_reduce_fusion.1
  18.2 10.7 %all-to-all-done = bf16[4,2,2048]{2,1,0:T(2,128)(2,1)S(1)} async-done(((bf16[4,2,2048]{2,1,0:T(2,128)(2,1)}), bf16[4,2,2048]{2,1,0:T(2,128)(2,1)S(1)}, u32[]{:S(2)}, u32[]{:S(2)}) %all-to-all-start) | async-done | bytes 32800 | tf_op jit(solution)/shard_map/all_to_all | solution.py:43
  28.9 0.9 broadcast_in_dim.72
  29.8 7.0 %all-to-all-start.1 = ((bf16[16,8,2048]{2,1,0:T(8,128)(2,1)}), bf16[16,8,2048]{2,1,0:T(8,128)(2,1)S(1)}, u32[]{:S(2)}, u32[]{:S(2)}) async-start(bf16[16,8,2048]{2,1,0:T(8,128)(2,1)} %broadcast_in_dim.72), calls=%async_computation.1 | async-start | bytes 1048576 | tf_op jit(solution)/shard_map/all_to_all | solution.py:43
  36.9 0.7 copy-done.2
  37.6 4.7 %images.1 = (bf16[1024,512]{1,0:T(8,128)(2,1)S(1)}, bf16[1024,1536]{1,0:T(8,128)(2,1)}, bf16[256,2048]{1,0:T(8,128)(2,1)S(1)}, bf16[768,2048]{1,0:T(8,128)(2,1)}) custom-call(bf16[1024,2048]{1,0:T(8,128)(2,1)} %x_ref.1, s32[1,1024]{1,0:T(1,128)S(1)} %bitcast.13, bf16[48,1024]{1,0:T(8,128)(2,1)S(1)} %pad_maximum_fusion.table_ref, f32[1,1024]{1,0:T(1,128)S(1)} %bitcast.16), custom_call_target="tpu_custom_call" | custom-call | tf_op jit(solution)/shard_map/images/pallas_call | solution.py:346
  42.3 4.6 %all-to-all-done.1 = bf16[16,8,2048]{2,1,0:T(8,128)(2,1)S(1)} async-done(((bf16[16,8,2048]{2,1,0:T(8,128)(2,1)}), bf16[16,8,2048]{2,1,0:T(8,128)(2,1)S(1)}, u32[]{:S(2)}, u32[]{:S(2)}) %all-to-all-start.1) | async-done | bytes 524320 | tf_op jit(solution)/shard_map/all_to_all | solution.py:43
  46.9 3.5 %scores.1 = (f32[128,1024]{1,0:T(8,128)S(1)}, f32[8,2,1024]{2,1,0:T(2,128)}) custom-call(bf16[128,2048]{1,0:T(8,128)(2,1)S(1)} %bitcast.11, bf16[16,1024]{1,0:T(8,128)(2,1)S(1)} %get-tuple-element.20.power_ref, s32[1,1024]{1,0:T(1,128)S(1)} %bitcast.14, s32[1,1024]{1,0:T(1,128)S(1)} %bitcast.17, bf16[256,2048]{1,0:T(8,128)(2,1)S(1)} %get-tuple-element.24.near_ref, ...), custom_call_target="tpu_custom_call" | custom-call | tf_op jit(solution)/shard_map/scores/pallas_call | solution.py:346
  50.4 0.8 copy-done
  51.2 4.5 %all-to-all-start.2 = ((f32[8,2,1024]{2,1,0:T(2,128)}), f32[8,2,1024]{2,1,0:T(2,128)S(1)}, u32[]{:S(2)}, u32[]{:S(2)}) async-start(f32[8,2,1024]{2,1,0:T(2,128)} %get-tuple-element.28.own_ref), calls=%async_computation.2 | async-start | bytes 131072 | tf_op jit(solution)/shard_map/all_to_all | solution.py:43
  55.9 1.0 copy-done.1
  57.3 3.0 %all-to-all-done.2.both_ref = f32[8,2,1024]{2,1,0:T(2,128)S(1)} async-done(((f32[8,2,1024]{2,1,0:T(2,128)}), f32[8,2,1024]{2,1,0:T(2,128)S(1)}, u32[]{:S(2)}, u32[]{:S(2)}) %all-to-all-start.2) | async-done | bytes 65568 | tf_op jit(solution)/shard_map/all_to_all | solution.py:43
  60.4 4.5 %project.1 = (s16[256,2176]{1,0:T(8,128)(2,1)S(1)}, f32[1,1024]{1,0:T(1,128)}) custom-call(f32[256,1024]{1,0:T(8,128)S(1)} %split.1.split_ref, f32[8,2,1024]{2,1,0:T(2,128)} %get-tuple-element.28.own_ref, f32[8,2,1024]{2,1,0:T(2,128)S(1)} %all-to-all-done.2.both_ref, s32[1,1024]{1,0:T(1,128)S(1)} %bitcast.15, ...), custom_call_target="tpu_custom_call" | custom-call | tf_op jit(solution)/shard_map/project/pallas_call | solution.py:346
  64.9 20.7 %all_to_all.30.came_ref = s16[16,16,2176]{2,1,0:T(8,128)(2,1)S(1)} all-to-all(s16[16,16,2176]{2,1,0:T(8,128)(2,1)S(1)} %bitcast.12), channel_id=1, replica_groups=mesh['zl'=4,'co'=2,'y'=4,'zh'=4,'x'=4] {'y','x'}, dimensions={0} | all-to-all | bytes 2228224 | tf_op jit(solution)/shard_map/all_to_all | solution.py:43
  85.6 1.5 %plane.1 = s16[4,16,2176]{2,1,0:T(8,128)(2,1)} custom-call(s16[16,16,2176]{2,1,0:T(8,128)(2,1)S(1)} %all_to_all.30.came_ref), custom_call_target="tpu_custom_call" | custom-call | tf_op jit(solution)/shard_map/plane/pallas_call | solution.py:346
  87.1 3.4 %all-to-all-start.4 = ((s16[4,16,2176]{2,1,0:T(8,128)(2,1)}), s16[4,16,2176]{2,1,0:T(8,128)(2,1)S(1)}, u32[]{:S(2)}, u32[]{:S(2)}) async-start(s16[4,16,2176]{2,1,0:T(8,128)(2,1)} %plane.1), calls=%async_computation.4 | async-start | bytes 557056 | tf_op jit(solution)/shard_map/all_to_all | solution.py:43
  90.8 17.6 %all-to-all-done.4.came_ref = s16[4,16,2176]{2,1,0:T(8,128)(2,1)S(1)} async-done(((s16[4,16,2176]{2,1,0:T(8,128)(2,1)}), s16[4,16,2176]{2,1,0:T(8,128)(2,1)S(1)}, u32[]{:S(2)}, u32[]{:S(2)}) %all-to-all-start.4) | async-done | bytes 278560 | tf_op jit(solution)/shard_map/all_to_all | solution.py:43
  108.5 1.9 %shells.1 = (f32[2,2048]{1,0:T(2,128)S(1)}, f32[16,8,640]{2,1,0:T(8,128)}) custom-call(s32[3]{0:T(128)S(1)} %pad_add_fusion.where_ref, s16[4,16,2176]{2,1,0:T(8,128)(2,1)S(1)} %all-to-all-done.4.came_ref, bf16[16,1024]{1,0:T(8,128)(2,1)S(1)} %get-tuple-element.32.squares_ref, bf16[1024,128]{1,0:T(8,128)(2,1)S(1)} %fusion.shells_ref), custom_call_target="tpu_custom_call" | custom-call | tf_op jit(solution)/shard_map/shells/pallas_call | solution.py:346
  110.3 5.2 %all-to-all-start.5 = ((f32[16,8,640]{2,1,0:T(8,128)}), f32[16,8,640]{2,1,0:T(8,128)S(1)}, u32[]{:S(2)}, u32[]{:S(2)}) async-start(f32[16,8,640]{2,1,0:T(8,128)} %get-tuple-element.33), calls=%async_computation.5 | async-start | bytes 655360 | tf_op jit(solution)/shard_map/all_to_all | solution.py:43
  115.7 9.0 %all-to-all-done.5.came_ref = f32[16,8,640]{2,1,0:T(8,128)S(1)} async-done(((f32[16,8,640]{2,1,0:T(8,128)}), f32[16,8,640]{2,1,0:T(8,128)S(1)}, u32[]{:S(2)}, u32[]{:S(2)}) %all-to-all-start.5) | async-done | bytes 327712 | tf_op jit(solution)/shard_map/all_to_all | solution.py:43
  124.7 1.4 %finish.1 = f32[1,4,2048]{2,1,0:T(4,128)} custom-call(s32[3]{0:T(128)S(1)} %pad_add_fusion.where_ref, f32[16,8,640]{2,1,0:T(8,128)S(1)} %all-to-all-done.5.came_ref, f32[2,2048]{1,0:T(2,128)S(1)} %get-tuple-element.34.keep_ref, bf16[128,1024]{1,0:T(8,128)(2,1)S(1)} %fusion.1.spread_ref), custom_call_target="tpu_custom_call" | custom-call | tf_op jit(solution)/shard_map/finish/pallas_call | solution.py:346
  (24 shorter events, 1.5 us)
Async XLA Ops:
  2.0 26.9 %all-to-all-start = ((bf16[4,2,2048]{2,1,0:T(2,128)(2,1)}), bf16[4,2,2048]{2,1,0:T(2,128)(2,1)S(1)}, u32[]{:S(2)}, u32[]{:S(2)}) async-start(bf16[4,2,2048]{2,1,0:T(2,128)(2,1)} %broadcast_in_dim.39), calls=%async_computation | async-start | bytes 65536 | tf_op jit(solution)/shard_map/all_to_all | solution.py:43
  17.3 29.6 %copy-start.3 = (s32[1024]{0:T(1024)S(1)}, s32[1024]{0:T(1024)}, u32[]{:S(2)}) copy-start(s32[1024]{0:T(1024)} %param.10) | copy-start | bytes 12292
  17.3 29.6 %copy-start.4 = (s32[1024,1]{0,1:T(1,128)S(1)}, s32[1024,1]{0,1:T(1,128)}, u32[]{:S(2)}) copy-start(s32[1024,1]{0,1:T(1,128)} %param.12) | copy-start | bytes 12292
  29.8 17.1 %all-to-all-start.1 = ((bf16[16,8,2048]{2,1,0:T(8,128)(2,1)}), bf16[16,8,2048]{2,1,0:T(8,128)(2,1)S(1)}, u32[]{:S(2)}, u32[]{:S(2)}) async-start(bf16[16,8,2048]{2,1,0:T(8,128)(2,1)} %broadcast_in_dim.72), calls=%async_computation.1 | async-start | bytes 1048576 | tf_op jit(solution)/shard_map/all_to_all | solution.py:43
  36.9 0.7 copy-start.2
  42.3 13.6 %copy-start.5 = (s32[1024]{0:T(1024)S(1)}, s32[1024]{0:T(1024)}, u32[]{:S(2)}) copy-start(s32[1024]{0:T(1024)} %param.11) | copy-start | bytes 12292
  50.4 0.8 copy-start
  51.2 9.2 %all-to-all-start.2 = ((f32[8,2,1024]{2,1,0:T(2,128)}), f32[8,2,1024]{2,1,0:T(2,128)S(1)}, u32[]{:S(2)}, u32[]{:S(2)}) async-start(f32[8,2,1024]{2,1,0:T(2,128)} %get-tuple-element.28.own_ref), calls=%async_computation.2 | async-start | bytes 131072 | tf_op jit(solution)/shard_map/all_to_all | solution.py:43
  55.9 1.0 copy-start.1
  87.1 21.4 %all-to-all-start.4 = ((s16[4,16,2176]{2,1,0:T(8,128)(2,1)}), s16[4,16,2176]{2,1,0:T(8,128)(2,1)S(1)}, u32[]{:S(2)}, u32[]{:S(2)}) async-start(s16[4,16,2176]{2,1,0:T(8,128)(2,1)} %plane.1), calls=%async_computation.4 | async-start | bytes 557056 | tf_op jit(solution)/shard_map/all_to_all | solution.py:43
  110.3 14.3 %all-to-all-start.5 = ((f32[16,8,640]{2,1,0:T(8,128)}), f32[16,8,640]{2,1,0:T(8,128)S(1)}, u32[]{:S(2)}, u32[]{:S(2)}) async-start(f32[16,8,640]{2,1,0:T(8,128)} %get-tuple-element.33), calls=%async_computation.5 | async-start | bytes 655360 | tf_op jit(solution)/shard_map/all_to_all | solution.py:43

commit v5 on v4

--- a/solution.py
+++ b/solution.py
@@ -221,16 +221,9 @@
     lax.fori_loop(0, PARTS - 1, far_chunk, 0)
 
 
-def split_kernel(exp_ref, permuter_ref, row_half_ref, half_ref, split_ref):
-    parts = three_parts(exp_ref[...], 0)
-    permuter = permuter_ref[...]
-    rows = contract(jnp.concatenate([permuter] * 3, axis=1), parts, ((1,), (0,)))
-    split_ref[...] = jnp.where(row_half_ref[...] == half_ref[...], rows, 0.0)
-
-
 def project_kernel(
-    split_ref, own_ref, both_ref, bins_ref, near_ref, far_ref, packed_ref, evidence_ref, far_buf,
-    sems
+    exp_ref, own_ref, both_ref, permuter_ref, row_half_ref, half_ref, bins_ref, near_ref, far_ref,
+    packed_ref, evidence_ref, far_buf, evidence_buf, sems
 ):
     spans = [slice(part * PART, (part + 1) * PART) for part in range(PARTS)]
     reads = [
@@ -240,14 +233,16 @@
     for read in reads:
         read.start()
     own_peak = own_ref[0, 0:1, :]
-    peak = both_ref[0, 0:1, :]
-    for c in range(1, both_ref.shape[0]):
-        peak = jnp.maximum(peak, both_ref[c, 0:1, :])
-    total = jnp.zeros_like(peak)
-    for c in range(both_ref.shape[0]):
-        total = total + both_ref[c, 1:2, :] * jnp.exp(both_ref[c, 0:1, :] - peak)
-    evidence_ref[...] = peak + jnp.log(total)
-    post = (split_ref[...] * (jnp.exp(own_peak - peak) / total)).astype(BF16)
+    peaks = both_ref[:, 0, :]
+    peak = jnp.max(peaks, axis=0, keepdims=True)
+    total = jnp.sum(both_ref[:, 1, :] * jnp.exp(peaks - peak), axis=0, keepdims=True)
+    evidence_buf[...] = peak + jnp.log(total)
+    evidence = pltpu.make_async_copy(evidence_buf, evidence_ref, sems.at[PARTS - 1])
+    evidence.start()
+    posterior = (exp_ref[...] * (jnp.exp(own_peak - peak) / total)).astype(BF16)
+    by_direction = contract(permuter_ref[...], posterior, ((1,), (0,)))
+    kept = row_half_ref[...] == half_ref[...]
+    post = jnp.where(kept, by_direction, 0.0).astype(BF16)
     sums = contract(post, bin_match(bins_ref[...], 1), ((1,), (1,)))
     expos = []
     for part, cols in enumerate(spans):
@@ -260,6 +255,7 @@
         expos.append(expo)
         packed_ref[:, cols] = codes
     packed_ref[:, COLS:] = side_block(sums, expos, 2.0**20)
+    evidence.wait()
 
 
 def plane_kernel(came_ref, packed_ref):
@@ -375,13 +371,17 @@
 
     near, far = pltpu.MemorySpace.VMEM, pltpu.MemorySpace.HBM
     first, rest = count // PARTS, count - count // PARTS
-    by_zh, bins_row, parts, noise_row, power, squares, select = lax.optimization_barrier(
+    permuter = (direction[:, None] == select[None, :]).astype(BF16)
+    (
+        by_zh, bins_row, parts, noise_row, power, squares, permuter, row_half, where, shell_match,
+        shell_spread, half_row, mask_row,
+    ) = lax.optimization_barrier(
         (
             from_all(panels[0], "zh", 4), defocus_bins[None, :], table_parts(table),
-            inverse_noise[None, :], power, squares, select,
+            inverse_noise[None, :], power, squares, permuter, row_half[:, None], where,
+            shell_match, shell_spread, half_sets[None, :], prior_mask.reshape(1, count),
         )
     )
-    permuter = (direction[:, None] == select[None, :]).astype(BF16)
     centred_near, centred_far, weighted_near, weighted_far = call(
         image_kernel, "images",
         [
@@ -399,17 +399,17 @@
 
     own_exp, pair = call(
         score_kernel, "scores", [of((ORIENT, count), F32), of((8, 2, count), F32)], 14,
-        piece, power, bins_row, prior_mask.reshape(1, count), weighted_near, weighted_far,
+        piece, power, bins_row, mask_row, weighted_near, weighted_far,
         far=(5,), scratch=[near((rest, COLS), BF16), pltpu.SemaphoreType.DMA((PARTS,))],
-    )
-    (split,) = call(
-        split_kernel, "split", [of((ROWS, count), F32)], 8,
-        own_exp, permuter, row_half[:, None], half_sets[None, :],
     )
     packed, evidence = call(
         project_kernel, "project", [of((ROWS, WIDE), jnp.int16), of((1, count), F32)], 20,
-        split, pair, exchange(pair, CLS), bins_row, centred_near, centred_far, far=(5,),
-        scratch=[near((count, COLS - PART), BF16), pltpu.SemaphoreType.DMA((PARTS,))],
+        own_exp, pair, exchange(pair, CLS), permuter, row_half, half_row, bins_row,
+        centred_near, centred_far, far=(8,), far_out=(1,),
+        scratch=[
+            near((count, COLS - PART), BF16), near((1, count), F32),
+            pltpu.SemaphoreType.DMA((PARTS,)),
+        ],
     )
     (second,) = call(
         plane_kernel, "plane", [of((4, 16, WIDE), jnp.int16)], 8,

time: 127 us -> 123 us (0.969)
  blocking collectives: 20.7 us -> 65.3 us
  waiting for transfers between devices: 45 us -> 14.8 us
  starting transfers between devices: 34.4 us -> 21.2 us
  Pallas kernels: 17.9 us -> 14.4 us
  local copies, waits for them, and re-layouts: 4.74 us -> 2.92 us
    all_to_all x1 -> x4, blocking collectives: 20.7 us -> 65.3 us  [exchange(): return lax.all_to_all(blocks, axes, split_axis=0, concat_axis=0, tiled=True)]
    all_to_all x5 -> x2, waiting for transfers between devices: 45 us -> 14.8 us  [exchange(): return lax.all_to_all(blocks, axes, split_axis=0, concat_axis=0, tiled=True)]
    all_to_all x5 -> x2, starting transfers between devices: 34.4 us -> 21.2 us  [exchange(): return lax.all_to_all(blocks, axes, split_axis=0, concat_axis=0, tiled=True)]
    pallas_call x7 -> x6, Pallas kernels: 17.9 us -> 14.4 us  [call(): pl.pallas_call(kernel, in_specs=[space(i if i >= scalars else -1, far) fo...]
    unnamed x12 -> x8, local copies, waits for them, and re-layouts: 2.53 us -> 0.7 us
  transfers between devices with their start and end apart: 5 -> 2, of which waited for: 5 -> 2; matrix products, arithmetic and copies ran while one was open for 2% -> 2% of each run, Pallas kernels for 4% -> 4%
where the time goes in v5:
time: 123 us; the launch traced here: 122 us
  blocking collectives  65.3 us (53%)
  starting transfers between devices  21.2 us (17%)
  waiting for transfers between devices  14.8 us (12%)
  Pallas kernels  14.4 us (12%)
  local copies, waits for them, and re-layouts  2.92 us (2%)
  other arithmetic  2.5 us (2%)
    all_to_all x4, blocking collectives, exchange(): return lax.all_to_all(blocks, axes, split_axis=0, concat_axis=0, tiled=True)  65.3 us
    all_to_all x2, starting transfers between devices, exchange(): return lax.all_to_all(blocks, axes, split_axis=0, concat_axis=0, tiled=True)  21.2 us
    all_to_all x2, waiting for transfers between devices, exchange(): return lax.all_to_all(blocks, axes, split_axis=0, concat_axis=0, tiled=True)  14.8 us
    pallas_call x6, Pallas kernels, call(): pl.pallas_call(kernel, in_specs=[space(i if i >= scalars else -1, far) fo...  14.4 us
  transfers between devices with their start and end apart: 2, of which 2 were waited for; matrix products, arithmetic and copies ran while one was open for 2% of the time, Pallas kernels for 4%

profile of v5, /device:TPU:32, one launch (start us, length us, event | category | flops | bytes accessed | tf_op | source)
XLA Modules:
  0.0 122.0 jit_solution(10114312319485562478)
XLA Ops:
  0.6 1.3 %broadcast_in_dim.39 = bf16[4,2,2048]{2,1,0:T(2,128)(2,1)} broadcast(bf16[2,2048]{1,0:T(2,128)(2,1)} %bitcast.19), dimensions={1,2} | broadcast | bytes 40960 | tf_op jit(solution)/shard_map/broadcast_in_dim | solution.py:47
  2.0 14.2 %all-to-all-start = ((bf16[4,2,2048]{2,1,0:T(2,128)(2,1)}), bf16[4,2,2048]{2,1,0:T(2,128)(2,1)S(1)}, u32[]{:S(2)}, u32[]{:S(2)}) async-start(bf16[4,2,2048]{2,1,0:T(2,128)(2,1)} %broadcast_in_dim.39), calls=%async_computation | async-start | bytes 65536 | tf_op jit(solution)/shard_map/all_to_all | solution.py:43
  16.2 0.1 add_select_fusion.row_half_ref
  16.4 0.2 fusion.shells_ref
  16.6 0.7 broadcast_divide_fusion
  17.2 0.1 select_reduce_fusion
  17.4 0.8 select_reduce_fusion.1
  18.2 0.1 compare_convert_fusion.permuter_ref
  18.3 0.3 fusion.17
  18.8 10.1 %all-to-all-done = bf16[4,2,2048]{2,1,0:T(2,128)(2,1)S(1)} async-done(((bf16[4,2,2048]{2,1,0:T(2,128)(2,1)}), bf16[4,2,2048]{2,1,0:T(2,128)(2,1)S(1)}, u32[]{:S(2)}, u32[]{:S(2)}) %all-to-all-start) | async-done | bytes 32800 | tf_op jit(solution)/shard_map/all_to_all | solution.py:43
  28.9 0.9 broadcast_in_dim.73
  29.8 7.0 %all-to-all-start.1 = ((bf16[16,8,2048]{2,1,0:T(8,128)(2,1)}), bf16[16,8,2048]{2,1,0:T(8,128)(2,1)S(1)}, u32[]{:S(2)}, u32[]{:S(2)}) async-start(bf16[16,8,2048]{2,1,0:T(8,128)(2,1)} %broadcast_in_dim.73), calls=%async_computation.1 | async-start | bytes 1048576 | tf_op jit(solution)/shard_map/all_to_all | solution.py:43
  36.8 0.7 copy-done
  37.5 4.7 %images.1 = (bf16[1024,512]{1,0:T(8,128)(2,1)S(1)}, bf16[1024,1536]{1,0:T(8,128)(2,1)}, bf16[256,2048]{1,0:T(8,128)(2,1)S(1)}, bf16[768,2048]{1,0:T(8,128)(2,1)}) custom-call(bf16[1024,2048]{1,0:T(8,128)(2,1)} %x_ref.1, s32[1,1024]{1,0:T(1,128)S(1)} %bitcast.13, bf16[48,1024]{1,0:T(8,128)(2,1)S(1)} %pad_maximum_fusion.table_ref, f32[1,1024]{1,0:T(1,128)S(1)} %bitcast.16), custom_call_target="tpu_custom_call" | custom-call | tf_op jit(solution)/shard_map/images/pallas_call | solution.py:342
  42.2 4.7 %all-to-all-done.1 = bf16[16,8,2048]{2,1,0:T(8,128)(2,1)S(1)} async-done(((bf16[16,8,2048]{2,1,0:T(8,128)(2,1)}), bf16[16,8,2048]{2,1,0:T(8,128)(2,1)S(1)}, u32[]{:S(2)}, u32[]{:S(2)}) %all-to-all-start.1) | async-done | bytes 524320 | tf_op jit(solution)/shard_map/all_to_all | solution.py:43
  46.9 2.9 %scores.1 = (f32[128,1024]{1,0:T(8,128)S(1)}, f32[8,2,1024]{2,1,0:T(2,128)S(1)}) custom-call(bf16[128,2048]{1,0:T(8,128)(2,1)S(1)} %bitcast.11, bf16[16,1024]{1,0:T(8,128)(2,1)S(1)} %get-tuple-element.27.power_ref, s32[1,1024]{1,0:T(1,128)S(1)} %bitcast.14, s32[1,1024]{1,0:T(1,128)S(1)} %bitcast.17, bf16[256,2048]{1,0:T(8,128)(2,1)S(1)} %get-tuple-element.32.near_ref, ...), custom_call_target="tpu_custom_call" | custom-call | tf_op jit(solution)/shard_map/scores/pallas_call | solution.py:342
  49.8 8.9 %all_to_all.30.both_ref = f32[8,2,1024]{2,1,0:T(2,128)S(1)} all-to-all(f32[8,2,1024]{2,1,0:T(2,128)S(1)} %get-tuple-element.35.own_ref), channel_id=1, replica_groups=mesh['zl'=4,'co'=2,'y'=4,'zh'=4,'x'=4] {'zl','co'}, dimensions={0} | all-to-all | bytes 131072 | tf_op jit(solution)/shard_map/all_to_all | solution.py:43
  58.7 3.5 %project.1 = (s16[256,2176]{1,0:T(8,128)(2,1)S(1)}, f32[1,1024]{1,0:T(1,128)}) custom-call(f32[128,1024]{1,0:T(8,128)S(1)} %get-tuple-element.34.exp_ref, f32[8,2,1024]{2,1,0:T(2,128)S(1)} %get-tuple-element.35.own_ref, f32[8,2,1024]{2,1,0:T(2,128)S(1)} %all_to_all.30.both_ref, bf16[256,128]{1,0:T(8,128)(2,1)S(1)} %compare_convert_fusion.permuter_ref, ...), custom_call_target="tpu_custom_call" | custom-call | tf_op jit(solution)/shard_map/project/pallas_call | solution.py:342
  62.2 20.7 %all_to_all.31.came_ref = s16[16,16,2176]{2,1,0:T(8,128)(2,1)S(1)} all-to-all(s16[16,16,2176]{2,1,0:T(8,128)(2,1)S(1)} %bitcast.12), channel_id=1, replica_groups=mesh['zl'=4,'co'=2,'y'=4,'zh'=4,'x'=4] {'y','x'}, dimensions={0} | all-to-all | bytes 2228224 | tf_op jit(solution)/shard_map/all_to_all | solution.py:43
  82.9 0.8 plane.1
  83.7 23.5 %all_to_all.32.came_ref = s16[4,16,2176]{2,1,0:T(8,128)(2,1)S(1)} all-to-all(s16[4,16,2176]{2,1,0:T(8,128)(2,1)S(1)} %plane.1), channel_id=1, replica_groups=mesh['zl'=4,'co'=2,'y'=4,'zh'=4,'x'=4] {'zh'}, dimensions={0} | all-to-all | bytes 557056 | tf_op jit(solution)/shard_map/all_to_all | solution.py:43
  107.3 1.1 shells.1
  108.4 12.2 %all_to_all.33.came_ref = f32[16,8,640]{2,1,0:T(8,128)S(1)} all-to-all(f32[16,8,640]{2,1,0:T(8,128)S(1)} %get-tuple-element.44), channel_id=1, replica_groups=mesh['zl'=4,'co'=2,'y'=4,'zh'=4,'x'=4] {'y','x'}, dimensions={0} | all-to-all | bytes 655360 | tf_op jit(solution)/shard_map/all_to_all | solution.py:43
  120.6 1.4 %finish.1 = f32[1,4,2048]{2,1,0:T(4,128)} custom-call(s32[3]{0:T(128)S(1)} %pad_add_fusion.where_ref, f32[16,8,640]{2,1,0:T(8,128)S(1)} %all_to_all.33.came_ref, f32[2,2048]{1,0:T(2,128)S(1)} %get-tuple-element.45.keep_ref, bf16[128,1024]{1,0:T(8,128)(2,1)S(1)} %fusion.1.spread_ref), custom_call_target="tpu_custom_call" | custom-call | tf_op jit(solution)/shard_map/finish/pallas_call | solution.py:342
  (16 shorter events, 0.2 us)
Async XLA Ops:
  2.0 26.9 %all-to-all-start = ((bf16[4,2,2048]{2,1,0:T(2,128)(2,1)}), bf16[4,2,2048]{2,1,0:T(2,128)(2,1)S(1)}, u32[]{:S(2)}, u32[]{:S(2)}) async-start(bf16[4,2,2048]{2,1,0:T(2,128)(2,1)} %broadcast_in_dim.39), calls=%async_computation | async-start | bytes 65536 | tf_op jit(solution)/shard_map/all_to_all | solution.py:43
  18.3 28.6 %copy-start.1 = (s32[1024]{0:T(1024)S(1)}, s32[1024]{0:T(1024)}, u32[]{:S(2)}) copy-start(s32[1024]{0:T(1024)} %param.10) | copy-start | bytes 12292
  18.3 28.6 %copy-start.2 = (s32[1024,1]{0,1:T(1,128)S(1)}, s32[1024,1]{0,1:T(1,128)}, u32[]{:S(2)}) copy-start(s32[1024,1]{0,1:T(1,128)} %param.12) | copy-start | bytes 12292
  29.8 17.1 %all-to-all-start.1 = ((bf16[16,8,2048]{2,1,0:T(8,128)(2,1)}), bf16[16,8,2048]{2,1,0:T(8,128)(2,1)S(1)}, u32[]{:S(2)}, u32[]{:S(2)}) async-start(bf16[16,8,2048]{2,1,0:T(8,128)(2,1)} %broadcast_in_dim.73), calls=%async_computation.1 | async-start | bytes 1048576 | tf_op jit(solution)/shard_map/all_to_all | solution.py:43
  36.8 0.7 copy-start
  42.2 16.5 %copy-start.3 = (s32[1024]{0:T(1024)S(1)}, s32[1024]{0:T(1024)}, u32[]{:S(2)}) copy-start(s32[1024]{0:T(1024)} %param.11) | copy-start | bytes 12292

commit v6 on v5

--- a/solution.py
+++ b/solution.py
@@ -20,6 +20,7 @@
 WIDE = COLS + SIDE
 CODE = 32767.0
 PARTS = 4
+CHUNK = 256
 PART = COLS // PARTS
 F32 = jnp.float32
 BF16 = jnp.bfloat16
@@ -128,8 +129,8 @@
 
 
 def image_kernel(
-    x_ref, bins_ref, table_ref, noise_ref, centred_near, centred_far, weighted_near, weighted_far,
-    x_buf, centred_buf, weighted_buf, sems
+    x_ref, bins_ref, table_ref, noise_ref, centred_0, centred_1, centred_2, centred_3,
+    weighted_near, weighted_far, x_buf, centred_buf, weighted_buf, sems
 ):
     noise = noise_ref[...]
     steps = PARTS
@@ -141,11 +142,12 @@
         return pltpu.make_async_copy(x_ref.at[rows], x_buf.at[rows], sems.at[0, i])
 
     def write(i, k):
-        if k == 1:
-            rows, buf, out = pl.ds(i * step, step), centred_buf, centred_far
+        if k < PARTS:
+            rows, out = pl.ds(i * step, step), (centred_0, centred_1, centred_2, centred_3)[k]
+            buf = centred_buf.at[:, k * PART : (k + 1) * PART]
         else:
             rows, buf, out = pl.ds((i - edge) * step, step), weighted_buf, weighted_far
-        return pltpu.make_async_copy(buf.at[rows], out.at[rows], sems.at[k, i])
+        return pltpu.make_async_copy(buf.at[rows], out.at[rows], sems.at[k + 1, i])
 
     def chunk(i, keep):
         rows = pl.ds(pl.multiple_of(i * step, step), step)
@@ -155,41 +157,38 @@
         for part in range(2):
             cols = slice(part * PIXC, (part + 1) * PIXC)
             product = x_buf[rows, cols].astype(F32) * contrast
-            rounded = product.astype(BF16)
-            if part == 0:
-                centred_near[rows, :] = rounded[:, :PART]
-                centred_buf[rows, : PIXC - PART] = rounded[:, PART:]
-            else:
-                centred_buf[rows, PIXC - PART :] = rounded
+            centred_buf[rows, cols] = product.astype(BF16)
             scaled = (product * noise).astype(BF16)
             if keep:
                 weighted_near[rows, cols] = scaled
             else:
                 weighted_buf[pl.ds(pl.multiple_of((i - edge) * step, step), step), cols] = scaled
-        write(i, 1).start()
+        for k in range(PARTS):
+            write(i, k).start()
         if not keep:
-            write(i, 2).start()
+            write(i, PARTS).start()
 
     for i in range(steps):
         read(i).start()
     lax.fori_loop(0, edge, lambda i, c: (chunk(i, True), c)[1], 0)
     lax.fori_loop(edge, steps, lambda i, c: (chunk(i, False), c)[1], 0)
     for i in range(steps):
-        write(i, 1).wait()
+        for k in range(PARTS):
+            write(i, k).wait()
         if i >= edge:
-            write(i, 2).wait()
+            write(i, PARTS).wait()
 
 
 def score_kernel(
     panel_ref, power_ref, bins_ref, mask_ref, near_ref, far_ref, exp_ref, pair_ref, far_buf, sems
 ):
-    step = near_ref.shape[0]
+    steps = far_ref.shape[0] // CHUNK
 
     def read(i):
-        rows = pl.ds(i * step, step)
+        rows = pl.ds(i * CHUNK, CHUNK)
         return pltpu.make_async_copy(far_ref.at[rows], far_buf.at[rows], sems.at[i])
 
-    for i in range(PARTS - 1):
+    for i in range(steps):
         read(i).start()
     real = panel_ref[:, :PIXC].astype(F32)
     imag = panel_ref[:, PIXC:].astype(F32)
@@ -197,7 +196,7 @@
     norm = three_parts(contract(panel_power, power_ref[...], ((1,), (1,))), 1)
 
     def chunk(at, weighted):
-        rows = pl.ds(at, step)
+        rows = pl.ds(at, CHUNK)
         norm_part = contract(norm, bin_match(bins_ref[:, rows], 3), ((1,), (0,)))
         direct = contract(panel_ref[...], weighted, ((1,), (1,)))
         scores = direct - 0.5 * norm_part
@@ -211,33 +210,32 @@
         for other in range(8):
             pair_ref[other, :, rows] = pair
 
+    def near_chunk(i, carry):
+        start = pl.multiple_of(i * CHUNK, CHUNK)
+        chunk(start, near_ref[pl.ds(start, CHUNK), :])
+        return carry
+
     def far_chunk(i, carry):
         read(i).wait()
-        start = pl.multiple_of(i * step, step)
-        chunk(pl.multiple_of(start + step, step), far_buf[pl.ds(start, step), :])
+        start = pl.multiple_of(i * CHUNK, CHUNK)
+        chunk(pl.multiple_of(start + near_ref.shape[0], CHUNK), far_buf[pl.ds(start, CHUNK), :])
         return carry
 
-    chunk(0, near_ref[...])
-    lax.fori_loop(0, PARTS - 1, far_chunk, 0)
+    lax.fori_loop(0, near_ref.shape[0] // CHUNK, near_chunk, 0)
+    lax.fori_loop(0, steps, far_chunk, 0)
 
 
 def project_kernel(
-    exp_ref, own_ref, both_ref, permuter_ref, row_half_ref, half_ref, bins_ref, near_ref, far_ref,
-    packed_ref, evidence_ref, far_buf, evidence_buf, sems
+    exp_ref, own_ref, both_ref, permuter_ref, row_half_ref, half_ref, bins_ref, *rest_refs
 ):
+    packed_ref, evidence_ref, evidence_buf, sem = rest_refs[PARTS:]
     spans = [slice(part * PART, (part + 1) * PART) for part in range(PARTS)]
-    reads = [
-        pltpu.make_async_copy(far_ref.at[:, cols], far_buf.at[:, cols], sems.at[part])
-        for part, cols in enumerate(spans[:-1])
-    ]
-    for read in reads:
-        read.start()
     own_peak = own_ref[0, 0:1, :]
     peaks = both_ref[:, 0, :]
     peak = jnp.max(peaks, axis=0, keepdims=True)
     total = jnp.sum(both_ref[:, 1, :] * jnp.exp(peaks - peak), axis=0, keepdims=True)
     evidence_buf[...] = peak + jnp.log(total)
-    evidence = pltpu.make_async_copy(evidence_buf, evidence_ref, sems.at[PARTS - 1])
+    evidence = pltpu.make_async_copy(evidence_buf, evidence_ref, sem)
     evidence.start()
     posterior = (exp_ref[...] * (jnp.exp(own_peak - peak) / total)).astype(BF16)
     by_direction = contract(permuter_ref[...], posterior, ((1,), (0,)))
@@ -246,12 +244,7 @@
     sums = contract(post, bin_match(bins_ref[...], 1), ((1,), (1,)))
     expos = []
     for part, cols in enumerate(spans):
-        if part == 0:
-            centred = near_ref[...]
-        else:
-            reads[part - 1].wait()
-            centred = far_buf[:, spans[part - 1]]
-        codes, expo = encode(contract(post, centred, ((1,), (0,))))
+        codes, expo = encode(contract(post, rest_refs[part][...], ((1,), (0,))))
         expos.append(expo)
         packed_ref[:, cols] = codes
     packed_ref[:, COLS:] = side_block(sums, expos, 2.0**20)
@@ -271,8 +264,8 @@
 
 
 def shell_kernel(where_ref, came_ref, squares_ref, shells_ref, keep_ref, stats_ref):
-    upper = where_ref[0]
-    zh = where_ref[1]
+    upper = where_ref[0:1, 0:1]
+    zh = where_ref[1:2, 0:1]
     data = jnp.concatenate([decode_part(came_ref, 4, part) for part in range(PARTS)], axis=1)
     sums = decode_bins(came_ref, 4, 2.0**16)
     cross = jnp.zeros((1, COLS), F32)
@@ -315,14 +308,17 @@
     half = jnp.broadcast_to((1.0 + fsc) / 2.0, (8, ORIENT))
     factor = contract(three_parts(half, 0), spread_ref[...], ((1,), (0,)))
     factor = factor[0:1] + factor[8:9] + factor[16:17]
-    low = where_ref[0] == 0
-    partner = came_ref[where_ref[2]]
+    low = where_ref[0:1, 0:1] == 0
+    source = where_ref[2:3, 0:1]
+    partner = jnp.zeros((8, PART), F32)
+    for other in range(16):
+        partner = jnp.where(source == other, came_ref[other, :, :PART], partner)
     for part in range(PARTS):
         cols = slice(part * PART, (part + 1) * PART)
         start = (part * PART) % PIXC
         scale = factor[:, start : start + PART]
         keep = keep_ref[:, cols] * scale
-        got = partner[2 * part : 2 * part + 2, :PART] * scale
+        got = partner[2 * part : 2 * part + 2] * scale
         out_ref[0, 0:2, cols] = jnp.where(low, keep, got)
         out_ref[0, 2:4, cols] = jnp.where(low, got, keep)
 
@@ -363,14 +359,15 @@
     shell_match = (shells[:, None] == lanes[None, :]).astype(BF16)
     shell_spread = (lanes[:, None] == shells[None, :]).astype(BF16)
     y, zh, x = lax.axis_index("y"), lax.axis_index("zh"), lax.axis_index("x")
-    where = jnp.stack([y // 2, zh, (y ^ 2) * 4 + x]).astype(jnp.int32)
+    places = jnp.stack([y // 2, zh, (y ^ 2) * 4 + x]).astype(jnp.int32)
+    where = jnp.broadcast_to(jnp.pad(places, (0, 5))[:, None], (8, ORIENT))
 
     direction, row_half = row_maps()
     match = gathered_orients()[:, None] == jnp.arange(ORIENT, dtype=jnp.int32)[None, :]
     select = jnp.sum(jnp.where(match, orient_ids[None, :], 0), axis=1)
 
     near, far = pltpu.MemorySpace.VMEM, pltpu.MemorySpace.HBM
-    first, rest = count // PARTS, count - count // PARTS
+    first, rest = 2 * CHUNK, count - 2 * CHUNK
     permuter = (direction[:, None] == select[None, :]).astype(BF16)
     (
         by_zh, bins_row, parts, noise_row, power, squares, permuter, row_half, where, shell_match,
@@ -382,17 +379,17 @@
             shell_match, shell_spread, half_sets[None, :], prior_mask.reshape(1, count),
         )
     )
-    centred_near, centred_far, weighted_near, weighted_far = call(
+    *centred, weighted_near, weighted_far = call(
         image_kernel, "images",
         [
-            near((count, PART), BF16), far((count, COLS - PART), BF16),
+            *[far((count, PART), BF16)] * PARTS,
             near((first, COLS), BF16), far((rest, COLS), BF16),
         ],
         24, particles, bins_row, parts, noise_row,
-        far=(0,), far_out=(1, 3),
+        far=(0,), far_out=(0, 1, 2, 3, 5),
         scratch=[
-            near((count, COLS), BF16), near((count, COLS - PART), BF16), near((rest, COLS), BF16),
-            pltpu.SemaphoreType.DMA((3, PARTS)),
+            near((count, COLS), BF16), near((count, COLS), BF16), near((rest, COLS), BF16),
+            pltpu.SemaphoreType.DMA((PARTS + 2, PARTS)),
         ],
     )
     piece = from_all(by_zh.reshape(8, COLS), PLANE, 16).reshape(ORIENT, COLS)
@@ -405,11 +402,7 @@
     packed, evidence = call(
         project_kernel, "project", [of((ROWS, WIDE), jnp.int16), of((1, count), F32)], 20,
         own_exp, pair, exchange(pair, CLS), permuter, row_half, half_row, bins_row,
-        centred_near, centred_far, far=(8,), far_out=(1,),
-        scratch=[
-            near((count, COLS - PART), BF16), near((1, count), F32),
-            pltpu.SemaphoreType.DMA((PARTS,)),
-        ],
+        *centred, far_out=(1,), scratch=[near((1, count), F32), pltpu.SemaphoreType.DMA],
     )
     (second,) = call(
         plane_kernel, "plane", [of((4, 16, WIDE), jnp.int16)], 8,
@@ -417,11 +410,11 @@
     )
     keep, stats = call(
         shell_kernel, "shells", [of((2, COLS), F32), of((16, 8, PART + ORIENT), F32)], 8,
-        where, exchange(second, "zh"), squares, shell_match, scalars=1,
+        where, exchange(second, "zh"), squares, shell_match,
     )
     (half_maps,) = call(
         finish_kernel, "finish", [of((1, 4, COLS), F32)], 8,
-        where, exchange(stats, PLANE), keep, shell_spread, scalars=1,
+        where, exchange(stats, PLANE), keep, shell_spread,
     )
     return (half_maps, evidence.reshape(count))
 

time: 123 us -> 121 us (0.984)
  Pallas kernels: 14.4 us -> 12.7 us
    pallas_call x6, Pallas kernels: 14.4 us -> 12.7 us  [call(): pl.pallas_call(kernel, in_specs=[space(i if i >= scalars else -1, far) fo...]
where the time goes in v6:
time: 121 us; the launch traced here: 120 us
  blocking collectives  65.3 us (54%)
  starting transfers between devices  21.2 us (18%)
  waiting for transfers between devices  15.3 us (13%)
  Pallas kernels  12.7 us (10%)
  other arithmetic  2.49 us (2%)
  local copies, waits for them, and re-layouts  2.33 us (2%)
    all_to_all x4, blocking collectives, exchange(): return lax.all_to_all(blocks, axes, split_axis=0, concat_axis=0, tiled=True)  65.3 us
    all_to_all x2, starting transfers between devices, exchange(): return lax.all_to_all(blocks, axes, split_axis=0, concat_axis=0, tiled=True)  21.2 us
    all_to_all x2, waiting for transfers between devices, exchange(): return lax.all_to_all(blocks, axes, split_axis=0, concat_axis=0, tiled=True)  15.3 us
    pallas_call x6, Pallas kernels, call(): pl.pallas_call(kernel, in_specs=[space(i if i >= scalars else -1, far) fo...  12.7 us
  transfers between devices with their start and end apart: 2, of which 2 were waited for; matrix products, arithmetic and copies ran while one was open for 2% of the time, Pallas kernels for 4%

profile of v6, /device:TPU:32, one launch (start us, length us, event | category | flops | bytes accessed | tf_op | source)
XLA Modules:
  0.0 120.1 jit_solution(11550138520357710826)
XLA Ops:
  0.6 1.3 %broadcast_in_dim.41 = bf16[4,2,2048]{2,1,0:T(2,128)(2,1)} broadcast(bf16[2,2048]{1,0:T(2,128)(2,1)} %bitcast.19), dimensions={1,2} | broadcast | bytes 40960 | tf_op jit(solution)/shard_map/broadcast_in_dim | solution.py:48
  2.0 14.2 %all-to-all-start = ((bf16[4,2,2048]{2,1,0:T(2,128)(2,1)}), bf16[4,2,2048]{2,1,0:T(2,128)(2,1)S(1)}, u32[]{:S(2)}, u32[]{:S(2)}) async-start(bf16[4,2,2048]{2,1,0:T(2,128)(2,1)} %broadcast_in_dim.41), calls=%async_computation | async-start | bytes 65536 | tf_op jit(solution)/shard_map/all_to_all | solution.py:44
  16.2 0.1 add_select_fusion.row_half_ref
  16.4 0.2 fusion.shells_ref
  16.6 0.1 pad_add_fusion
  16.7 0.7 broadcast_divide_fusion
  17.3 0.1 select_reduce_fusion
  17.4 0.8 select_reduce_fusion.1
  18.3 0.1 compare_convert_fusion.permuter_ref
  18.4 0.3 fusion.17
  18.7 10.2 %all-to-all-done = bf16[4,2,2048]{2,1,0:T(2,128)(2,1)S(1)} async-done(((bf16[4,2,2048]{2,1,0:T(2,128)(2,1)}), bf16[4,2,2048]{2,1,0:T(2,128)(2,1)S(1)}, u32[]{:S(2)}, u32[]{:S(2)}) %all-to-all-start) | async-done | bytes 32800 | tf_op jit(solution)/shard_map/all_to_all | solution.py:44
  29.0 0.9 broadcast_in_dim.80
  29.9 7.0 %all-to-all-start.1 = ((bf16[16,8,2048]{2,1,0:T(8,128)(2,1)}), bf16[16,8,2048]{2,1,0:T(8,128)(2,1)S(1)}, u32[]{:S(2)}, u32[]{:S(2)}) async-start(bf16[16,8,2048]{2,1,0:T(8,128)(2,1)} %broadcast_in_dim.80), calls=%async_computation.1 | async-start | bytes 1048576 | tf_op jit(solution)/shard_map/all_to_all | solution.py:44
  36.9 4.9 %images.1 = (bf16[1024,512]{1,0:T(8,128)(2,1)}, bf16[1024,512]{1,0:T(8,128)(2,1)}, bf16[1024,512]{1,0:T(8,128)(2,1)}, bf16[1024,512]{1,0:T(8,128)(2,1)}, bf16[51...) custom-call(bf16[1024,2048]{1,0:T(8,128)(2,1)} %x_ref.1, s32[1,1024]{1,0:T(1,128)S(1)} %bitcast.13, ...), custom_call_target="tpu_custom_call" | custom-call | tf_op jit(solution)/shard_map/images/pallas_call | solution.py:338
  41.8 5.2 %all-to-all-done.1 = bf16[16,8,2048]{2,1,0:T(8,128)(2,1)S(1)} async-done(((bf16[16,8,2048]{2,1,0:T(8,128)(2,1)}), bf16[16,8,2048]{2,1,0:T(8,128)(2,1)S(1)}, u32[]{:S(2)}, u32[]{:S(2)}) %all-to-all-start.1) | async-done | bytes 524320 | tf_op jit(solution)/shard_map/all_to_all | solution.py:44
  47.0 2.5 %scores.1 = (f32[128,1024]{1,0:T(8,128)S(1)}, f32[8,2,1024]{2,1,0:T(2,128)S(1)}) custom-call(bf16[128,2048]{1,0:T(8,128)(2,1)S(1)} %bitcast.11, bf16[16,1024]{1,0:T(8,128)(2,1)S(1)} %get-tuple-element.29.power_ref, s32[1,1024]{1,0:T(1,128)S(1)} %bitcast.14, s32[1,1024]{1,0:T(1,128)S(1)} %bitcast.17, bf16[512,2048]{1,0:T(8,128)(2,1)S(1)} %get-tuple-element.34.near_ref, ...), custom_call_target="tpu_custom_call" | custom-call | tf_op jit(solution)/shard_map/scores/pallas_call | solution.py:338
  49.5 8.9 %all_to_all.30.both_ref = f32[8,2,1024]{2,1,0:T(2,128)S(1)} all-to-all(f32[8,2,1024]{2,1,0:T(2,128)S(1)} %get-tuple-element.37.own_ref), channel_id=1, replica_groups=mesh['zl'=4,'co'=2,'y'=4,'zh'=4,'x'=4] {'zl','co'}, dimensions={0} | all-to-all | bytes 131072 | tf_op jit(solution)/shard_map/all_to_all | solution.py:44
  58.4 3.1 %project.1 = (s16[256,2176]{1,0:T(8,128)(2,1)S(1)}, f32[1,1024]{1,0:T(1,128)}) custom-call(f32[128,1024]{1,0:T(8,128)S(1)} %get-tuple-element.36.exp_ref, f32[8,2,1024]{2,1,0:T(2,128)S(1)} %get-tuple-element.37.own_ref, f32[8,2,1024]{2,1,0:T(2,128)S(1)} %all_to_all.30.both_ref, bf16[256,128]{1,0:T(8,128)(2,1)S(1)} %compare_convert_fusion.permuter_ref, ...), custom_call_target="tpu_custom_call" | custom-call | tf_op jit(solution)/shard_map/project/pallas_call | solution.py:338
  61.5 20.7 %all_to_all.31.came_ref = s16[16,16,2176]{2,1,0:T(8,128)(2,1)S(1)} all-to-all(s16[16,16,2176]{2,1,0:T(8,128)(2,1)S(1)} %bitcast.12), channel_id=1, replica_groups=mesh['zl'=4,'co'=2,'y'=4,'zh'=4,'x'=4] {'y','x'}, dimensions={0} | all-to-all | bytes 2228224 | tf_op jit(solution)/shard_map/all_to_all | solution.py:44
  82.2 0.8 plane.1
  83.0 23.5 %all_to_all.32.came_ref = s16[4,16,2176]{2,1,0:T(8,128)(2,1)S(1)} all-to-all(s16[4,16,2176]{2,1,0:T(8,128)(2,1)S(1)} %plane.1), channel_id=1, replica_groups=mesh['zl'=4,'co'=2,'y'=4,'zh'=4,'x'=4] {'zh'}, dimensions={0} | all-to-all | bytes 557056 | tf_op jit(solution)/shard_map/all_to_all | solution.py:44
  106.5 0.6 shells.1
  107.1 12.2 %all_to_all.33.came_ref = f32[16,8,640]{2,1,0:T(8,128)S(1)} all-to-all(f32[16,8,640]{2,1,0:T(8,128)S(1)} %get-tuple-element.48), channel_id=1, replica_groups=mesh['zl'=4,'co'=2,'y'=4,'zh'=4,'x'=4] {'y','x'}, dimensions={0} | all-to-all | bytes 655360 | tf_op jit(solution)/shard_map/all_to_all | solution.py:44
  119.3 0.8 finish.1
  (24 shorter events, 0.2 us)
Async XLA Ops:
  0.6 36.3 %copy-start.4 = (s32[1024]{0:T(1024)S(1)}, s32[1024]{0:T(1024)}, u32[]{:S(2)}) copy-start(s32[1024]{0:T(1024)} %param.10) | copy-start | bytes 12292
  2.0 26.9 %all-to-all-start = ((bf16[4,2,2048]{2,1,0:T(2,128)(2,1)}), bf16[4,2,2048]{2,1,0:T(2,128)(2,1)S(1)}, u32[]{:S(2)}, u32[]{:S(2)}) async-start(bf16[4,2,2048]{2,1,0:T(2,128)(2,1)} %broadcast_in_dim.41), calls=%async_computation | async-start | bytes 65536 | tf_op jit(solution)/shard_map/all_to_all | solution.py:44
  29.9 17.1 %all-to-all-start.1 = ((bf16[16,8,2048]{2,1,0:T(8,128)(2,1)}), bf16[16,8,2048]{2,1,0:T(8,128)(2,1)S(1)}, u32[]{:S(2)}, u32[]{:S(2)}) async-start(bf16[16,8,2048]{2,1,0:T(8,128)(2,1)} %broadcast_in_dim.80), calls=%async_computation.1 | async-start | bytes 1048576 | tf_op jit(solution)/shard_map/all_to_all | solution.py:44
  36.9 10.1 %copy-start.5 = (s32[1024,1]{0,1:T(1,128)S(1)}, s32[1024,1]{0,1:T(1,128)}, u32[]{:S(2)}) copy-start(s32[1024,1]{0,1:T(1,128)} %param.12) | copy-start | bytes 12292
  47.0 11.4 %copy-start = (bf16[1024,512]{1,0:T(8,128)(2,1)S(1)}, bf16[1024,512]{1,0:T(8,128)(2,1)}, u32[]{:S(2)}) copy-start(bf16[1024,512]{1,0:T(8,128)(2,1)} %get-tuple-element.41.rest_refs_0_) | copy-start | bytes 3145732
  47.0 11.4 %copy-start.1 = (bf16[1024,512]{1,0:T(8,128)(2,1)S(1)}, bf16[1024,512]{1,0:T(8,128)(2,1)}, u32[]{:S(2)}) copy-start(bf16[1024,512]{1,0:T(8,128)(2,1)} %get-tuple-element.42.rest_refs_1_) | copy-start | bytes 3145732
  47.0 11.4 %copy-start.2 = (bf16[1024,512]{1,0:T(8,128)(2,1)S(1)}, bf16[1024,512]{1,0:T(8,128)(2,1)}, u32[]{:S(2)}) copy-start(bf16[1024,512]{1,0:T(8,128)(2,1)} %get-tuple-element.43.rest_refs_2_) | copy-start | bytes 3145732
  47.0 11.4 %copy-start.3 = (bf16[1024,512]{1,0:T(8,128)(2,1)S(1)}, bf16[1024,512]{1,0:T(8,128)(2,1)}, u32[]{:S(2)}) copy-start(bf16[1024,512]{1,0:T(8,128)(2,1)} %get-tuple-element.44.rest_refs_3_) | copy-start | bytes 3145732
  47.0 11.4 %copy-start.6 = (s32[1024]{0:T(1024)S(1)}, s32[1024]{0:T(1024)}, u32[]{:S(2)}) copy-start(s32[1024]{0:T(1024)} %param.11) | copy-start | bytes 12292

commit v7 on v6

--- a/solution.py
+++ b/solution.py
@@ -48,11 +48,13 @@
     return exchange(jnp.broadcast_to(shard[None], (count,) + shard.shape), axes)
 
 
-def row_maps():
-    r = jnp.arange(ROWS, dtype=jnp.int32)
-    j, swap, zh, x, y = r % 2, (r // 2) % 2, (r // 4) % 4, (r // 16) % 4, r // 64
-    direction = 4 * (((y % 2) * 4 + zh) * 4 + x) + 2 * (y // 2) + j
-    return direction, (swap + y // 2) % 2
+def row_direction(r):
+    j, zh, x, y = r & 1, (r >> 2) & 3, (r >> 4) & 3, r >> 6
+    return 4 * (((y & 1) * 4 + zh) * 4 + x) + 2 * (y >> 1) + j
+
+
+def row_half(r):
+    return ((r >> 1) & 1) ^ (r >> 7)
 
 
 def gathered_orients():
@@ -88,7 +90,7 @@
 def encode(values):
     size = jnp.abs(values)
     top = jnp.max(size, axis=1, keepdims=True)
-    expo = jnp.floor(jnp.log2(jnp.maximum(top, 1e-30))) + 1.0
+    expo = jnp.floor(jnp.log2(jnp.maximum(top, 1e-37))) + 1.0
     root = lax.rsqrt(lax.rsqrt(jnp.maximum(size * jnp.exp2(-expo), 1e-36)))
     code = root * CODE + 0.5
     codes = jnp.where(values < 0.0, -code, code).astype(jnp.int32).astype(jnp.int16)
@@ -113,8 +115,8 @@
     data = jnp.zeros((ref.shape[1], PART), F32)
     for source in range(count):
         expo = ref[source, :, COLS:].astype(jnp.int32)[:, at - COLS : at - COLS + 1]
-        scale = jnp.exp2(expo.astype(F32)) * (1.0 / CODE**4)
-        root = ref[source, :, cols].astype(jnp.int32).astype(F32)
+        scale = jnp.exp2(expo.astype(F32))
+        root = ref[source, :, cols].astype(jnp.int32).astype(F32) * (1.0 / CODE)
         data = data + root * jnp.abs(root) * (root * root) * scale
     return data
 
@@ -226,7 +228,7 @@
 
 
 def project_kernel(
-    exp_ref, own_ref, both_ref, permuter_ref, row_half_ref, half_ref, bins_ref, *rest_refs
+    exp_ref, own_ref, both_ref, permuter_ref, half_ref, bins_ref, *rest_refs
 ):
     packed_ref, evidence_ref, evidence_buf, sem = rest_refs[PARTS:]
     spans = [slice(part * PART, (part + 1) * PART) for part in range(PARTS)]
@@ -239,7 +241,8 @@
     evidence.start()
     posterior = (exp_ref[...] * (jnp.exp(own_peak - peak) / total)).astype(BF16)
     by_direction = contract(permuter_ref[...], posterior, ((1,), (0,)))
-    kept = row_half_ref[...] == half_ref[...]
+    row = lax.broadcasted_iota(jnp.int32, (ROWS, 1), 0)
+    kept = row_half(row) == half_ref[...]
     post = jnp.where(kept, by_direction, 0.0).astype(BF16)
     sums = contract(post, bin_match(bins_ref[...], 1), ((1,), (1,)))
     expos = []
@@ -284,7 +287,7 @@
     power1 = jnp.where(upper == 0, second, first)
     three = jnp.concatenate([cross, power0, power1, jnp.zeros((5, COLS), F32)], axis=0)
     folded = three[:, :PIXC] + three[:, PIXC:]
-    by_shell = contract(three_parts(folded, 0), shells_ref[...], ((1,), (0,)))
+    by_shell = contract(three_parts(folded, 0), shells_ref[...], ((1,), (1,)))
     by_shell = by_shell[0:8] + by_shell[8:16] + by_shell[16:24]
     squares = squares_ref[...]
     weight = contract(
@@ -356,13 +359,12 @@
     power = (table * table * inverse_noise[None, :]).astype(BF16)
     squares = (table * table).astype(BF16)
     lanes = jnp.arange(ORIENT, dtype=jnp.int32)
-    shell_match = (shells[:, None] == lanes[None, :]).astype(BF16)
     shell_spread = (lanes[:, None] == shells[None, :]).astype(BF16)
     y, zh, x = lax.axis_index("y"), lax.axis_index("zh"), lax.axis_index("x")
     places = jnp.stack([y // 2, zh, (y ^ 2) * 4 + x]).astype(jnp.int32)
     where = jnp.broadcast_to(jnp.pad(places, (0, 5))[:, None], (8, ORIENT))
 
-    direction, row_half = row_maps()
+    direction = row_direction(jnp.arange(ROWS, dtype=jnp.int32))
     match = gathered_orients()[:, None] == jnp.arange(ORIENT, dtype=jnp.int32)[None, :]
     select = jnp.sum(jnp.where(match, orient_ids[None, :], 0), axis=1)
 
@@ -370,13 +372,12 @@
     first, rest = 2 * CHUNK, count - 2 * CHUNK
     permuter = (direction[:, None] == select[None, :]).astype(BF16)
     (
-        by_zh, bins_row, parts, noise_row, power, squares, permuter, row_half, where, shell_match,
-        shell_spread, half_row, mask_row,
+        by_zh, bins_row, parts, noise_row, power, squares, permuter, where, shell_spread, half_row,
+        mask_row,
     ) = lax.optimization_barrier(
         (
             from_all(panels[0], "zh", 4), defocus_bins[None, :], table_parts(table),
-            inverse_noise[None, :], power, squares, permuter, row_half[:, None], where,
-            shell_match, shell_spread, half_sets[None, :], prior_mask.reshape(1, count),
+            inverse_noise[None, :], power, squares, permuter, where, shell_spread, half_sets[None, :], prior_mask.reshape(1, count),
         )
     )
     *centred, weighted_near, weighted_far = call(
@@ -401,7 +402,7 @@
     )
     packed, evidence = call(
         project_kernel, "project", [of((ROWS, WIDE), jnp.int16), of((1, count), F32)], 20,
-        own_exp, pair, exchange(pair, CLS), permuter, row_half, half_row, bins_row,
+        own_exp, pair, exchange(pair, CLS), permuter, half_row, bins_row,
         *centred, far_out=(1,), scratch=[near((1, count), F32), pltpu.SemaphoreType.DMA],
     )
     (second,) = call(
@@ -410,7 +411,7 @@
     )
     keep, stats = call(
         shell_kernel, "shells", [of((2, COLS), F32), of((16, 8, PART + ORIENT), F32)], 8,
-        where, exchange(second, "zh"), squares, shell_match,
+        where, exchange(second, "zh"), squares, shell_spread,
     )
     (half_maps,) = call(
         finish_kernel, "finish", [of((1, 4, COLS), F32)], 8,

time: 121 us -> 121 us (level)
  no operation moved by 1% of the time
where the time goes in v7:
time: 121 us; the launch traced here: 120 us
  blocking collectives  65.3 us (54%)
  starting transfers between devices  21.2 us (18%)
  waiting for transfers between devices  15.7 us (13%)
  Pallas kernels  12.7 us (10%)
  local copies, waits for them, and re-layouts  2.33 us (2%)
  other arithmetic  2.21 us (2%)
    all_to_all x4, blocking collectives, exchange(): return lax.all_to_all(blocks, axes, split_axis=0, concat_axis=0, tiled=True)  65.3 us
    all_to_all x2, starting transfers between devices, exchange(): return lax.all_to_all(blocks, axes, split_axis=0, concat_axis=0, tiled=True)  21.2 us
    all_to_all x2, waiting for transfers between devices, exchange(): return lax.all_to_all(blocks, axes, split_axis=0, concat_axis=0, tiled=True)  15.7 us
    pallas_call x6, Pallas kernels, call(): pl.pallas_call(kernel, in_specs=[space(i if i >= scalars else -1, far) fo...  12.7 us
  transfers between devices with their start and end apart: 2, of which 2 were waited for; matrix products, arithmetic and copies ran while one was open for 2% of the time, Pallas kernels for 4%

profile of v7, /device:TPU:32, one launch (start us, length us, event | category | flops | bytes accessed | tf_op | source)
XLA Modules:
  0.0 120.2 jit_solution(7083999227849563033)
XLA Ops:
  0.6 1.3 %broadcast_in_dim.41 = bf16[4,2,2048]{2,1,0:T(2,128)(2,1)} broadcast(bf16[2,2048]{1,0:T(2,128)(2,1)} %bitcast.19), dimensions={1,2} | broadcast | bytes 40960 | tf_op jit(solution)/shard_map/broadcast_in_dim | solution.py:48
  2.0 14.2 %all-to-all-start = ((bf16[4,2,2048]{2,1,0:T(2,128)(2,1)}), bf16[4,2,2048]{2,1,0:T(2,128)(2,1)S(1)}, u32[]{:S(2)}, u32[]{:S(2)}) async-start(bf16[4,2,2048]{2,1,0:T(2,128)(2,1)} %broadcast_in_dim.41), calls=%async_computation | async-start | bytes 65536 | tf_op jit(solution)/shard_map/all_to_all | solution.py:44
  16.2 0.1 pad_add_fusion
  16.3 0.7 broadcast_divide_fusion
  17.0 0.1 fusion.shells_ref.spread_ref
  17.0 0.1 select_reduce_fusion
  17.1 0.8 select_reduce_fusion.1
  18.0 0.1 compare_convert_fusion.permuter_ref
  18.1 0.3 fusion.3
  18.4 10.5 %all-to-all-done = bf16[4,2,2048]{2,1,0:T(2,128)(2,1)S(1)} async-done(((bf16[4,2,2048]{2,1,0:T(2,128)(2,1)}), bf16[4,2,2048]{2,1,0:T(2,128)(2,1)S(1)}, u32[]{:S(2)}, u32[]{:S(2)}) %all-to-all-start) | async-done | bytes 32800 | tf_op jit(solution)/shard_map/all_to_all | solution.py:44
  28.9 0.1 broadcast_in_dim.74.where_ref
  29.0 0.9 broadcast_in_dim.77
  29.9 7.0 %all-to-all-start.1 = ((bf16[16,8,2048]{2,1,0:T(8,128)(2,1)}), bf16[16,8,2048]{2,1,0:T(8,128)(2,1)S(1)}, u32[]{:S(2)}, u32[]{:S(2)}) async-start(bf16[16,8,2048]{2,1,0:T(8,128)(2,1)} %broadcast_in_dim.77), calls=%async_computation.1 | async-start | bytes 1048576 | tf_op jit(solution)/shard_map/all_to_all | solution.py:44
  36.9 4.9 %images.1 = (bf16[1024,512]{1,0:T(8,128)(2,1)}, bf16[1024,512]{1,0:T(8,128)(2,1)}, bf16[1024,512]{1,0:T(8,128)(2,1)}, bf16[1024,512]{1,0:T(8,128)(2,1)}, bf16[51...) custom-call(bf16[1024,2048]{1,0:T(8,128)(2,1)} %x_ref.1, s32[1,1024]{1,0:T(1,128)S(1)} %bitcast.13, ...), custom_call_target="tpu_custom_call" | custom-call | tf_op jit(solution)/shard_map/images/pallas_call | solution.py:341
  41.8 5.2 %all-to-all-done.1 = bf16[16,8,2048]{2,1,0:T(8,128)(2,1)S(1)} async-done(((bf16[16,8,2048]{2,1,0:T(8,128)(2,1)}), bf16[16,8,2048]{2,1,0:T(8,128)(2,1)S(1)}, u32[]{:S(2)}, u32[]{:S(2)}) %all-to-all-start.1) | async-done | bytes 524320 | tf_op jit(solution)/shard_map/all_to_all | solution.py:44
  47.0 2.5 %scores.1 = (f32[128,1024]{1,0:T(8,128)S(1)}, f32[8,2,1024]{2,1,0:T(2,128)S(1)}) custom-call(bf16[128,2048]{1,0:T(8,128)(2,1)S(1)} %bitcast.11, bf16[16,1024]{1,0:T(8,128)(2,1)S(1)} %get-tuple-element.27.power_ref, s32[1,1024]{1,0:T(1,128)S(1)} %bitcast.14, s32[1,1024]{1,0:T(1,128)S(1)} %bitcast.17, bf16[512,2048]{1,0:T(8,128)(2,1)S(1)} %get-tuple-element.32.near_ref, ...), custom_call_target="tpu_custom_call" | custom-call | tf_op jit(solution)/shard_map/scores/pallas_call | solution.py:341
  49.5 8.9 %all_to_all.30.both_ref = f32[8,2,1024]{2,1,0:T(2,128)S(1)} all-to-all(f32[8,2,1024]{2,1,0:T(2,128)S(1)} %get-tuple-element.35.own_ref), channel_id=1, replica_groups=mesh['zl'=4,'co'=2,'y'=4,'zh'=4,'x'=4] {'zl','co'}, dimensions={0} | all-to-all | bytes 131072 | tf_op jit(solution)/shard_map/all_to_all | solution.py:44
  58.4 3.1 %project.1 = (s16[256,2176]{1,0:T(8,128)(2,1)S(1)}, f32[1,1024]{1,0:T(1,128)}) custom-call(f32[128,1024]{1,0:T(8,128)S(1)} %get-tuple-element.34.exp_ref, f32[8,2,1024]{2,1,0:T(2,128)S(1)} %get-tuple-element.35.own_ref, f32[8,2,1024]{2,1,0:T(2,128)S(1)} %all_to_all.30.both_ref, bf16[256,128]{1,0:T(8,128)(2,1)S(1)} %compare_convert_fusion.permuter_ref, ...), custom_call_target="tpu_custom_call" | custom-call | tf_op jit(solution)/shard_map/project/pallas_call | solution.py:341
  61.5 20.7 %all_to_all.31.came_ref = s16[16,16,2176]{2,1,0:T(8,128)(2,1)S(1)} all-to-all(s16[16,16,2176]{2,1,0:T(8,128)(2,1)S(1)} %bitcast.12), channel_id=1, replica_groups=mesh['zl'=4,'co'=2,'y'=4,'zh'=4,'x'=4] {'y','x'}, dimensions={0} | all-to-all | bytes 2228224 | tf_op jit(solution)/shard_map/all_to_all | solution.py:44
  82.2 0.9 plane.1
  83.0 23.6 %all_to_all.32.came_ref = s16[4,16,2176]{2,1,0:T(8,128)(2,1)S(1)} all-to-all(s16[4,16,2176]{2,1,0:T(8,128)(2,1)S(1)} %plane.1), channel_id=1, replica_groups=mesh['zl'=4,'co'=2,'y'=4,'zh'=4,'x'=4] {'zh'}, dimensions={0} | all-to-all | bytes 557056 | tf_op jit(solution)/shard_map/all_to_all | solution.py:44
  106.6 0.6 shells.1
  107.2 12.2 %all_to_all.33.came_ref = f32[16,8,640]{2,1,0:T(8,128)S(1)} all-to-all(f32[16,8,640]{2,1,0:T(8,128)S(1)} %get-tuple-element.45), channel_id=1, replica_groups=mesh['zl'=4,'co'=2,'y'=4,'zh'=4,'x'=4] {'y','x'}, dimensions={0} | all-to-all | bytes 655360 | tf_op jit(solution)/shard_map/all_to_all | solution.py:44
  119.4 0.8 finish.1
  (22 shorter events, 0.1 us)
Async XLA Ops:
  0.6 36.3 %copy-start.4 = (s32[1024]{0:T(1024)S(1)}, s32[1024]{0:T(1024)}, u32[]{:S(2)}) copy-start(s32[1024]{0:T(1024)} %param.10) | copy-start | bytes 12292
  2.0 26.9 %all-to-all-start = ((bf16[4,2,2048]{2,1,0:T(2,128)(2,1)}), bf16[4,2,2048]{2,1,0:T(2,128)(2,1)S(1)}, u32[]{:S(2)}, u32[]{:S(2)}) async-start(bf16[4,2,2048]{2,1,0:T(2,128)(2,1)} %broadcast_in_dim.41), calls=%async_computation | async-start | bytes 65536 | tf_op jit(solution)/shard_map/all_to_all | solution.py:44
  29.9 17.1 %all-to-all-start.1 = ((bf16[16,8,2048]{2,1,0:T(8,128)(2,1)}), bf16[16,8,2048]{2,1,0:T(8,128)(2,1)S(1)}, u32[]{:S(2)}, u32[]{:S(2)}) async-start(bf16[16,8,2048]{2,1,0:T(8,128)(2,1)} %broadcast_in_dim.77), calls=%async_computation.1 | async-start | bytes 1048576 | tf_op jit(solution)/shard_map/all_to_all | solution.py:44
  36.9 10.1 %copy-start.5 = (s32[1024,1]{0,1:T(1,128)S(1)}, s32[1024,1]{0,1:T(1,128)}, u32[]{:S(2)}) copy-start(s32[1024,1]{0,1:T(1,128)} %param.12) | copy-start | bytes 12292
  47.0 11.4 %copy-start = (bf16[1024,512]{1,0:T(8,128)(2,1)S(1)}, bf16[1024,512]{1,0:T(8,128)(2,1)}, u32[]{:S(2)}) copy-start(bf16[1024,512]{1,0:T(8,128)(2,1)} %get-tuple-element.38.rest_refs_0_) | copy-start | bytes 3145732
  47.0 11.4 %copy-start.1 = (bf16[1024,512]{1,0:T(8,128)(2,1)S(1)}, bf16[1024,512]{1,0:T(8,128)(2,1)}, u32[]{:S(2)}) copy-start(bf16[1024,512]{1,0:T(8,128)(2,1)} %get-tuple-element.39.rest_refs_1_) | copy-start | bytes 3145732
  47.0 11.4 %copy-start.2 = (bf16[1024,512]{1,0:T(8,128)(2,1)S(1)}, bf16[1024,512]{1,0:T(8,128)(2,1)}, u32[]{:S(2)}) copy-start(bf16[1024,512]{1,0:T(8,128)(2,1)} %get-tuple-element.40.rest_refs_2_) | copy-start | bytes 3145732
  47.0 11.4 %copy-start.3 = (bf16[1024,512]{1,0:T(8,128)(2,1)S(1)}, bf16[1024,512]{1,0:T(8,128)(2,1)}, u32[]{:S(2)}) copy-start(bf16[1024,512]{1,0:T(8,128)(2,1)} %get-tuple-element.41.rest_refs_3_) | copy-start | bytes 3145732
  47.0 11.4 %copy-start.6 = (s32[1024]{0:T(1024)S(1)}, s32[1024]{0:T(1024)}, u32[]{:S(2)}) copy-start(s32[1024]{0:T(1024)} %param.11) | copy-start | bytes 12292

commit v8 on v7

--- a/solution.py
+++ b/solution.py
@@ -259,11 +259,8 @@
     for part in range(PARTS):
         codes, expo = encode(decode_part(came_ref, 16, part))
         expos.append(expo)
-        for other in range(4):
-            packed_ref[other, :, part * PART : (part + 1) * PART] = codes
-    side = side_block(decode_bins(came_ref, 16, 2.0**20), expos, 2.0**16)
-    for other in range(4):
-        packed_ref[other, :, COLS:] = side
+        packed_ref[:, part * PART : (part + 1) * PART] = codes
+    packed_ref[:, COLS:] = side_block(decode_bins(came_ref, 16, 2.0**20), expos, 2.0**16)
 
 
 def shell_kernel(where_ref, came_ref, squares_ref, shells_ref, keep_ref, stats_ref):
@@ -406,12 +403,12 @@
         *centred, far_out=(1,), scratch=[near((1, count), F32), pltpu.SemaphoreType.DMA],
     )
     (second,) = call(
-        plane_kernel, "plane", [of((4, 16, WIDE), jnp.int16)], 8,
+        plane_kernel, "plane", [of((16, WIDE), jnp.int16)], 8,
         exchange(packed.reshape(16, 16, WIDE), PLANE),
     )
     keep, stats = call(
         shell_kernel, "shells", [of((2, COLS), F32), of((16, 8, PART + ORIENT), F32)], 8,
-        where, exchange(second, "zh"), squares, shell_spread,
+        where, lax.all_gather(second, "zh"), squares, shell_spread,
     )
     (half_maps,) = call(
         finish_kernel, "finish", [of((1, 4, COLS), F32)], 8,

time: 121 us -> 117 us (0.967)
  the two profiles are of different devices: /device:TPU:32 before, /device:TPU:2 now
where the time goes in v8:
time: 117 us
  blocking collectives  61.6 us (53%)
  starting transfers between devices  22.6 us (19%)
  waiting for transfers between devices  14.5 us (12%)
  Pallas kernels  12.7 us (11%)
  local copies, waits for them, and re-layouts  2.33 us (2%)
  other arithmetic  2.21 us (2%)
    all_to_all x3, blocking collectives, exchange(): return lax.all_to_all(blocks, axes, split_axis=0, concat_axis=0, tiled=True)  42.2 us
    all_to_all x2, starting transfers between devices, exchange(): return lax.all_to_all(blocks, axes, split_axis=0, concat_axis=0, tiled=True)  22.6 us
    all_gather x1, blocking collectives, on_device(): lax.all_gather(second, 'zh')  19.4 us
    all_to_all x2, waiting for transfers between devices, exchange(): return lax.all_to_all(blocks, axes, split_axis=0, concat_axis=0, tiled=True)  14.5 us
    pallas_call x6, Pallas kernels, call(): pl.pallas_call(kernel, in_specs=[space(i if i >= scalars else -1, far) fo...  12.7 us
  transfers between devices with their start and end apart: 2, of which 2 were waited for; matrix products, arithmetic and copies ran while one was open for 2% of the time, Pallas kernels for 4%

profile of v8, /device:TPU:2, one launch (start us, length us, event | category | flops | bytes accessed | tf_op | source)
XLA Modules:
  0.0 116.8 jit_solution(13143227602203366198)
XLA Ops:
  0.6 1.3 %broadcast_in_dim.41 = bf16[4,2,2048]{2,1,0:T(2,128)(2,1)} broadcast(bf16[2,2048]{1,0:T(2,128)(2,1)} %bitcast.21), dimensions={1,2} | broadcast | bytes 40960 | tf_op jit(solution)/shard_map/broadcast_in_dim | solution.py:48
  2.0 15.1 %all-to-all-start = ((bf16[4,2,2048]{2,1,0:T(2,128)(2,1)}), bf16[4,2,2048]{2,1,0:T(2,128)(2,1)S(1)}, u32[]{:S(2)}, u32[]{:S(2)}) async-start(bf16[4,2,2048]{2,1,0:T(2,128)(2,1)} %broadcast_in_dim.41), calls=%async_computation | async-start | bytes 65536 | tf_op jit(solution)/shard_map/all_to_all | solution.py:44
  17.1 0.1 pad_add_fusion
  17.2 0.7 broadcast_divide_fusion
  17.9 0.1 fusion.shells_ref.spread_ref
  17.9 0.1 select_reduce_fusion
  18.0 0.8 select_reduce_fusion.1
  18.9 0.1 compare_convert_fusion.permuter_ref
  19.0 0.3 fusion.3
  19.3 10.5 %all-to-all-done = bf16[4,2,2048]{2,1,0:T(2,128)(2,1)S(1)} async-done(((bf16[4,2,2048]{2,1,0:T(2,128)(2,1)}), bf16[4,2,2048]{2,1,0:T(2,128)(2,1)S(1)}, u32[]{:S(2)}, u32[]{:S(2)}) %all-to-all-start) | async-done | bytes 32800 | tf_op jit(solution)/shard_map/all_to_all | solution.py:44
  29.8 0.1 broadcast_in_dim.74.where_ref
  29.9 0.9 broadcast_in_dim.77
  30.8 7.5 %all-to-all-start.1 = ((bf16[16,8,2048]{2,1,0:T(8,128)(2,1)}), bf16[16,8,2048]{2,1,0:T(8,128)(2,1)S(1)}, u32[]{:S(2)}, u32[]{:S(2)}) async-start(bf16[16,8,2048]{2,1,0:T(8,128)(2,1)} %broadcast_in_dim.77), calls=%async_computation.1 | async-start | bytes 1048576 | tf_op jit(solution)/shard_map/all_to_all | solution.py:44
  38.3 4.9 %images.1 = (bf16[1024,512]{1,0:T(8,128)(2,1)}, bf16[1024,512]{1,0:T(8,128)(2,1)}, bf16[1024,512]{1,0:T(8,128)(2,1)}, bf16[1024,512]{1,0:T(8,128)(2,1)}, bf16[51...) custom-call(bf16[1024,2048]{1,0:T(8,128)(2,1)} %x_ref.1, s32[1,1024]{1,0:T(1,128)S(1)} %bitcast.15, ...), custom_call_target="tpu_custom_call" | custom-call | tf_op jit(solution)/shard_map/images/pallas_call | solution.py:338
  43.2 4.1 %all-to-all-done.1 = bf16[16,8,2048]{2,1,0:T(8,128)(2,1)S(1)} async-done(((bf16[16,8,2048]{2,1,0:T(8,128)(2,1)}), bf16[16,8,2048]{2,1,0:T(8,128)(2,1)S(1)}, u32[]{:S(2)}, u32[]{:S(2)}) %all-to-all-start.1) | async-done | bytes 524320 | tf_op jit(solution)/shard_map/all_to_all | solution.py:44
  47.2 2.5 %scores.1 = (f32[128,1024]{1,0:T(8,128)S(1)}, f32[8,2,1024]{2,1,0:T(2,128)S(1)}) custom-call(bf16[128,2048]{1,0:T(8,128)(2,1)S(1)} %bitcast.12, bf16[16,1024]{1,0:T(8,128)(2,1)S(1)} %get-tuple-element.27.power_ref, s32[1,1024]{1,0:T(1,128)S(1)} %bitcast.16, s32[1,1024]{1,0:T(1,128)S(1)} %bitcast.19, bf16[512,2048]{1,0:T(8,128)(2,1)S(1)} %get-tuple-element.32.near_ref, ...), custom_call_target="tpu_custom_call" | custom-call | tf_op jit(solution)/shard_map/scores/pallas_call | solution.py:338
  49.7 8.9 %all_to_all.25.both_ref = f32[8,2,1024]{2,1,0:T(2,128)S(1)} all-to-all(f32[8,2,1024]{2,1,0:T(2,128)S(1)} %get-tuple-element.35.own_ref), channel_id=1, replica_groups=mesh['zl'=4,'co'=2,'y'=4,'zh'=4,'x'=4] {'zl','co'}, dimensions={0} | all-to-all | bytes 131072 | tf_op jit(solution)/shard_map/all_to_all | solution.py:44
  58.7 3.1 %project.1 = (s16[256,2176]{1,0:T(8,128)(2,1)S(1)}, f32[1,1024]{1,0:T(1,128)}) custom-call(f32[128,1024]{1,0:T(8,128)S(1)} %get-tuple-element.34.exp_ref, f32[8,2,1024]{2,1,0:T(2,128)S(1)} %get-tuple-element.35.own_ref, f32[8,2,1024]{2,1,0:T(2,128)S(1)} %all_to_all.25.both_ref, bf16[256,128]{1,0:T(8,128)(2,1)S(1)} %compare_convert_fusion.permuter_ref, ...), custom_call_target="tpu_custom_call" | custom-call | tf_op jit(solution)/shard_map/project/pallas_call | solution.py:338
  61.7 20.6 %all_to_all.26.came_ref = s16[16,16,2176]{2,1,0:T(8,128)(2,1)S(1)} all-to-all(s16[16,16,2176]{2,1,0:T(8,128)(2,1)S(1)} %bitcast.13), channel_id=1, replica_groups=mesh['zl'=4,'co'=2,'y'=4,'zh'=4,'x'=4] {'y','x'}, dimensions={0} | all-to-all | bytes 2228224 | tf_op jit(solution)/shard_map/all_to_all | solution.py:44
  82.4 0.9 plane.1
  83.2 19.4 %all-gather = s16[64,2176]{1,0:T(8,128)(2,1)S(1)} all-gather(s16[16,2176]{1,0:T(8,128)(2,1)S(1)} %plane.1), channel_id=2, replica_groups=mesh['zl'=4,'co'=2,'y'=4,'zh'=4,'x'=4] {'zh'}, dimensions={0}, use_global_device_ids=true | all-gather | bytes 348160 | tf_op jit(solution)/shard_map/all_gather | solution.py:411
  102.6 0.6 shells.1
  103.3 12.7 %all_to_all.27.came_ref = f32[16,8,640]{2,1,0:T(8,128)S(1)} all-to-all(f32[16,8,640]{2,1,0:T(8,128)S(1)} %get-tuple-element.45), channel_id=1, replica_groups=mesh['zl'=4,'co'=2,'y'=4,'zh'=4,'x'=4] {'y','x'}, dimensions={0} | all-to-all | bytes 655360 | tf_op jit(solution)/shard_map/all_to_all | solution.py:44
  116.0 0.8 finish.1
  (22 shorter events, 0.1 us)
Async XLA Ops:
  0.6 37.6 %copy-start.4 = (s32[1024]{0:T(1024)S(1)}, s32[1024]{0:T(1024)}, u32[]{:S(2)}) copy-start(s32[1024]{0:T(1024)} %param.10) | copy-start | bytes 12292
  2.0 27.8 %all-to-all-start = ((bf16[4,2,2048]{2,1,0:T(2,128)(2,1)}), bf16[4,2,2048]{2,1,0:T(2,128)(2,1)S(1)}, u32[]{:S(2)}, u32[]{:S(2)}) async-start(bf16[4,2,2048]{2,1,0:T(2,128)(2,1)} %broadcast_in_dim.41), calls=%async_computation | async-start | bytes 65536 | tf_op jit(solution)/shard_map/all_to_all | solution.py:44
  30.8 16.4 %all-to-all-start.1 = ((bf16[16,8,2048]{2,1,0:T(8,128)(2,1)}), bf16[16,8,2048]{2,1,0:T(8,128)(2,1)S(1)}, u32[]{:S(2)}, u32[]{:S(2)}) async-start(bf16[16,8,2048]{2,1,0:T(8,128)(2,1)} %broadcast_in_dim.77), calls=%async_computation.1 | async-start | bytes 1048576 | tf_op jit(solution)/shard_map/all_to_all | solution.py:44
  38.2 9.0 %copy-start.5 = (s32[1024,1]{0,1:T(1,128)S(1)}, s32[1024,1]{0,1:T(1,128)}, u32[]{:S(2)}) copy-start(s32[1024,1]{0,1:T(1,128)} %param.12) | copy-start | bytes 12292
  47.2 11.4 %copy-start = (bf16[1024,512]{1,0:T(8,128)(2,1)S(1)}, bf16[1024,512]{1,0:T(8,128)(2,1)}, u32[]{:S(2)}) copy-start(bf16[1024,512]{1,0:T(8,128)(2,1)} %get-tuple-element.38.rest_refs_0_) | copy-start | bytes 3145732
  47.2 11.4 %copy-start.1 = (bf16[1024,512]{1,0:T(8,128)(2,1)S(1)}, bf16[1024,512]{1,0:T(8,128)(2,1)}, u32[]{:S(2)}) copy-start(bf16[1024,512]{1,0:T(8,128)(2,1)} %get-tuple-element.39.rest_refs_1_) | copy-start | bytes 3145732
  47.2 11.4 %copy-start.2 = (bf16[1024,512]{1,0:T(8,128)(2,1)S(1)}, bf16[1024,512]{1,0:T(8,128)(2,1)}, u32[]{:S(2)}) copy-start(bf16[1024,512]{1,0:T(8,128)(2,1)} %get-tuple-element.40.rest_refs_2_) | copy-start | bytes 3145732
  47.2 11.4 %copy-start.3 = (bf16[1024,512]{1,0:T(8,128)(2,1)S(1)}, bf16[1024,512]{1,0:T(8,128)(2,1)}, u32[]{:S(2)}) copy-start(bf16[1024,512]{1,0:T(8,128)(2,1)} %get-tuple-element.41.rest_refs_3_) | copy-start | bytes 3145732
  47.2 11.4 %copy-start.6 = (s32[1024]{0:T(1024)S(1)}, s32[1024]{0:T(1024)}, u32[]{:S(2)}) copy-start(s32[1024]{0:T(1024)} %param.11) | copy-start | bytes 12292

commit v9 on v8

--- a/solution.py
+++ b/solution.py
@@ -182,8 +182,10 @@
 
 
 def score_kernel(
-    panel_ref, power_ref, bins_ref, mask_ref, near_ref, far_ref, exp_ref, pair_ref, far_buf, sems
+    panel_ref, power_ref, bins_ref, mask_ref, near_ref, far_ref, *more_refs
 ):
+    exp_ref, pair_ref = more_refs[PARTS : PARTS + 2]
+    far_buf, sems = more_refs[-2:]
     steps = far_ref.shape[0] // CHUNK
 
     def read(i):
@@ -323,7 +325,7 @@
         out_ref[0, 2:4, cols] = jnp.where(low, got, keep)
 
 
-def call(kernel, name, out_shape, mega, *args, scalars=0, far=(), far_out=(), scratch=()):
+def call(kernel, name, out_shape, mega, *args, scalars=0, far=(), far_out=(), scratch=(), alias={}):
     def space(i, hbm):
         if i < 0:
             return pl.BlockSpec(memory_space=pltpu.MemorySpace.SMEM)
@@ -341,6 +343,7 @@
         out_specs=[space(i, far_out) for i in range(len(out_shape))],
         out_shape=out_shape,
         scratch_shapes=scratch,
+        input_output_aliases=alias,
         compiler_params=pltpu.CompilerParams(vmem_limit_bytes=mega * 1024 * 1024),
         name=name,
     )(*args)
@@ -392,10 +395,11 @@
     )
     piece = from_all(by_zh.reshape(8, COLS), PLANE, 16).reshape(ORIENT, COLS)
 
-    own_exp, pair = call(
-        score_kernel, "scores", [of((ORIENT, count), F32), of((8, 2, count), F32)], 14,
-        piece, power, bins_row, mask_row, weighted_near, weighted_far,
-        far=(5,), scratch=[near((rest, COLS), BF16), pltpu.SemaphoreType.DMA((PARTS,))],
+    own_exp, pair, *centred = call(
+        score_kernel, "scores",
+        [of((ORIENT, count), F32), of((8, 2, count), F32), *[far((count, PART), BF16)] * PARTS],
+        14, piece, power, bins_row, mask_row, weighted_near, weighted_far, *centred,
+        far=(5, 6, 7, 8, 9), far_out=(2, 3, 4, 5), alias={6: 2, 7: 3, 8: 4, 9: 5}, scratch=[near((rest, COLS), BF16), pltpu.SemaphoreType.DMA((PARTS,))],
     )
     packed, evidence = call(
         project_kernel, "project", [of((ROWS, WIDE), jnp.int16), of((1, count), F32)], 20,

time: 117 us -> 122 us (1.043)
  local copies, waits for them, and re-layouts: 2.33 us -> 7.21 us
    unnamed x14, local copies, waits for them, and re-layouts: 0.03 us -> 4.91 us
where the time goes in v9:
time: 122 us
  blocking collectives  61.6 us (50%)
  starting transfers between devices  22.6 us (19%)
  waiting for transfers between devices  14.5 us (12%)
  Pallas kernels  12.7 us (10%)
  local copies, waits for them, and re-layouts  7.21 us (6%)
  other arithmetic  2.21 us (2%)
    all_to_all x3, blocking collectives, exchange(): return lax.all_to_all(blocks, axes, split_axis=0, concat_axis=0, tiled=True)  42.3 us
    all_to_all x2, starting transfers between devices, exchange(): return lax.all_to_all(blocks, axes, split_axis=0, concat_axis=0, tiled=True)  22.6 us
    all_gather x1, blocking collectives, on_device(): lax.all_gather(second, 'zh')  19.4 us
    all_to_all x2, waiting for transfers between devices, exchange(): return lax.all_to_all(blocks, axes, split_axis=0, concat_axis=0, tiled=True)  14.5 us
    pallas_call x6, Pallas kernels, call(): pl.pallas_call(kernel, in_specs=[space(i if i >= scalars else -1, far) fo...  12.7 us
    unnamed x14, local copies, waits for them, and re-layouts  4.91 us
  transfers between devices with their start and end apart: 2, of which 2 were waited for; matrix products, arithmetic and copies ran while one was open for 2% of the time, Pallas kernels for 4%

profile of v9, /device:TPU:2, one launch (start us, length us, event | category | flops | bytes accessed | tf_op | source)
XLA Modules:
  0.0 121.6 jit_solution(17268458793409651432)
XLA Ops:
  0.6 1.3 %broadcast_in_dim.41 = bf16[4,2,2048]{2,1,0:T(2,128)(2,1)} broadcast(bf16[2,2048]{1,0:T(2,128)(2,1)} %bitcast.21), dimensions={1,2} | broadcast | bytes 40960 | tf_op jit(solution)/shard_map/broadcast_in_dim | solution.py:48
  2.0 15.1 %all-to-all-start = ((bf16[4,2,2048]{2,1,0:T(2,128)(2,1)}), bf16[4,2,2048]{2,1,0:T(2,128)(2,1)S(1)}, u32[]{:S(2)}, u32[]{:S(2)}) async-start(bf16[4,2,2048]{2,1,0:T(2,128)(2,1)} %broadcast_in_dim.41), calls=%async_computation | async-start | bytes 65536 | tf_op jit(solution)/shard_map/all_to_all | solution.py:44
  17.2 0.7 broadcast_divide_fusion
  18.0 0.8 select_reduce_fusion.1
  18.9 0.1 compare_convert_fusion.permuter_ref
  19.0 0.3 fusion.3
  19.3 10.5 %all-to-all-done = bf16[4,2,2048]{2,1,0:T(2,128)(2,1)S(1)} async-done(((bf16[4,2,2048]{2,1,0:T(2,128)(2,1)}), bf16[4,2,2048]{2,1,0:T(2,128)(2,1)S(1)}, u32[]{:S(2)}, u32[]{:S(2)}) %all-to-all-start) | async-done | bytes 32800 | tf_op jit(solution)/shard_map/all_to_all | solution.py:44
  29.9 0.9 broadcast_in_dim.77
  30.8 7.5 %all-to-all-start.1 = ((bf16[16,8,2048]{2,1,0:T(8,128)(2,1)}), bf16[16,8,2048]{2,1,0:T(8,128)(2,1)S(1)}, u32[]{:S(2)}, u32[]{:S(2)}) async-start(bf16[16,8,2048]{2,1,0:T(8,128)(2,1)} %broadcast_in_dim.77), calls=%async_computation.1 | async-start | bytes 1048576 | tf_op jit(solution)/shard_map/all_to_all | solution.py:44
  38.3 4.9 %images.1 = (bf16[1024,512]{1,0:T(8,128)(2,1)}, bf16[1024,512]{1,0:T(8,128)(2,1)}, bf16[1024,512]{1,0:T(8,128)(2,1)}, bf16[1024,512]{1,0:T(8,128)(2,1)}, bf16[51...) custom-call(bf16[1024,2048]{1,0:T(8,128)(2,1)} %x_ref.1, s32[1,1024]{1,0:T(1,128)S(1)} %bitcast.15, ...), custom_call_target="tpu_custom_call" | custom-call | tf_op jit(solution)/shard_map/images/pallas_call | solution.py:340
  43.2 4.0 %all-to-all-done.1 = bf16[16,8,2048]{2,1,0:T(8,128)(2,1)S(1)} async-done(((bf16[16,8,2048]{2,1,0:T(8,128)(2,1)}), bf16[16,8,2048]{2,1,0:T(8,128)(2,1)S(1)}, u32[]{:S(2)}, u32[]{:S(2)}) %all-to-all-start.1) | async-done | bytes 524320 | tf_op jit(solution)/shard_map/all_to_all | solution.py:44
  47.2 2.5 %scores.1 = (f32[128,1024]{1,0:T(8,128)S(1)}, f32[8,2,1024]{2,1,0:T(2,128)S(1)}, bf16[1024,512]{1,0:T(8,128)(2,1)}, bf16[1024,512]{1,0:T(8,128)(2,1)}, bf16[1024...) custom-call(bf16[128,2048]{1,0:T(8,128)(2,1)S(1)} %bitcast.12, ...), custom_call_target="tpu_custom_call", output_to_operand_aliasing={{2}: (6, {}), {3}: (7, {}), {4}: (8, {}), {5}: (9, {})} | custom-call | tf_op jit(solution)/shard_map/scores/pallas_call | solution.py:340
  49.7 8.9 %all_to_all.25.both_ref = f32[8,2,1024]{2,1,0:T(2,128)S(1)} all-to-all(f32[8,2,1024]{2,1,0:T(2,128)S(1)} %get-tuple-element.43.own_ref), channel_id=1, replica_groups=mesh['zl'=4,'co'=2,'y'=4,'zh'=4,'x'=4] {'zl','co'}, dimensions={0} | all-to-all | bytes 131072 | tf_op jit(solution)/shard_map/all_to_all | solution.py:44
  58.6 1.2 %copy-done = bf16[1024,512]{1,0:T(8,128)(2,1)S(1)} copy-done((bf16[1024,512]{1,0:T(8,128)(2,1)S(1)}, bf16[1024,512]{1,0:T(8,128)(2,1)}, u32[]{:S(2)}) %copy-start) | copy-done | bytes 1048600
  59.8 1.2 %copy-done.1 = bf16[1024,512]{1,0:T(8,128)(2,1)S(1)} copy-done((bf16[1024,512]{1,0:T(8,128)(2,1)S(1)}, bf16[1024,512]{1,0:T(8,128)(2,1)}, u32[]{:S(2)}) %copy-start.1) | copy-done | bytes 1048600
  61.1 1.2 %copy-done.2 = bf16[1024,512]{1,0:T(8,128)(2,1)S(1)} copy-done((bf16[1024,512]{1,0:T(8,128)(2,1)S(1)}, bf16[1024,512]{1,0:T(8,128)(2,1)}, u32[]{:S(2)}) %copy-start.2) | copy-done | bytes 1048600
  62.3 1.2 %copy-done.3 = bf16[1024,512]{1,0:T(8,128)(2,1)S(1)} copy-done((bf16[1024,512]{1,0:T(8,128)(2,1)S(1)}, bf16[1024,512]{1,0:T(8,128)(2,1)}, u32[]{:S(2)}) %copy-start.3) | copy-done | bytes 1048600
  63.5 3.1 %project.1 = (s16[256,2176]{1,0:T(8,128)(2,1)S(1)}, f32[1,1024]{1,0:T(1,128)}) custom-call(f32[128,1024]{1,0:T(8,128)S(1)} %get-tuple-element.42.exp_ref, f32[8,2,1024]{2,1,0:T(2,128)S(1)} %get-tuple-element.43.own_ref, f32[8,2,1024]{2,1,0:T(2,128)S(1)} %all_to_all.25.both_ref, bf16[256,128]{1,0:T(8,128)(2,1)S(1)} %compare_convert_fusion.permuter_ref, ...), custom_call_target="tpu_custom_call" | custom-call | tf_op jit(solution)/shard_map/project/pallas_call | solution.py:340
  66.6 20.6 %all_to_all.26.came_ref = s16[16,16,2176]{2,1,0:T(8,128)(2,1)S(1)} all-to-all(s16[16,16,2176]{2,1,0:T(8,128)(2,1)S(1)} %bitcast.13), channel_id=1, replica_groups=mesh['zl'=4,'co'=2,'y'=4,'zh'=4,'x'=4] {'y','x'}, dimensions={0} | all-to-all | bytes 2228224 | tf_op jit(solution)/shard_map/all_to_all | solution.py:44
  87.2 0.9 plane.1
  88.0 19.4 %all-gather = s16[64,2176]{1,0:T(8,128)(2,1)S(1)} all-gather(s16[16,2176]{1,0:T(8,128)(2,1)S(1)} %plane.1), channel_id=2, replica_groups=mesh['zl'=4,'co'=2,'y'=4,'zh'=4,'x'=4] {'zh'}, dimensions={0}, use_global_device_ids=true | all-gather | bytes 348160 | tf_op jit(solution)/shard_map/all_gather | solution.py:415
  107.4 0.6 shells.1
  108.1 12.7 %all_to_all.27.came_ref = f32[16,8,640]{2,1,0:T(8,128)S(1)} all-to-all(f32[16,8,640]{2,1,0:T(8,128)S(1)} %get-tuple-element.53), channel_id=1, replica_groups=mesh['zl'=4,'co'=2,'y'=4,'zh'=4,'x'=4] {'y','x'}, dimensions={0} | all-to-all | bytes 655360 | tf_op jit(solution)/shard_map/all_to_all | solution.py:44
  120.8 0.8 finish.1
  (22 shorter events, 0.4 us)
Async XLA Ops:
  0.6 37.6 %copy-start.4 = (s32[1024]{0:T(1024)S(1)}, s32[1024]{0:T(1024)}, u32[]{:S(2)}) copy-start(s32[1024]{0:T(1024)} %param.10) | copy-start | bytes 12292
  2.0 27.8 %all-to-all-start = ((bf16[4,2,2048]{2,1,0:T(2,128)(2,1)}), bf16[4,2,2048]{2,1,0:T(2,128)(2,1)S(1)}, u32[]{:S(2)}, u32[]{:S(2)}) async-start(bf16[4,2,2048]{2,1,0:T(2,128)(2,1)} %broadcast_in_dim.41), calls=%async_computation | async-start | bytes 65536 | tf_op jit(solution)/shard_map/all_to_all | solution.py:44
  30.8 16.4 %all-to-all-start.1 = ((bf16[16,8,2048]{2,1,0:T(8,128)(2,1)}), bf16[16,8,2048]{2,1,0:T(8,128)(2,1)S(1)}, u32[]{:S(2)}, u32[]{:S(2)}) async-start(bf16[16,8,2048]{2,1,0:T(8,128)(2,1)} %broadcast_in_dim.77), calls=%async_computation.1 | async-start | bytes 1048576 | tf_op jit(solution)/shard_map/all_to_all | solution.py:44
  38.2 9.0 %copy-start.5 = (s32[1024,1]{0,1:T(1,128)S(1)}, s32[1024,1]{0,1:T(1,128)}, u32[]{:S(2)}) copy-start(s32[1024,1]{0,1:T(1,128)} %param.12) | copy-start | bytes 12292
  47.2 11.4 %copy-start.6 = (s32[1024]{0:T(1024)S(1)}, s32[1024]{0:T(1024)}, u32[]{:S(2)}) copy-start(s32[1024]{0:T(1024)} %param.11) | copy-start | bytes 12292
  58.6 1.2 %copy-start = (bf16[1024,512]{1,0:T(8,128)(2,1)S(1)}, bf16[1024,512]{1,0:T(8,128)(2,1)}, u32[]{:S(2)}) copy-start(bf16[1024,512]{1,0:T(8,128)(2,1)} %get-tuple-element.46.rest_refs_0_) | copy-start | bytes 3145732
  59.8 1.2 %copy-start.1 = (bf16[1024,512]{1,0:T(8,128)(2,1)S(1)}, bf16[1024,512]{1,0:T(8,128)(2,1)}, u32[]{:S(2)}) copy-start(bf16[1024,512]{1,0:T(8,128)(2,1)} %get-tuple-element.47.rest_refs_1_) | copy-start | bytes 3145732
  61.1 1.2 %copy-start.2 = (bf16[1024,512]{1,0:T(8,128)(2,1)S(1)}, bf16[1024,512]{1,0:T(8,128)(2,1)}, u32[]{:S(2)}) copy-start(bf16[1024,512]{1,0:T(8,128)(2,1)} %get-tuple-element.48.rest_refs_2_) | copy-start | bytes 3145732
  62.3 1.2 %copy-start.3 = (bf16[1024,512]{1,0:T(8,128)(2,1)S(1)}, bf16[1024,512]{1,0:T(8,128)(2,1)}, u32[]{:S(2)}) copy-start(bf16[1024,512]{1,0:T(8,128)(2,1)} %get-tuple-element.49.rest_refs_3_) | copy-start | bytes 3145732

commit v10 on v8

--- a/solution.py
+++ b/solution.py
@@ -350,6 +350,9 @@
     count = particles.shape[0]
     of = jax.ShapeDtypeStruct
 
+    by_zh, sigma2, orient_ids = lax.optimization_barrier(
+        (lax.all_gather(panels[0], "zh"), sigma2, orient_ids)
+    )
     shells = jnp.arange(PIXC, dtype=jnp.int32) * NSHELL // PIXC
     inverse_noise = lookup_small(shells, 1.0 / sigma2)
     table = ctf_table()
@@ -368,29 +371,29 @@
     near, far = pltpu.MemorySpace.VMEM, pltpu.MemorySpace.HBM
     first, rest = 2 * CHUNK, count - 2 * CHUNK
     permuter = (direction[:, None] == select[None, :]).astype(BF16)
-    (
-        by_zh, bins_row, parts, noise_row, power, squares, permuter, where, shell_spread, half_row,
-        mask_row,
-    ) = lax.optimization_barrier(
-        (
-            from_all(panels[0], "zh", 4), defocus_bins[None, :], table_parts(table),
-            inverse_noise[None, :], power, squares, permuter, where, shell_spread, half_sets[None, :], prior_mask.reshape(1, count),
-        )
-    )
+    bins_row = defocus_bins[None, :]
     *centred, weighted_near, weighted_far = call(
         image_kernel, "images",
         [
             *[far((count, PART), BF16)] * PARTS,
             near((first, COLS), BF16), far((rest, COLS), BF16),
         ],
-        24, particles, bins_row, parts, noise_row,
+        24, particles, bins_row, table_parts(table), inverse_noise[None, :],
         far=(0,), far_out=(0, 1, 2, 3, 5),
         scratch=[
             near((count, COLS), BF16), near((count, COLS), BF16), near((rest, COLS), BF16),
             pltpu.SemaphoreType.DMA((PARTS + 2, PARTS)),
         ],
     )
-    piece = from_all(by_zh.reshape(8, COLS), PLANE, 16).reshape(ORIENT, COLS)
+    piece, power, squares, permuter, where, shell_spread, half_row, mask_row = (
+        lax.optimization_barrier(
+            (
+                from_all(by_zh.reshape(8, COLS), PLANE, 16).reshape(ORIENT, COLS),
+                power, squares, permuter, where, shell_spread, half_sets[None, :],
+                prior_mask.reshape(1, count),
+            )
+        )
+    )
 
     own_exp, pair = call(
         score_kernel, "scores", [of((ORIENT, count), F32), of((8, 2, count), F32)], 14,

time: 117 us -> 116 us (level)
  the two profiles are of different devices: /device:TPU:2 before, /device:TPU:32 now
where the time goes in v10:
time: 116 us; the launch traced here: 115 us
  blocking collectives  88.8 us (77%)
  Pallas kernels  12.8 us (11%)
  starting transfers between devices  7.03 us (6%)
  waiting for transfers between devices  2.92 us (3%)
  other arithmetic  2.21 us (2%)
    all_to_all x3, blocking collectives, exchange(): return lax.all_to_all(blocks, axes, split_axis=0, concat_axis=0, tiled=True)  42.7 us
    all_gather x1, blocking collectives, on_device(): lax.all_gather(panels[0], 'zh')  25.1 us
    all_gather x1, blocking collectives, on_device(): lax.all_gather(second, 'zh')  21 us
    pallas_call x6, Pallas kernels, call(): pl.pallas_call(kernel, in_specs=[space(i if i >= scalars else -1, far) fo...  12.8 us
    all_to_all x1, starting transfers between devices, exchange(): return lax.all_to_all(blocks, axes, split_axis=0, concat_axis=0, tiled=True)  7.03 us
    all_to_all x1, waiting for transfers between devices, exchange(): return lax.all_to_all(blocks, axes, split_axis=0, concat_axis=0, tiled=True)  2.92 us
  transfers between devices with their start and end apart: 1, of which 1 were waited for; matrix products, arithmetic and copies ran while one was open for 2% of the time, Pallas kernels for 4%

profile of v10, /device:TPU:32, one launch (start us, length us, event | category | flops | bytes accessed | tf_op | source)
XLA Modules:
  0.0 115.5 jit_solution(9938533289059839338)
XLA Ops:
  0.6 25.1 %all_gather.9 = bf16[4,2,2048]{2,1,0:T(2,128)(2,1)S(1)} all-gather(bf16[1,2,2048]{2,1,0:T(2,128)(2,1)} %param.8), channel_id=1, replica_groups=mesh['zl'=4,'co'=2,'y'=4,'zh'=4,'x'=4] {'zh'}, dimensions={0}, use_global_device_ids=true | all-gather | bytes 40960 | tf_op jit(solution)/shard_map/all_gather | solution.py:354
  25.7 0.9 broadcast_in_dim.37
  26.6 7.0 %all-to-all-start = ((bf16[16,8,2048]{2,1,0:T(8,128)(2,1)}), bf16[16,8,2048]{2,1,0:T(8,128)(2,1)S(1)}, u32[]{:S(2)}, u32[]{:S(2)}) async-start(bf16[16,8,2048]{2,1,0:T(8,128)(2,1)} %broadcast_in_dim.37), calls=%async_computation | async-start | bytes 1048576 | tf_op jit(solution)/shard_map/all_to_all | solution.py:44
  33.7 0.7 broadcast_divide_fusion
  34.4 0.8 select_reduce_fusion.1
  35.2 0.1 select_reduce_fusion
  35.3 0.3 reduce-precision_convert_fusion.1
  35.7 0.1 pad_add_fusion
  35.8 4.9 %images.1 = (bf16[1024,512]{1,0:T(8,128)(2,1)}, bf16[1024,512]{1,0:T(8,128)(2,1)}, bf16[1024,512]{1,0:T(8,128)(2,1)}, bf16[1024,512]{1,0:T(8,128)(2,1)}, bf16[51...) custom-call(bf16[1024,2048]{1,0:T(8,128)(2,1)} %x_ref.1, s32[1,1024]{1,0:T(1,128)S(1)} %bitcast.14, ...), custom_call_target="tpu_custom_call" | custom-call | tf_op jit(solution)/shard_map/images/pallas_call | solution.py:338
  40.7 0.1 compare_convert_fusion.permuter_ref
  40.8 0.1 fusion.shells_ref.spread_ref
  40.8 2.9 %all-to-all-done = bf16[16,8,2048]{2,1,0:T(8,128)(2,1)S(1)} async-done(((bf16[16,8,2048]{2,1,0:T(8,128)(2,1)}), bf16[16,8,2048]{2,1,0:T(8,128)(2,1)S(1)}, u32[]{:S(2)}, u32[]{:S(2)}) %all-to-all-start) | async-done | bytes 524320 | tf_op jit(solution)/shard_map/all_to_all | solution.py:44
  43.8 0.1 broadcast_in_dim.65.where_ref
  43.9 0.0 copy-start.6
  43.9 2.5 %scores.1 = (f32[128,1024]{1,0:T(8,128)S(1)}, f32[8,2,1024]{2,1,0:T(2,128)S(1)}) custom-call(bf16[128,2048]{1,0:T(8,128)(2,1)S(1)} %bitcast.11, bf16[16,1024]{1,0:T(8,128)(2,1)S(1)} %get-tuple-element.30.power_ref, s32[1,1024]{1,0:T(1,128)S(1)} %bitcast.15, s32[1,1024]{1,0:T(1,128)S(1)} %bitcast.18, bf16[512,2048]{1,0:T(8,128)(2,1)S(1)} %get-tuple-element.32.near_ref, ...), custom_call_target="tpu_custom_call" | custom-call | tf_op jit(solution)/shard_map/scores/pallas_call | solution.py:338
  46.4 8.6 %all_to_all.20.both_ref = f32[8,2,1024]{2,1,0:T(2,128)S(1)} all-to-all(f32[8,2,1024]{2,1,0:T(2,128)S(1)} %get-tuple-element.35.own_ref), channel_id=1, replica_groups=mesh['zl'=4,'co'=2,'y'=4,'zh'=4,'x'=4] {'zl','co'}, dimensions={0} | all-to-all | bytes 131072 | tf_op jit(solution)/shard_map/all_to_all | solution.py:44
  55.0 0.0 copy-done.1
  55.0 3.1 %project.1 = (s16[256,2176]{1,0:T(8,128)(2,1)S(1)}, f32[1,1024]{1,0:T(1,128)}) custom-call(f32[128,1024]{1,0:T(8,128)S(1)} %get-tuple-element.34.exp_ref, f32[8,2,1024]{2,1,0:T(2,128)S(1)} %get-tuple-element.35.own_ref, f32[8,2,1024]{2,1,0:T(2,128)S(1)} %all_to_all.20.both_ref, bf16[256,128]{1,0:T(8,128)(2,1)S(1)} %compare_convert_fusion.permuter_ref, ...), custom_call_target="tpu_custom_call" | custom-call | tf_op jit(solution)/shard_map/project/pallas_call | solution.py:338
  58.1 21.9 %all_to_all.21.came_ref = s16[16,16,2176]{2,1,0:T(8,128)(2,1)S(1)} all-to-all(s16[16,16,2176]{2,1,0:T(8,128)(2,1)S(1)} %bitcast.12), channel_id=1, replica_groups=mesh['zl'=4,'co'=2,'y'=4,'zh'=4,'x'=4] {'y','x'}, dimensions={0} | all-to-all | bytes 2228224 | tf_op jit(solution)/shard_map/all_to_all | solution.py:44
  80.0 0.9 plane.1
  80.8 21.0 %all-gather = s16[64,2176]{1,0:T(8,128)(2,1)S(1)} all-gather(s16[16,2176]{1,0:T(8,128)(2,1)S(1)} %plane.1), channel_id=2, replica_groups=mesh['zl'=4,'co'=2,'y'=4,'zh'=4,'x'=4] {'zh'}, dimensions={0}, use_global_device_ids=true | all-gather | bytes 348160 | tf_op jit(solution)/shard_map/all_gather | solution.py:414
  101.8 0.6 shells.1
  102.5 12.2 %all_to_all.22.came_ref = f32[16,8,640]{2,1,0:T(8,128)S(1)} all-to-all(f32[16,8,640]{2,1,0:T(8,128)S(1)} %get-tuple-element.45), channel_id=1, replica_groups=mesh['zl'=4,'co'=2,'y'=4,'zh'=4,'x'=4] {'y','x'}, dimensions={0} | all-to-all | bytes 655360 | tf_op jit(solution)/shard_map/all_to_all | solution.py:44
  114.6 0.8 finish.1
  (20 shorter events, 0.1 us)
Async XLA Ops:
  0.6 35.1 %copy-start.4 = (s32[1024]{0:T(1024)S(1)}, s32[1024]{0:T(1024)}, u32[]{:S(2)}) copy-start(s32[1024]{0:T(1024)} %param.10) | copy-start | bytes 12292
  26.6 17.2 %all-to-all-start = ((bf16[16,8,2048]{2,1,0:T(8,128)(2,1)}), bf16[16,8,2048]{2,1,0:T(8,128)(2,1)S(1)}, u32[]{:S(2)}, u32[]{:S(2)}) async-start(bf16[16,8,2048]{2,1,0:T(8,128)(2,1)} %broadcast_in_dim.37), calls=%async_computation | async-start | bytes 1048576 | tf_op jit(solution)/shard_map/all_to_all | solution.py:44
  35.8 8.1 %copy-start.5 = (s32[1024,1]{0,1:T(1,128)S(1)}, s32[1024,1]{0,1:T(1,128)}, u32[]{:S(2)}) copy-start(s32[1024,1]{0,1:T(1,128)} %param.12) | copy-start | bytes 12292
  43.8 11.2 %copy-start = (bf16[1024,512]{1,0:T(8,128)(2,1)S(1)}, bf16[1024,512]{1,0:T(8,128)(2,1)}, u32[]{:S(2)}) copy-start(bf16[1024,512]{1,0:T(8,128)(2,1)} %get-tuple-element.38.rest_refs_0_) | copy-start | bytes 3145732
  43.8 11.2 %copy-start.1 = (bf16[1024,512]{1,0:T(8,128)(2,1)S(1)}, bf16[1024,512]{1,0:T(8,128)(2,1)}, u32[]{:S(2)}) copy-start(bf16[1024,512]{1,0:T(8,128)(2,1)} %get-tuple-element.39.rest_refs_1_) | copy-start | bytes 3145732
  43.8 11.2 %copy-start.2 = (bf16[1024,512]{1,0:T(8,128)(2,1)S(1)}, bf16[1024,512]{1,0:T(8,128)(2,1)}, u32[]{:S(2)}) copy-start(bf16[1024,512]{1,0:T(8,128)(2,1)} %get-tuple-element.40.rest_refs_2_) | copy-start | bytes 3145732
  43.8 11.2 %copy-start.3 = (bf16[1024,512]{1,0:T(8,128)(2,1)S(1)}, bf16[1024,512]{1,0:T(8,128)(2,1)}, u32[]{:S(2)}) copy-start(bf16[1024,512]{1,0:T(8,128)(2,1)} %get-tuple-element.41.rest_refs_3_) | copy-start | bytes 3145732
  43.9 11.2 %copy-start.6 = (s32[1024]{0:T(1024)S(1)}, s32[1024]{0:T(1024)}, u32[]{:S(2)}) copy-start(s32[1024]{0:T(1024)} %param.11) | copy-start | bytes 12292

commit v11 on v10

--- a/solution.py
+++ b/solution.py
@@ -57,10 +57,18 @@
     return ((r >> 1) & 1) ^ (r >> 7)
 
 
-def gathered_orients():
-    r = jnp.arange(ORIENT, dtype=jnp.int32)
-    j, zh, x, y = r % 2, (r // 2) % 4, (r // 8) % 4, r // 32
+def gathered_orient(r):
+    j, zh, x, y = r & 1, (r >> 1) & 3, (r >> 3) & 3, r >> 5
     return ((y * 4 + zh) * 4 + x) * 2 + j
+
+
+def row_permuter(orient_ids):
+    row = lax.broadcasted_iota(jnp.int32, (ROWS, ORIENT), 0)
+    wanted = jnp.where(row_direction(row) == orient_ids, 1.0, 0.0).astype(BF16)
+    orient = lax.broadcasted_iota(jnp.int32, (ORIENT, ORIENT), 0)
+    column = lax.broadcasted_iota(jnp.int32, (ORIENT, ORIENT), 1)
+    order = jnp.where(orient == gathered_orient(column), 1.0, 0.0).astype(BF16)
+    return contract(wanted, order, ((1,), (0,))).astype(BF16)
 
 
 def three_parts(table, axis):
@@ -228,7 +236,7 @@
 
 
 def project_kernel(
-    exp_ref, own_ref, both_ref, permuter_ref, half_ref, bins_ref, *rest_refs
+    exp_ref, own_ref, both_ref, orient_ref, half_ref, bins_ref, *rest_refs
 ):
     packed_ref, evidence_ref, evidence_buf, sem = rest_refs[PARTS:]
     spans = [slice(part * PART, (part + 1) * PART) for part in range(PARTS)]
@@ -240,7 +248,7 @@
     evidence = pltpu.make_async_copy(evidence_buf, evidence_ref, sem)
     evidence.start()
     posterior = (exp_ref[...] * (jnp.exp(own_peak - peak) / total)).astype(BF16)
-    by_direction = contract(permuter_ref[...], posterior, ((1,), (0,)))
+    by_direction = contract(row_permuter(orient_ref[...]), posterior, ((1,), (0,)))
     row = lax.broadcasted_iota(jnp.int32, (ROWS, 1), 0)
     kept = row_half(row) == half_ref[...]
     post = jnp.where(kept, by_direction, 0.0).astype(BF16)
@@ -350,9 +358,7 @@
     count = particles.shape[0]
     of = jax.ShapeDtypeStruct
 
-    by_zh, sigma2, orient_ids = lax.optimization_barrier(
-        (lax.all_gather(panels[0], "zh"), sigma2, orient_ids)
-    )
+    by_zh, sigma2 = lax.optimization_barrier((lax.all_gather(panels[0], "zh"), sigma2))
     shells = jnp.arange(PIXC, dtype=jnp.int32) * NSHELL // PIXC
     inverse_noise = lookup_small(shells, 1.0 / sigma2)
     table = ctf_table()
@@ -364,13 +370,8 @@
     places = jnp.stack([y // 2, zh, (y ^ 2) * 4 + x]).astype(jnp.int32)
     where = jnp.broadcast_to(jnp.pad(places, (0, 5))[:, None], (8, ORIENT))
 
-    direction = row_direction(jnp.arange(ROWS, dtype=jnp.int32))
-    match = gathered_orients()[:, None] == jnp.arange(ORIENT, dtype=jnp.int32)[None, :]
-    select = jnp.sum(jnp.where(match, orient_ids[None, :], 0), axis=1)
-
     near, far = pltpu.MemorySpace.VMEM, pltpu.MemorySpace.HBM
     first, rest = 2 * CHUNK, count - 2 * CHUNK
-    permuter = (direction[:, None] == select[None, :]).astype(BF16)
     bins_row = defocus_bins[None, :]
     *centred, weighted_near, weighted_far = call(
         image_kernel, "images",
@@ -385,11 +386,11 @@
             pltpu.SemaphoreType.DMA((PARTS + 2, PARTS)),
         ],
     )
-    piece, power, squares, permuter, where, shell_spread, half_row, mask_row = (
+    piece, power, squares, where, shell_spread, half_row, mask_row = (
         lax.optimization_barrier(
             (
                 from_all(by_zh.reshape(8, COLS), PLANE, 16).reshape(ORIENT, COLS),
-                power, squares, permuter, where, shell_spread, half_sets[None, :],
+                power, squares, where, shell_spread, half_sets[None, :],
                 prior_mask.reshape(1, count),
             )
         )
@@ -402,7 +403,7 @@
     )
     packed, evidence = call(
         project_kernel, "project", [of((ROWS, WIDE), jnp.int16), of((1, count), F32)], 20,
-        own_exp, pair, exchange(pair, CLS), permuter, half_row, bins_row,
+        own_exp, pair, exchange(pair, CLS), orient_ids[None, :], half_row, bins_row,
         *centred, far_out=(1,), scratch=[near((1, count), F32), pltpu.SemaphoreType.DMA],
     )
     (second,) = call(

time: 116 us -> 115 us (level)
  transfers between devices with their start and end apart: 1 -> 1, of which waited for: 1 -> 1; matrix products, arithmetic and copies ran while one was open for 2% -> 1% of each run, Pallas kernels for 4% -> 4%
where the time goes in v11:
time: 115 us
  blocking collectives  87.8 us (76%)
  Pallas kernels  12.9 us (11%)
  starting transfers between devices  7.03 us (6%)
  waiting for transfers between devices  3.89 us (3%)
  other arithmetic  1.25 us (1%)
    all_to_all x3, blocking collectives, exchange(): return lax.all_to_all(blocks, axes, split_axis=0, concat_axis=0, tiled=True)  41.7 us
    all_gather x1, blocking collectives, on_device(): lax.all_gather(panels[0], 'zh')  25.1 us
    all_gather x1, blocking collectives, on_device(): lax.all_gather(second, 'zh')  21 us
    pallas_call x6, Pallas kernels, call(): pl.pallas_call(kernel, in_specs=[space(i if i >= scalars else -1, far) fo...  12.9 us
    all_to_all x1, starting transfers between devices, exchange(): return lax.all_to_all(blocks, axes, split_axis=0, concat_axis=0, tiled=True)  7.03 us
    all_to_all x1, waiting for transfers between devices, exchange(): return lax.all_to_all(blocks, axes, split_axis=0, concat_axis=0, tiled=True)  3.89 us
  transfers between devices with their start and end apart: 1, of which 1 were waited for; matrix products, arithmetic and copies ran while one was open for 1% of the time, Pallas kernels for 4%

profile of v11, /device:TPU:32, one launch (start us, length us, event | category | flops | bytes accessed | tf_op | source)
XLA Modules:
  0.0 114.7 jit_solution(4888481601872000558)
XLA Ops:
  0.6 25.1 %all_gather.9 = bf16[4,2,2048]{2,1,0:T(2,128)(2,1)S(1)} all-gather(bf16[1,2,2048]{2,1,0:T(2,128)(2,1)} %param.8), channel_id=1, replica_groups=mesh['zl'=4,'co'=2,'y'=4,'zh'=4,'x'=4] {'zh'}, dimensions={0}, use_global_device_ids=true | all-gather | bytes 40960 | tf_op jit(solution)/shard_map/all_gather | solution.py:361
  25.7 0.9 broadcast_in_dim.46
  26.6 7.0 %all-to-all-start = ((bf16[16,8,2048]{2,1,0:T(8,128)(2,1)}), bf16[16,8,2048]{2,1,0:T(8,128)(2,1)S(1)}, u32[]{:S(2)}, u32[]{:S(2)}) async-start(bf16[16,8,2048]{2,1,0:T(8,128)(2,1)} %broadcast_in_dim.46), calls=%async_computation | async-start | bytes 1048576 | tf_op jit(solution)/shard_map/all_to_all | solution.py:44
  33.7 0.1 pad_add_fusion
  33.8 0.7 broadcast_divide_fusion
  34.4 0.1 select_reduce_fusion
  34.5 0.3 reduce-precision_convert_fusion.1
  34.9 0.0 copy-done.4
  34.9 0.0 copy-start.5
  34.9 4.9 %images.1 = (bf16[1024,512]{1,0:T(8,128)(2,1)}, bf16[1024,512]{1,0:T(8,128)(2,1)}, bf16[1024,512]{1,0:T(8,128)(2,1)}, bf16[1024,512]{1,0:T(8,128)(2,1)}, bf16[51...) custom-call(bf16[1024,2048]{1,0:T(8,128)(2,1)} %x_ref.1, s32[1,1024]{1,0:T(1,128)S(1)} %bitcast.15, ...), custom_call_target="tpu_custom_call" | custom-call | tf_op jit(solution)/shard_map/images/pallas_call | solution.py:346
  39.8 0.1 fusion.shells_ref.spread_ref
  39.9 3.9 %all-to-all-done = bf16[16,8,2048]{2,1,0:T(8,128)(2,1)S(1)} async-done(((bf16[16,8,2048]{2,1,0:T(8,128)(2,1)}), bf16[16,8,2048]{2,1,0:T(8,128)(2,1)S(1)}, u32[]{:S(2)}, u32[]{:S(2)}) %all-to-all-start) | async-done | bytes 524320 | tf_op jit(solution)/shard_map/all_to_all | solution.py:44
  43.8 0.1 broadcast_in_dim.49.where_ref
  43.9 0.0 copy-start.6
  43.9 0.0 copy-start.7
  43.9 2.5 %scores.1 = (f32[128,1024]{1,0:T(8,128)S(1)}, f32[8,2,1024]{2,1,0:T(2,128)S(1)}) custom-call(bf16[128,2048]{1,0:T(8,128)(2,1)S(1)} %bitcast.12, bf16[16,1024]{1,0:T(8,128)(2,1)S(1)} %get-tuple-element.27.power_ref, s32[1,1024]{1,0:T(1,128)S(1)} %bitcast.16, s32[1,1024]{1,0:T(1,128)S(1)} %bitcast.19, bf16[512,2048]{1,0:T(8,128)(2,1)S(1)} %get-tuple-element.29.near_ref, ...), custom_call_target="tpu_custom_call" | custom-call | tf_op jit(solution)/shard_map/scores/pallas_call | solution.py:346
  46.4 8.6 %all_to_all.20.both_ref = f32[8,2,1024]{2,1,0:T(2,128)S(1)} all-to-all(f32[8,2,1024]{2,1,0:T(2,128)S(1)} %get-tuple-element.32.own_ref), channel_id=1, replica_groups=mesh['zl'=4,'co'=2,'y'=4,'zh'=4,'x'=4] {'zl','co'}, dimensions={0} | all-to-all | bytes 131072 | tf_op jit(solution)/shard_map/all_to_all | solution.py:44
  55.0 3.2 %project.1 = (s16[256,2176]{1,0:T(8,128)(2,1)S(1)}, f32[1,1024]{1,0:T(1,128)}) custom-call(f32[128,1024]{1,0:T(8,128)S(1)} %get-tuple-element.31.exp_ref, f32[8,2,1024]{2,1,0:T(2,128)S(1)} %get-tuple-element.32.own_ref, f32[8,2,1024]{2,1,0:T(2,128)S(1)} %all_to_all.20.both_ref, s32[1,128]{1,0:T(1,128)S(1)} %bitcast.21, s32[1,1024]{1,0:T(1,128)S(1)} %bitcast.20, ...), custom_call_target="tpu_custom_call" | custom-call | tf_op jit(solution)/shard_map/project/pallas_call | solution.py:346
  58.2 20.9 %all_to_all.21.came_ref = s16[16,16,2176]{2,1,0:T(8,128)(2,1)S(1)} all-to-all(s16[16,16,2176]{2,1,0:T(8,128)(2,1)S(1)} %bitcast.13), channel_id=1, replica_groups=mesh['zl'=4,'co'=2,'y'=4,'zh'=4,'x'=4] {'y','x'}, dimensions={0} | all-to-all | bytes 2228224 | tf_op jit(solution)/shard_map/all_to_all | solution.py:44
  79.2 0.9 plane.1
  80.0 21.0 %all-gather = s16[64,2176]{1,0:T(8,128)(2,1)S(1)} all-gather(s16[16,2176]{1,0:T(8,128)(2,1)S(1)} %plane.1), channel_id=2, replica_groups=mesh['zl'=4,'co'=2,'y'=4,'zh'=4,'x'=4] {'zh'}, dimensions={0}, use_global_device_ids=true | all-gather | bytes 348160 | tf_op jit(solution)/shard_map/all_gather | solution.py:415
  101.0 0.6 shells.1
  101.7 12.2 %all_to_all.22.came_ref = f32[16,8,640]{2,1,0:T(8,128)S(1)} all-to-all(f32[16,8,640]{2,1,0:T(8,128)S(1)} %get-tuple-element.41), channel_id=1, replica_groups=mesh['zl'=4,'co'=2,'y'=4,'zh'=4,'x'=4] {'y','x'}, dimensions={0} | all-to-all | bytes 655360 | tf_op jit(solution)/shard_map/all_to_all | solution.py:44
  113.8 0.8 finish.1
  (18 shorter events, 0.1 us)
Async XLA Ops:
  0.6 34.3 %copy-start.4 = (s32[1024]{0:T(1024)S(1)}, s32[1024]{0:T(1024)}, u32[]{:S(2)}) copy-start(s32[1024]{0:T(1024)} %param.10) | copy-start | bytes 12292
  26.6 17.2 %all-to-all-start = ((bf16[16,8,2048]{2,1,0:T(8,128)(2,1)}), bf16[16,8,2048]{2,1,0:T(8,128)(2,1)S(1)}, u32[]{:S(2)}, u32[]{:S(2)}) async-start(bf16[16,8,2048]{2,1,0:T(8,128)(2,1)} %broadcast_in_dim.46), calls=%async_computation | async-start | bytes 1048576 | tf_op jit(solution)/shard_map/all_to_all | solution.py:44
  34.9 8.9 %copy-start.5 = (s32[1024,1]{0,1:T(1,128)S(1)}, s32[1024,1]{0,1:T(1,128)}, u32[]{:S(2)}) copy-start(s32[1024,1]{0,1:T(1,128)} %param.12) | copy-start | bytes 12292
  43.8 11.2 %copy-start = (bf16[1024,512]{1,0:T(8,128)(2,1)S(1)}, bf16[1024,512]{1,0:T(8,128)(2,1)}, u32[]{:S(2)}) copy-start(bf16[1024,512]{1,0:T(8,128)(2,1)} %get-tuple-element.34.rest_refs_0_) | copy-start | bytes 3145732
  43.8 11.2 %copy-start.1 = (bf16[1024,512]{1,0:T(8,128)(2,1)S(1)}, bf16[1024,512]{1,0:T(8,128)(2,1)}, u32[]{:S(2)}) copy-start(bf16[1024,512]{1,0:T(8,128)(2,1)} %get-tuple-element.35.rest_refs_1_) | copy-start | bytes 3145732
  43.8 11.2 %copy-start.2 = (bf16[1024,512]{1,0:T(8,128)(2,1)S(1)}, bf16[1024,512]{1,0:T(8,128)(2,1)}, u32[]{:S(2)}) copy-start(bf16[1024,512]{1,0:T(8,128)(2,1)} %get-tuple-element.36.rest_refs_2_) | copy-start | bytes 3145732
  43.8 11.2 %copy-start.3 = (bf16[1024,512]{1,0:T(8,128)(2,1)S(1)}, bf16[1024,512]{1,0:T(8,128)(2,1)}, u32[]{:S(2)}) copy-start(bf16[1024,512]{1,0:T(8,128)(2,1)} %get-tuple-element.37.rest_refs_3_) | copy-start | bytes 3145732
  43.9 11.2 %copy-start.6 = (s32[1024]{0:T(1024)S(1)}, s32[1024]{0:T(1024)}, u32[]{:S(2)}) copy-start(s32[1024]{0:T(1024)} %param.11) | copy-start | bytes 12292
  43.9 11.2 %copy-start.7 = (s32[128]{0:T(128)S(1)}, s32[128]{0:T(128)}, u32[]{:S(2)}) copy-start(s32[128]{0:T(128)} %param.13) | copy-start | bytes 1540

commit v12 on v11

--- a/solution.py
+++ b/solution.py
@@ -360,7 +360,7 @@
 
     by_zh, sigma2 = lax.optimization_barrier((lax.all_gather(panels[0], "zh"), sigma2))
     shells = jnp.arange(PIXC, dtype=jnp.int32) * NSHELL // PIXC
-    inverse_noise = lookup_small(shells, 1.0 / sigma2)
+    inverse_noise = 1.0 / lookup_small(shells, sigma2)
     table = ctf_table()
     power = (table * table * inverse_noise[None, :]).astype(BF16)
     squares = (table * table).astype(BF16)

time: 115 us -> 115 us (level)
  no operation moved by 1% of the time
where the time goes in v12:
time: 115 us
  blocking collectives  87.8 us (76%)
  Pallas kernels  12.9 us (11%)
  starting transfers between devices  7.03 us (6%)
  waiting for transfers between devices  3.91 us (3%)
  other arithmetic  1.25 us (1%)
    all_to_all x3, blocking collectives, exchange(): return lax.all_to_all(blocks, axes, split_axis=0, concat_axis=0, tiled=True)  41.7 us
    all_gather x1, blocking collectives, on_device(): lax.all_gather(panels[0], 'zh')  25.1 us
    all_gather x1, blocking collectives, on_device(): lax.all_gather(second, 'zh')  21 us
    pallas_call x6, Pallas kernels, call(): pl.pallas_call(kernel, in_specs=[space(i if i >= scalars else -1, far) fo...  12.9 us
    all_to_all x1, starting transfers between devices, exchange(): return lax.all_to_all(blocks, axes, split_axis=0, concat_axis=0, tiled=True)  7.03 us
    all_to_all x1, waiting for transfers between devices, exchange(): return lax.all_to_all(blocks, axes, split_axis=0, concat_axis=0, tiled=True)  3.91 us
  transfers between devices with their start and end apart: 1, of which 1 were waited for; matrix products, arithmetic and copies ran while one was open for 1% of the time, Pallas kernels for 4%

profile of v12, /device:TPU:32, one launch (start us, length us, event | category | flops | bytes accessed | tf_op | source)
XLA Modules:
  0.0 114.6 jit_solution(14343949103001532349)
XLA Ops:
  0.6 25.1 %all_gather.9 = bf16[4,2,2048]{2,1,0:T(2,128)(2,1)S(1)} all-gather(bf16[1,2,2048]{2,1,0:T(2,128)(2,1)} %param.8), channel_id=1, replica_groups=mesh['zl'=4,'co'=2,'y'=4,'zh'=4,'x'=4] {'zh'}, dimensions={0}, use_global_device_ids=true | all-gather | bytes 40960 | tf_op jit(solution)/shard_map/all_gather | solution.py:361
  25.7 0.9 broadcast_in_dim.25
  26.6 7.0 %all-to-all-start = ((bf16[16,8,2048]{2,1,0:T(8,128)(2,1)}), bf16[16,8,2048]{2,1,0:T(8,128)(2,1)S(1)}, u32[]{:S(2)}, u32[]{:S(2)}) async-start(bf16[16,8,2048]{2,1,0:T(8,128)(2,1)} %broadcast_in_dim.25), calls=%async_computation | async-start | bytes 1048576 | tf_op jit(solution)/shard_map/all_to_all | solution.py:44
  33.7 0.1 pad_add_fusion
  33.8 0.7 select_reduce_fusion
  34.5 0.3 reduce-precision_convert_fusion.1
  34.9 0.0 copy-done.4
  34.9 0.0 copy-start.5
  34.9 4.9 %images.1 = (bf16[1024,512]{1,0:T(8,128)(2,1)}, bf16[1024,512]{1,0:T(8,128)(2,1)}, bf16[1024,512]{1,0:T(8,128)(2,1)}, bf16[1024,512]{1,0:T(8,128)(2,1)}, bf16[51...) custom-call(bf16[1024,2048]{1,0:T(8,128)(2,1)} %x_ref.1, s32[1,1024]{1,0:T(1,128)S(1)} %bitcast.15, ...), custom_call_target="tpu_custom_call" | custom-call | tf_op jit(solution)/shard_map/images/pallas_call | solution.py:346
  39.8 0.1 fusion.shells_ref.spread_ref
  39.8 3.9 %all-to-all-done = bf16[16,8,2048]{2,1,0:T(8,128)(2,1)S(1)} async-done(((bf16[16,8,2048]{2,1,0:T(8,128)(2,1)}), bf16[16,8,2048]{2,1,0:T(8,128)(2,1)S(1)}, u32[]{:S(2)}, u32[]{:S(2)}) %all-to-all-start) | async-done | bytes 524320 | tf_op jit(solution)/shard_map/all_to_all | solution.py:44
  43.8 0.1 broadcast_in_dim.47.where_ref
  43.8 0.0 copy-start.6
  43.9 0.0 copy-start.7
  43.9 2.5 %scores.1 = (f32[128,1024]{1,0:T(8,128)S(1)}, f32[8,2,1024]{2,1,0:T(2,128)S(1)}) custom-call(bf16[128,2048]{1,0:T(8,128)(2,1)S(1)} %bitcast.12, bf16[16,1024]{1,0:T(8,128)(2,1)S(1)} %get-tuple-element.27.power_ref, s32[1,1024]{1,0:T(1,128)S(1)} %bitcast.16, s32[1,1024]{1,0:T(1,128)S(1)} %bitcast.19, bf16[512,2048]{1,0:T(8,128)(2,1)S(1)} %get-tuple-element.29.near_ref, ...), custom_call_target="tpu_custom_call" | custom-call | tf_op jit(solution)/shard_map/scores/pallas_call | solution.py:346
  46.4 8.6 %all_to_all.20.both_ref = f32[8,2,1024]{2,1,0:T(2,128)S(1)} all-to-all(f32[8,2,1024]{2,1,0:T(2,128)S(1)} %get-tuple-element.32.own_ref), channel_id=1, replica_groups=mesh['zl'=4,'co'=2,'y'=4,'zh'=4,'x'=4] {'zl','co'}, dimensions={0} | all-to-all | bytes 131072 | tf_op jit(solution)/shard_map/all_to_all | solution.py:44
  55.0 0.0 copy-done.1
  55.0 3.2 %project.1 = (s16[256,2176]{1,0:T(8,128)(2,1)S(1)}, f32[1,1024]{1,0:T(1,128)}) custom-call(f32[128,1024]{1,0:T(8,128)S(1)} %get-tuple-element.31.exp_ref, f32[8,2,1024]{2,1,0:T(2,128)S(1)} %get-tuple-element.32.own_ref, f32[8,2,1024]{2,1,0:T(2,128)S(1)} %all_to_all.20.both_ref, s32[1,128]{1,0:T(1,128)S(1)} %bitcast.21, s32[1,1024]{1,0:T(1,128)S(1)} %bitcast.20, ...), custom_call_target="tpu_custom_call" | custom-call | tf_op jit(solution)/shard_map/project/pallas_call | solution.py:346
  58.2 20.9 %all_to_all.21.came_ref = s16[16,16,2176]{2,1,0:T(8,128)(2,1)S(1)} all-to-all(s16[16,16,2176]{2,1,0:T(8,128)(2,1)S(1)} %bitcast.13), channel_id=1, replica_groups=mesh['zl'=4,'co'=2,'y'=4,'zh'=4,'x'=4] {'y','x'}, dimensions={0} | all-to-all | bytes 2228224 | tf_op jit(solution)/shard_map/all_to_all | solution.py:44
  79.1 0.9 plane.1
  80.0 21.0 %all-gather = s16[64,2176]{1,0:T(8,128)(2,1)S(1)} all-gather(s16[16,2176]{1,0:T(8,128)(2,1)S(1)} %plane.1), channel_id=2, replica_groups=mesh['zl'=4,'co'=2,'y'=4,'zh'=4,'x'=4] {'zh'}, dimensions={0}, use_global_device_ids=true | all-gather | bytes 348160 | tf_op jit(solution)/shard_map/all_gather | solution.py:415
  101.0 0.6 shells.1
  101.7 12.1 %all_to_all.22.came_ref = f32[16,8,640]{2,1,0:T(8,128)S(1)} all-to-all(f32[16,8,640]{2,1,0:T(8,128)S(1)} %get-tuple-element.41), channel_id=1, replica_groups=mesh['zl'=4,'co'=2,'y'=4,'zh'=4,'x'=4] {'y','x'}, dimensions={0} | all-to-all | bytes 655360 | tf_op jit(solution)/shard_map/all_to_all | solution.py:44
  113.8 0.8 finish.1
  (17 shorter events, 0.1 us)
Async XLA Ops:
  0.6 34.2 %copy-start.4 = (s32[1024]{0:T(1024)S(1)}, s32[1024]{0:T(1024)}, u32[]{:S(2)}) copy-start(s32[1024]{0:T(1024)} %param.10) | copy-start | bytes 12292
  26.6 17.2 %all-to-all-start = ((bf16[16,8,2048]{2,1,0:T(8,128)(2,1)}), bf16[16,8,2048]{2,1,0:T(8,128)(2,1)S(1)}, u32[]{:S(2)}, u32[]{:S(2)}) async-start(bf16[16,8,2048]{2,1,0:T(8,128)(2,1)} %broadcast_in_dim.25), calls=%async_computation | async-start | bytes 1048576 | tf_op jit(solution)/shard_map/all_to_all | solution.py:44
  34.9 8.9 %copy-start.5 = (s32[1024,1]{0,1:T(1,128)S(1)}, s32[1024,1]{0,1:T(1,128)}, u32[]{:S(2)}) copy-start(s32[1024,1]{0,1:T(1,128)} %param.12) | copy-start | bytes 12292
  43.8 11.2 %copy-start = (bf16[1024,512]{1,0:T(8,128)(2,1)S(1)}, bf16[1024,512]{1,0:T(8,128)(2,1)}, u32[]{:S(2)}) copy-start(bf16[1024,512]{1,0:T(8,128)(2,1)} %get-tuple-element.34.rest_refs_0_) | copy-start | bytes 3145732
  43.8 11.2 %copy-start.1 = (bf16[1024,512]{1,0:T(8,128)(2,1)S(1)}, bf16[1024,512]{1,0:T(8,128)(2,1)}, u32[]{:S(2)}) copy-start(bf16[1024,512]{1,0:T(8,128)(2,1)} %get-tuple-element.35.rest_refs_1_) | copy-start | bytes 3145732
  43.8 11.2 %copy-start.2 = (bf16[1024,512]{1,0:T(8,128)(2,1)S(1)}, bf16[1024,512]{1,0:T(8,128)(2,1)}, u32[]{:S(2)}) copy-start(bf16[1024,512]{1,0:T(8,128)(2,1)} %get-tuple-element.36.rest_refs_2_) | copy-start | bytes 3145732
  43.8 11.2 %copy-start.3 = (bf16[1024,512]{1,0:T(8,128)(2,1)S(1)}, bf16[1024,512]{1,0:T(8,128)(2,1)}, u32[]{:S(2)}) copy-start(bf16[1024,512]{1,0:T(8,128)(2,1)} %get-tuple-element.37.rest_refs_3_) | copy-start | bytes 3145732
  43.8 11.2 %copy-start.6 = (s32[1024]{0:T(1024)S(1)}, s32[1024]{0:T(1024)}, u32[]{:S(2)}) copy-start(s32[1024]{0:T(1024)} %param.11) | copy-start | bytes 12292
  43.9 11.2 %copy-start.7 = (s32[128]{0:T(128)S(1)}, s32[128]{0:T(128)}, u32[]{:S(2)}) copy-start(s32[128]{0:T(128)} %param.13) | copy-start | bytes 1540
